TPU v7x, 32 devices: a whole 2x2x4 slice. The times are simulated.
32 devices in a mesh: dp: 8 (over z, x), tensor: 4 (over y, core).
Axes of the slice: x: 2, y: 2, z: 4, core: 2. Of those that a mesh axis runs over, the one named last changes fastest.
Arguments:
- prefix: bfloat16 [8, 128, 8192], P('dp'), may hold values from -6 to 6
- kv_weight: bfloat16 [8192, 2, 512], P(None, None, 'tensor'), may hold values from -0.044194174 to 0.044194174
- ans_query: bfloat16 [8192, 4096], P('dp', 'tensor'), may hold values from -60 to 60
- ans_kv: bfloat16 [8192, 2, 512], P('dp', None, 'tensor'), may hold values from -8 to 8
- d_out: bfloat16 [8192, 4096], P('dp', 'tensor'), may hold values from -192 to 192
- branch_prompt: int32 [16], P('dp'), may hold values from 0 to 7, as said below
Outputs:
- attn_out: bfloat16 [8192, 4096], P('dp', 'tensor')
- prefix_grad: bfloat16 [8, 128, 8192], P('dp', 'tensor')
Inputs may be any that keep to these rules, and one draw needn't show every extreme that they name: `branch_prompt`: prompt p is owned by dp index p. The dp index that holds a branch and the owner of its prompt are at most 3 steps apart, counting around the axis. Every dp index holds at least one answer to its own prompt.
All inputs are finite; a program needn't handle non-finite values.
Results may differ from a plain program's by a relative error of at most 0.014.
The roundings to bfloat16 on the way count: a program that leaves them out, or rounds other values in their place, can miss the bound.
Values may be sent and summed in bfloat16 or wider, within the bound.
No kernel may reach another device: no remote copies, remote signals or barrier semaphores. Data moves between devices by JAX's collectives and lax.ppermute only.
A program may use at most 128 MiB of HBM per device.

v0:
```python
import jax
import jax.numpy as jnp
from jax import lax
from jax.sharding import PartitionSpec as P

HD = 128
REACH = 3


def shifted(x, axis, by):
    devices = lax.axis_size(axis)
    return lax.ppermute(x, axis, [(i, (i + by) % devices) for i in range(devices)])


def branch_pass(queries, key_rows, value_rows, upstream):
    answers = queries.shape[0]
    prefix_len = key_rows.shape[0] - answers
    scaling = queries.shape[-1] ** (-0.5)
    scores = (
        jnp.einsum("ahgd,khd->hgak", queries, key_rows, preferred_element_type=jnp.float32)
        * scaling
    )
    key_pos = jnp.arange(key_rows.shape[0])
    row_pos = jnp.arange(answers)
    allowed = (key_pos[None, :] < prefix_len) | (key_pos[None, :] - prefix_len <= row_pos[:, None])
    scores = jnp.where(allowed, scores, -jnp.inf)
    row_max = jnp.max(scores, axis=-1, keepdims=True)
    exps = jnp.exp(scores - row_max)
    prob_full = exps / jnp.sum(exps, axis=-1, keepdims=True)
    prob_half = prob_full.astype(jnp.bfloat16)
    context = jnp.einsum(
        "hgak,khd->ahgd", prob_half, value_rows, preferred_element_type=jnp.float32
    )
    prob_grad = jnp.einsum(
        "ahgd,khd->hgak", upstream, value_rows, preferred_element_type=jnp.float32
    )
    delta_row = jnp.einsum("ahgd,ahgd->hga", upstream, context, preferred_element_type=jnp.float32)
    score_half = (prob_full * (prob_grad - delta_row[..., None])).astype(jnp.bfloat16)
    key_grad = (
        jnp.einsum(
            "hgak,ahgd->khd",
            score_half[..., :prefix_len],
            queries,
            preferred_element_type=jnp.float32,
        )
        * scaling
    )
    value_grad = jnp.einsum(
        "hgak,ahgd->khd", prob_half[..., :prefix_len], upstream, preferred_element_type=jnp.float32
    )
    return (context.astype(jnp.bfloat16), key_grad, value_grad)


def shards(prefix, kv_weight, ans_query, ans_kv, d_out, branch_prompt):
    prefix_len = prefix.shape[1]
    model_width = prefix.shape[2]
    columns = kv_weight.shape[2]
    heads_here = columns // HD
    groups = ans_query.shape[1] // columns
    branches = branch_prompt.shape[0]
    answers = ans_query.shape[0] // branches
    flat_weight = kv_weight.reshape(kv_weight.shape[0], 2 * columns)
    own_kv = jnp.dot(prefix[0], flat_weight, preferred_element_type=jnp.float32).astype(
        jnp.bfloat16
    )
    my_index = lax.axis_index("dp")
    dp_count = lax.axis_size("dp")
    window = 2 * REACH + 1
    slot_index = (branch_prompt - my_index + REACH) % dp_count
    pieces = [own_kv] * window
    for offset in range(window):
        if offset != REACH:
            pieces[offset] = shifted(own_kv, "dp", REACH - offset)
    nearby = jnp.stack(pieces, axis=0)
    chosen = jnp.take(nearby, slot_index, axis=0).reshape(branches, prefix_len, 2, heads_here, HD)
    queries = ans_query.reshape(branches, answers, heads_here, groups, HD)
    answer_kv = ans_kv.reshape(branches, answers, 2, heads_here, HD)
    upstream = d_out.reshape(branches, answers, heads_here, groups, HD)

    def one_branch(packed):
        branch_q, branch_kv, branch_up, prompt_kv = packed
        key_rows = jnp.concatenate([prompt_kv[:, 0], branch_kv[:, 0]], axis=0)
        value_rows = jnp.concatenate([prompt_kv[:, 1], branch_kv[:, 1]], axis=0)
        return branch_pass(branch_q, key_rows, value_rows, branch_up)

    context, key_grad, value_grad = lax.map(one_branch, (queries, answer_kv, upstream, chosen))
    attn_out = context.reshape(branches * answers, groups * columns)
    both_grads = jnp.stack([key_grad, value_grad], axis=2).reshape(
        branches, prefix_len * 2 * columns
    )
    selector = (slot_index[:, None] == jnp.arange(window)[None, :]).astype(jnp.float32)
    placed = jnp.dot(selector.T, both_grads, precision=lax.Precision.HIGHEST).reshape(
        window, prefix_len, 2 * columns
    )
    kv_sum = placed[REACH]
    for offset in range(window):
        if offset != REACH:
            kv_sum = kv_sum + shifted(
                placed[offset].astype(jnp.bfloat16), "dp", offset - REACH
            ).astype(jnp.float32)
    kv_grad = kv_sum.astype(jnp.bfloat16)
    tensor_count = lax.axis_size("tensor")
    prefix_rows = lax.psum_scatter(
        lax.dot_general(
            kv_grad, flat_weight, (((1,), (1,)), ((), ())), preferred_element_type=jnp.float32
        ).astype(jnp.bfloat16),
        "tensor",
        scatter_dimension=0,
        tiled=True,
    )
    prefix_grad = prefix_rows.reshape(1, prefix_len // tensor_count, model_width)
    return (attn_out, prefix_grad)


def solution(mesh):
    return jax.shard_map(
        shards,
        mesh=mesh,
        in_specs=(
            P("dp", None, None),
            P(None, None, "tensor"),
            P("dp", "tensor"),
            P("dp", None, "tensor"),
            P("dp", "tensor"),
            P("dp"),
        ),
        out_specs=(P("dp", "tensor"), P("dp", "tensor", None)),
        check_vma=False,
    )
```

profile of v0, /device:TPU:0, one launch (start us, length us, event | category | flops | bytes accessed | tf_op | source)
XLA Modules:
  0.0 153.4 jit_solution(12192768941647793026)
XLA Ops:
  8.8 2.9 %fusion.32 = bf16[128,256]{1,0:T(8,128)(2,1)S(1)} fusion(bf16[1024,8,2,128]{3,2,1,0:T(2,128)(2,1)} %bitcast.207, bf16[1,128,8192]{2,1,0:T(8,128)(2,1)S(1)} %copy-done), kind=kOutput, calls=%fused_computation.61 | convolution fusion | flops 536903680 | bytes 6356992 | tf_op jit(solution)/shard_map/dot_general | solution.py:63
  11.7 4.0 %collective-permute-start = (bf16[128,256]{1,0:T(8,128)(2,1)S(1)}, bf16[128,256]{1,0:T(8,128)(2,1)S(1)}, u32[]{:S(2)}, u32[]{:S(2)}) collective-permute-start(bf16[128,256]{1,0:T(8,128)(2,1)S(1)} %fusion.32), channel_id=1, source_target_pairs={{0,12},{4,16},{8,20},{12,24},{16,28},{20,0},{24,4},{28,8},{1,13},{... | collective-permute-start | bytes 196616 | tf_op jit(solution)/shard_map/ppermute | solution.py:12
  18.8 3.2 %collective-permute-start.3 = (bf16[128,256]{1,0:T(8,128)(2,1)S(1)}, bf16[128,256]{1,0:T(8,128)(2,1)S(1)}, u32[]{:S(2)}, u32[]{:S(2)}) collective-permute-start(bf16[128,256]{1,0:T(8,128)(2,1)S(1)} %fusion.32), channel_id=1, source_target_pairs={{0,28},{4,0},{8,4},{12,8},{16,12},{20,16},{24,20},{28,24},{1,29},{... | collective-permute-start | bytes 196616 | tf_op jit(solution)/shard_map/ppermute | solution.py:12
  22.5 3.5 %copy.50 = bf16[128,8,8,128]{3,2,1,0:T(8,128)(2,1)} copy(bf16[128,8,8,128]{3,1,2,0:T(8,128)(2,1)} %bitcast.210) | data formatting | bytes 4194304
  28.2 5.0 %collective-permute-done.5 = bf16[128,256]{1,0:T(8,128)(2,1)S(1)} collective-permute-done((bf16[128,256]{1,0:T(8,128)(2,1)S(1)}, bf16[128,256]{1,0:T(8,128)(2,1)S(1)}, u32[]{:S(2)}, u32[]{:S(2)}) %collective-permute-start.5) | collective-permute-done | bytes 65568 | tf_op jit(solution)/shard_map/ppermute | solution.py:12
  33.9 60.1 %while.16 = (s32[]{:T(128)}, bf16[2,512,1,8,128]{4,3,1,0,2:T(8,128)(2,1)}, f32[2,128,1,128]{1,3,2,0:T(8,128)S(1)}, f32[2,128,1,128]{1,3,2,0:T(8,128)S(1)}, bf16[...) while((s32[]{:T(128)}, ...), condition=%wide.region_3.4_spmd, body=%wide.region_0.3_spmd.sunk | while | flops 2318472448 | bytes 97214312 | solution.py:86
  39.1 2.1 %fusion.62 = f32[8,512]{1,0:T(8,128)S(1)} fusion(f32[640,512,8]{1,0,2:T(8,128)S(1)} %get-tuple-element.221, f32[8,512]{1,0:T(8,128)S(1)} %get-tuple-element.222, pred[512,640]{0,1:T(8,128)(4,1)S(1)} %fusion.60), kind=kLoop, calls=%fused_computation.4.clone.1 | loop fusion | flops 10481664 | bytes 10846208 | tf_op jit(solution)/shard_map/while/body/eval_jaxpr/reduce_sum | solution.py:29
  41.2 6.6 %fusion.63 = (bf16[1,8,512,640]{2,3,1,0:T(8,128)(2,1)}, f32[1,8,512,640]{2,3,1,0:T(8,128)}) fusion(f32[8,512]{1,0:T(8,128)S(1)} %fusion.62, f32[8,512]{1,0:T(8,128)S(1)} %get-tuple-element.222, f32[640,512,8]{1,0,2:T(8,128)S(1)} %get-tuple-element.221, pred[512,640]{0,1:T(8,128)(4,1)S(1)} %fusion.60), kind=kLoop, calls=%fused_computation.90.clone.1 | loop fusion | flops 13107200 | bytes 26574848 | tf_op jit(solution)/shard_map/while/body/eval_jaxpr/convert_element_type | solution.py:30
  49.3 2.9 %copy.95 = f32[8,512,128]{1,2,0:T(8,128)} copy(f32[8,512,128]{2,1,0:T(8,128)} %bitcast_convert_fusion.3) | data formatting | bytes 4194304 | tf_op jit(solution)/shard_map/while
  52.2 4.2 %fusion.64 = (f32[8,512]{1,0:T(8,128)S(1)}, bf16[128,8,512]{2,0,1:T(8,128)(2,1)S(1)}) fusion(f32[8,512,128]{1,2,0:T(8,128)} %copy.95, bf16[1,8,512,640]{2,3,1,0:T(8,128)(2,1)} %get-tuple-element.223, bf16[512,1,128]{2,0,1:T(8,128)(2,1)S(1)} %get-tuple-element.224, bf16[128,1,128]{2,0,1:T(8,128)(2,1)S(1)} %get-tuple-element.225), kind=kOutput, calls=%fused_computation.13.clone.1 | convolution fusion | flops 672985088 | bytes 8568832 | tf_op jit(solution)/shard_map/while/body/eval_jaxpr/hgak,khd->ahgd/dot_general | solution.py:31
  58.0 2.3 %fusion.66 = f32[2,128,1,128]{1,3,2,0:T(8,128)S(1)} fusion(f32[2,128,1,128]{1,3,2,0:T(8,128)S(1)} %get-tuple-element.240, s32[]{:T(128)} %get-tuple-element.238, f32[1,8,512,640]{2,3,1,0:T(8,128)S(1)} %convolution_bitcast_fusion.4, f32[1,8,512,640]{2,3,1,0:T(8,128)} %get-tuple-element.227, f32[8,512]{1,0:T(8,128)S(1)} %get-tuple-element.228, ...), kind=kOutput, calls=%fused_computation.22.clone.1 | convolution fusion | flops 135806976 | bytes 5325312 | tf_op jit(solution)/shard_map/while/body/eval_jaxpr/hgak,ahgd->khd/dot_general | solution.py:40
  69.0 2.1 %fusion.62 = f32[8,512]{1,0:T(8,128)S(1)} fusion(f32[640,512,8]{1,0,2:T(8,128)S(1)} %get-tuple-element.221, f32[8,512]{1,0:T(8,128)S(1)} %get-tuple-element.222, pred[512,640]{0,1:T(8,128)(4,1)S(1)} %fusion.60), kind=kLoop, calls=%fused_computation.4.clone.1 | loop fusion | flops 10481664 | bytes 10846208 | tf_op jit(solution)/shard_map/while/body/eval_jaxpr/reduce_sum | solution.py:29
  71.2 6.6 %fusion.63 = (bf16[1,8,512,640]{2,3,1,0:T(8,128)(2,1)}, f32[1,8,512,640]{2,3,1,0:T(8,128)}) fusion(f32[8,512]{1,0:T(8,128)S(1)} %fusion.62, f32[8,512]{1,0:T(8,128)S(1)} %get-tuple-element.222, f32[640,512,8]{1,0,2:T(8,128)S(1)} %get-tuple-element.221, pred[512,640]{0,1:T(8,128)(4,1)S(1)} %fusion.60), kind=kLoop, calls=%fused_computation.90.clone.1 | loop fusion | flops 13107200 | bytes 26574848 | tf_op jit(solution)/shard_map/while/body/eval_jaxpr/convert_element_type | solution.py:30
  79.3 2.9 %copy.95 = f32[8,512,128]{1,2,0:T(8,128)} copy(f32[8,512,128]{2,1,0:T(8,128)} %bitcast_convert_fusion.3) | data formatting | bytes 4194304 | tf_op jit(solution)/shard_map/while
  82.2 4.2 %fusion.64 = (f32[8,512]{1,0:T(8,128)S(1)}, bf16[128,8,512]{2,0,1:T(8,128)(2,1)S(1)}) fusion(f32[8,512,128]{1,2,0:T(8,128)} %copy.95, bf16[1,8,512,640]{2,3,1,0:T(8,128)(2,1)} %get-tuple-element.223, bf16[512,1,128]{2,0,1:T(8,128)(2,1)S(1)} %get-tuple-element.224, bf16[128,1,128]{2,0,1:T(8,128)(2,1)S(1)} %get-tuple-element.225), kind=kOutput, calls=%fused_computation.13.clone.1 | convolution fusion | flops 672985088 | bytes 8568832 | tf_op jit(solution)/shard_map/while/body/eval_jaxpr/hgak,khd->ahgd/dot_general | solution.py:31
  87.9 2.3 %fusion.66 = f32[2,128,1,128]{1,3,2,0:T(8,128)S(1)} fusion(f32[2,128,1,128]{1,3,2,0:T(8,128)S(1)} %get-tuple-element.240, s32[]{:T(128)} %get-tuple-element.238, f32[1,8,512,640]{2,3,1,0:T(8,128)S(1)} %convolution_bitcast_fusion.4, f32[1,8,512,640]{2,3,1,0:T(8,128)} %get-tuple-element.227, f32[8,512]{1,0:T(8,128)S(1)} %get-tuple-element.228, ...), kind=kOutput, calls=%fused_computation.22.clone.1 | convolution fusion | flops 135806976 | bytes 5325312 | tf_op jit(solution)/shard_map/while/body/eval_jaxpr/hgak,ahgd->khd/dot_general | solution.py:40
  95.3 2.2 %slice_reduce_fusion.5 = (bf16[32768]{0:T(1024)(128)(2,1)S(1)}, bf16[32768]{0:T(1024)(128)(2,1)S(1)}, bf16[32768]{0:T(1024)(128)(2,1)S(1)}, bf16[32768]{0:T(1024...) fusion(bf16[7,32768]{1,0:T(8,128)(2,1)S(1)} %get-tuple-element.152), kind=kLoop, calls=%fused_computation.68 | loop fusion | bytes 786432 | tf_op jit(solution)/shard_map/slice | solution.py:99
  99.3 3.9 %collective-permute-start.6 = (bf16[128,256]{1,0:T(8,128)(2,1)S(1)}, bf16[128,256]{1,0:T(8,128)(2,1)S(1)}, u32[]{:S(2)}, u32[]{:S(2)}) collective-permute-start(bf16[128,256]{1,0:T(8,128)(2,1)S(1)} %convert_element_type.71), channel_id=1, source_target_pairs={{0,20},{4,24},{8,28},{12,0},{16,4},{20,8},{24,12},{28,16},{1,21},{... | collective-permute-start | bytes 196616 | tf_op jit(solution)/shard_map/ppermute | solution.py:12
  103.2 2.3 %collective-permute-start.7 = (bf16[128,256]{1,0:T(8,128)(2,1)S(1)}, bf16[128,256]{1,0:T(8,128)(2,1)S(1)}, u32[]{:S(2)}, u32[]{:S(2)}) collective-permute-start(bf16[128,256]{1,0:T(8,128)(2,1)S(1)} %convert_element_type.73), channel_id=1, source_target_pairs={{0,24},{4,28},{8,0},{12,4},{16,8},{20,12},{24,16},{28,20},{1,25},{... | collective-permute-start | bytes 196616 | tf_op jit(solution)/shard_map/ppermute | solution.py:12
  105.7 2.0 %collective-permute-start.9 = (bf16[128,256]{1,0:T(8,128)(2,1)S(1)}, bf16[128,256]{1,0:T(8,128)(2,1)S(1)}, u32[]{:S(2)}, u32[]{:S(2)}) collective-permute-start(bf16[128,256]{1,0:T(8,128)(2,1)S(1)} %convert_element_type.77), channel_id=1, source_target_pairs={{0,4},{4,8},{8,12},{12,16},{16,20},{20,24},{24,28},{28,0},{1,5},{5... | collective-permute-start | bytes 196616 | tf_op jit(solution)/shard_map/ppermute | solution.py:12
  109.8 2.9 %collective-permute-done.9 = bf16[128,256]{1,0:T(8,128)(2,1)S(1)} collective-permute-done((bf16[128,256]{1,0:T(8,128)(2,1)S(1)}, bf16[128,256]{1,0:T(8,128)(2,1)S(1)}, u32[]{:S(2)}, u32[]{:S(2)}) %collective-permute-start.9) | collective-permute-done | bytes 65568 | tf_op jit(solution)/shard_map/ppermute | solution.py:12
  112.7 5.2 %convolution_convert_fusion = bf16[128,8192]{1,0:T(8,128)(2,1)} fusion(bf16[1024,8,2,128]{3,2,1,0:T(2,128)(2,1)} %bitcast.208, bf16[128,256]{1,0:T(8,128)(2,1)S(1)} %collective-permute-done.11, bf16[128,256]{1,0:T(8,128)(2,1)S(1)} %collective-permute-done.10, bf16[128,256]{1,0:T(8,128)(2,1)S(1)} %collective-permute-done.9, ...), kind=kOutput, calls=%fused_computation.53 | convolution fusion | flops 538345472 | bytes 6815744 | tf_op jit(solution)/shard_map/dot_general | solution.py:104
  117.9 3.5 %copy.81 = bf16[128,8,8,128]{3,1,2,0:T(8,128)(2,1)} copy(bf16[128,8,8,128]{3,2,1,0:T(8,128)(2,1)} %bitcast.212) | data formatting | bytes 4194304
  121.5 25.0 %reduce-scatter.2.cloned.1.call-done = bf16[32,8192]{1,0:T(8,128)(2,1)} async-done(((bf16[128,8192]{1,0:T(8,128)(2,1)}), bf16[32,8192]{1,0:T(8,128)(2,1)}) %reduce-scatter.2.cloned.1.call-update) | async-done | bytes 524304 | tf_op jit(solution)/shard_map/reduce_scatter | solution.py:103
  (88 shorter events, 36.8 us)
Async XLA Ops:
  7.2 1.6 %copy-start = (bf16[1,128,8192]{2,1,0:T(8,128)(2,1)S(1)}, bf16[1,128,8192]{2,1,0:T(8,128)(2,1)}, u32[]{:S(2)}) copy-start(bf16[1,128,8192]{2,1,0:T(8,128)(2,1)} %param.8) | copy-start | bytes 6291460
  7.2 15.3 %copy-start.3 = (s32[2]{0:T(128)S(1)}, s32[2]{0:T(128)}, u32[]{:S(2)}) copy-start(s32[2]{0:T(128)} %param.13) | copy-start | bytes 28
  7.2 139.3 %reduce-scatter.2.cloned.1.call-start = ((), (), s32[]{:S(2)}) async-start(), calls=%async_computation.1 | async-start | bytes 2621440 | tf_op jit(solution)/shard_map/reduce_scatter | solution.py:103
  11.7 14.4 %copy-start.2 = (bf16[1024,1024]{1,0:T(8,128)(2,1)S(1)}, bf16[1024,1024]{1,0:T(8,128)(2,1)}, u32[]{:S(2)}) copy-start(bf16[1024,1024]{1,0:T(8,128)(2,1)} %param.12) | copy-start | bytes 6291460
  11.7 16.3 %collective-permute-start = (bf16[128,256]{1,0:T(8,128)(2,1)S(1)}, bf16[128,256]{1,0:T(8,128)(2,1)S(1)}, u32[]{:S(2)}, u32[]{:S(2)}) collective-permute-start(bf16[128,256]{1,0:T(8,128)(2,1)S(1)} %fusion.32), channel_id=1, source_target_pairs={{0,12},{4,16},{8,20},{12,24},{16,28},{20,0},{24,4},{28,8},{1,13},{... | collective-permute-start | bytes 196616 | tf_op jit(solution)/shard_map/ppermute | solution.py:12
  15.7 12.4 %collective-permute-start.1 = (bf16[128,256]{1,0:T(8,128)(2,1)S(1)}, bf16[128,256]{1,0:T(8,128)(2,1)S(1)}, u32[]{:S(2)}, u32[]{:S(2)}) collective-permute-start(bf16[128,256]{1,0:T(8,128)(2,1)S(1)} %fusion.32), channel_id=1, source_target_pairs={{0,8},{4,12},{8,16},{12,20},{16,24},{20,28},{24,0},{28,4},{1,9},{5... | collective-permute-start | bytes 196616 | tf_op jit(solution)/shard_map/ppermute | solution.py:12
  17.3 10.8 %collective-permute-start.2 = (bf16[128,256]{1,0:T(8,128)(2,1)S(1)}, bf16[128,256]{1,0:T(8,128)(2,1)S(1)}, u32[]{:S(2)}, u32[]{:S(2)}) collective-permute-start(bf16[128,256]{1,0:T(8,128)(2,1)S(1)} %fusion.32), channel_id=1, source_target_pairs={{0,4},{4,8},{8,12},{12,16},{16,20},{20,24},{24,28},{28,0},{1,5},{5... | collective-permute-start | bytes 196616 | tf_op jit(solution)/shard_map/ppermute | solution.py:12
  18.8 9.3 %collective-permute-start.3 = (bf16[128,256]{1,0:T(8,128)(2,1)S(1)}, bf16[128,256]{1,0:T(8,128)(2,1)S(1)}, u32[]{:S(2)}, u32[]{:S(2)}) collective-permute-start(bf16[128,256]{1,0:T(8,128)(2,1)S(1)} %fusion.32), channel_id=1, source_target_pairs={{0,28},{4,0},{8,4},{12,8},{16,12},{20,16},{24,20},{28,24},{1,29},{... | collective-permute-start | bytes 196616 | tf_op jit(solution)/shard_map/ppermute | solution.py:12
  22.0 6.2 %collective-permute-start.4 = (bf16[128,256]{1,0:T(8,128)(2,1)S(1)}, bf16[128,256]{1,0:T(8,128)(2,1)S(1)}, u32[]{:S(2)}, u32[]{:S(2)}) collective-permute-start(bf16[128,256]{1,0:T(8,128)(2,1)S(1)} %fusion.32), channel_id=1, source_target_pairs={{0,24},{4,28},{8,0},{12,4},{16,8},{20,12},{24,16},{28,20},{1,25},{... | collective-permute-start | bytes 196616 | tf_op jit(solution)/shard_map/ppermute | solution.py:12
  28.0 5.2 %collective-permute-start.5 = (bf16[128,256]{1,0:T(8,128)(2,1)S(1)}, bf16[128,256]{1,0:T(8,128)(2,1)S(1)}, u32[]{:S(2)}, u32[]{:S(2)}) collective-permute-start(bf16[128,256]{1,0:T(8,128)(2,1)S(1)} %fusion.32), channel_id=1, source_target_pairs={{0,20},{4,24},{8,28},{12,0},{16,4},{20,8},{24,12},{28,16},{1,21},{... | collective-permute-start | bytes 196616 | tf_op jit(solution)/shard_map/ppermute | solution.py:12
  97.5 8.2 %collective-permute-start.10 = (bf16[128,256]{1,0:T(8,128)(2,1)S(1)}, bf16[128,256]{1,0:T(8,128)(2,1)S(1)}, u32[]{:S(2)}, u32[]{:S(2)}) collective-permute-start(bf16[128,256]{1,0:T(8,128)(2,1)S(1)} %convert_element_type.79), channel_id=1, source_target_pairs={{0,8},{4,12},{8,16},{12,20},{16,24},{20,28},{24,0},{28,4},{1,9},{5... | collective-permute-start | bytes 196616 | tf_op jit(solution)/shard_map/ppermute | solution.py:12
  99.2 8.9 %collective-permute-start.11 = (bf16[128,256]{1,0:T(8,128)(2,1)S(1)}, bf16[128,256]{1,0:T(8,128)(2,1)S(1)}, u32[]{:S(2)}, u32[]{:S(2)}) collective-permute-start(bf16[128,256]{1,0:T(8,128)(2,1)S(1)} %convert_element_type.81), channel_id=1, source_target_pairs={{0,12},{4,16},{8,20},{12,24},{16,28},{20,0},{24,4},{28,8},{1,13},{... | collective-permute-start | bytes 196616 | tf_op jit(solution)/shard_map/ppermute | solution.py:12
  99.3 8.8 %collective-permute-start.6 = (bf16[128,256]{1,0:T(8,128)(2,1)S(1)}, bf16[128,256]{1,0:T(8,128)(2,1)S(1)}, u32[]{:S(2)}, u32[]{:S(2)}) collective-permute-start(bf16[128,256]{1,0:T(8,128)(2,1)S(1)} %convert_element_type.71), channel_id=1, source_target_pairs={{0,20},{4,24},{8,28},{12,0},{16,4},{20,8},{24,12},{28,16},{1,21},{... | collective-permute-start | bytes 196616 | tf_op jit(solution)/shard_map/ppermute | solution.py:12
  103.2 4.9 %collective-permute-start.7 = (bf16[128,256]{1,0:T(8,128)(2,1)S(1)}, bf16[128,256]{1,0:T(8,128)(2,1)S(1)}, u32[]{:S(2)}, u32[]{:S(2)}) collective-permute-start(bf16[128,256]{1,0:T(8,128)(2,1)S(1)} %convert_element_type.73), channel_id=1, source_target_pairs={{0,24},{4,28},{8,0},{12,4},{16,8},{20,12},{24,16},{28,20},{1,25},{... | collective-permute-start | bytes 196616 | tf_op jit(solution)/shard_map/ppermute | solution.py:12
  105.5 4.3 %collective-permute-start.8 = (bf16[128,256]{1,0:T(8,128)(2,1)S(1)}, bf16[128,256]{1,0:T(8,128)(2,1)S(1)}, u32[]{:S(2)}, u32[]{:S(2)}) collective-permute-start(bf16[128,256]{1,0:T(8,128)(2,1)S(1)} %convert_element_type.75), channel_id=1, source_target_pairs={{0,28},{4,0},{8,4},{12,8},{16,12},{20,16},{24,20},{28,24},{1,29},{... | collective-permute-start | bytes 196616 | tf_op jit(solution)/shard_map/ppermute | solution.py:12
  105.7 7.0 %collective-permute-start.9 = (bf16[128,256]{1,0:T(8,128)(2,1)S(1)}, bf16[128,256]{1,0:T(8,128)(2,1)S(1)}, u32[]{:S(2)}, u32[]{:S(2)}) collective-permute-start(bf16[128,256]{1,0:T(8,128)(2,1)S(1)} %convert_element_type.77), channel_id=1, source_target_pairs={{0,4},{4,8},{8,12},{12,16},{16,20},{20,24},{24,28},{28,0},{1,5},{5... | collective-permute-start | bytes 196616 | tf_op jit(solution)/shard_map/ppermute | solution.py:12
  112.7 33.8 %copy-start.1 = (bf16[1,128,8192]{2,1,0:T(8,128)(2,1)S(1)}, bf16[1,128,8192]{2,1,0:T(8,128)(2,1)}, u32[]{:S(2)}) copy-start(bf16[1,128,8192]{2,1,0:T(8,128)(2,1)} %param.8) | copy-start | bytes 6291460
Sparse Core Ops, SparseCore 0:
  118.0 28.4 reduce-scatter.1
where the time goes:
time: 154 us; the launch traced here: 153 us
  waiting for transfers between devices  34.7 us (23%)
  matrix products  32 us (21%)
  local copies, waits for them, and re-layouts  29.9 us (19%)
  other arithmetic  21.2 us (14%)
  starting transfers between devices  20.9 us (14%)
  between operations  14.3 us (9%)
    reduce_scatter x1, waiting for transfers between devices, shards(): lax.psum_scatter(lax.dot_general(kv_grad, flat_weight, (((1,), (1,)), (()...  25 us
    ppermute x12, starting transfers between devices, shifted(): lax.ppermute(x, axis, [(i, (i + by) % devices) for i in range(devices)])  20.8 us
    convert_element_type x2, other arithmetic, branch_pass(): prob_half = prob_full.astype(jnp.bfloat16)  13.2 us
    unnamed x17, local copies, waits for them, and re-layouts  10.6 us
    ppermute x12, waiting for transfers between devices, shifted(): lax.ppermute(x, axis, [(i, (i + by) % devices) for i in range(devices)])  9.63 us
    dot_general x2, matrix products, branch_pass(): jnp.einsum('hgak,khd->ahgd', prob_half, value_rows, preferred_element_typ...  8.35 us
    while x2, local copies, waits for them, and re-layouts  5.85 us
    dynamic_slice x6, local copies, waits for them, and re-layouts, shards(): lax.map(one_branch, (queries, answer_kv, upstream, chosen))  5.71 us
  transfers between devices with their start and end apart: 13, of which 4 were waited for; matrix products, arithmetic and copies ran while one was open for 6% of the time, Pallas kernels for 0%

commit v1 on v0

v1 whole, which is shorter than its diff:
```python
import functools
import math

import jax
import jax.numpy as jnp
from jax import lax
from jax.experimental import pallas as pl
from jax.experimental.pallas import tpu as pltpu
from jax.sharding import PartitionSpec as P

HD = 128
REACH = 3
BLOCK = 128
HEADS_PER_STEP = 2
OWN, PARTNER, LOW, LOW_PAIR, HIGH, HIGH_PAIR, FAR, SOURCES = range(8)


def dp_permute(x, target):
    devices = lax.axis_size("dp")
    return lax.ppermute(x, "dp", [(i, target(i) % devices) for i in range(devices)])


def far_of(i):
    return i + REACH if i % 2 else i - REACH


def first_own(prompts, me, branches):
    own = jnp.int32(branches - 1)
    for slot in reversed(range(branches)):
        own = jnp.where(prompts[slot] == me, slot, own)
    return own


def branch_at(step, first, prompts, me, branches):
    own = first_own(prompts, me, branches)
    if first:
        return own
    return step + jnp.where(step >= own, 1, 0)


def source_of(prompt, me, devices):
    rel = lax.rem(prompt - me + devices, devices)
    rel = jnp.where(rel > REACH, rel - devices, rel)
    odd = lax.rem(me, 2) == 1
    source = jnp.where(rel == 0, OWN, FAR)
    source = jnp.where(rel == -2, LOW, source)
    source = jnp.where(rel == 2, HIGH, source)
    source = jnp.where(rel == 1, jnp.where(odd, HIGH_PAIR, PARTNER), source)
    source = jnp.where(rel == -1, jnp.where(odd, PARTNER, LOW_PAIR), source)
    source = jnp.where(rel == 3, jnp.where(odd, FAR, HIGH_PAIR), source)
    source = jnp.where(rel == -3, jnp.where(odd, LOW_PAIR, FAR), source)
    return source


def contract(a, b, dim_a, dim_b):
    return lax.dot_general(
        a, b, (((dim_a,), (dim_b,)), ((), ())), preferred_element_type=jnp.float32
    )


def one_head(q_ref, up_ref, out_ref, keys, values, half_grad, half_prob, head, answers, prefix_len):
    scale = HD**-0.5 * math.log2(math.e)
    cols = pl.ds(head * HD, HD)
    rows_at = lax.broadcasted_iota(jnp.int32, (BLOCK, BLOCK), 0)
    keys_at = lax.broadcasted_iota(jnp.int32, (BLOCK, BLOCK), 1)
    allowed = keys_at <= rows_at
    for block in range(answers // BLOCK):
        rows = pl.ds(block * BLOCK, BLOCK)
        seen = prefix_len + (block + 1) * BLOCK
        scores = contract(q_ref[rows, cols], keys[:seen, :], 1, 1)
        last = jnp.where(allowed, scores[:, seen - BLOCK :], -1e30)
        scores = jnp.concatenate([scores[:, : seen - BLOCK], last], axis=1)
        row_max = jnp.max(scores, axis=1, keepdims=True)
        exps = jnp.exp2((scores - row_max) * scale)
        probs = exps * (1.0 / jnp.sum(exps, axis=1, keepdims=True))
        prob_half = probs.astype(jnp.bfloat16)
        context = contract(prob_half, values[:seen, :], 1, 0)
        out_ref[rows, cols] = context.astype(jnp.bfloat16)
        upstream = up_ref[rows, cols]
        prob_grad = contract(upstream, values[:prefix_len, :], 1, 1)
        delta_row = jnp.sum(upstream.astype(jnp.float32) * context, axis=1, keepdims=True)
        score_grad = probs[:, :prefix_len] * (prob_grad - delta_row)
        half_grad[rows, :] = score_grad.astype(jnp.bfloat16)
        half_prob[rows, :] = prob_half[:, :prefix_len]
    key_grad = contract(half_grad[...], q_ref[:, cols], 0, 0)
    value_grad = contract(half_prob[...], up_ref[:, cols], 0, 0)
    return key_grad, value_grad


def attention_kernel(first, devices, branches, info, prompts, *refs):
    if first:
        own_ref, q_ref, k_ref, v_ref, up_ref, out_ref, own_grad = refs[:7]
        keys, values, half_grad, half_prob, grads = refs[7:]
    else:
        own_ref, partner_ref, low_ref, high_ref, far_ref = refs[:5]
        q_ref, k_ref, v_ref, up_ref, _, out_ref = refs[5:11]
        own_grad, partner_grad, low_grad, high_grad, far_grad = refs[11:16]
        keys, values, half_grad, half_prob, grads = refs[16:]
    prefix_len = own_ref.shape[0]
    answers = q_ref.shape[0]
    step, part = pl.program_id(0), pl.program_id(1)
    me = info[0]
    branch = branch_at(step, first, prompts, me, branches)
    source = jnp.int32(OWN) if first else source_of(prompts[branch], me, devices)

    @pl.when((step == 0) & (part == 0))
    def _():
        grads[...] = jnp.zeros_like(grads)

    @pl.when(part == 0)
    def _():
        def take(piece):
            keys[:prefix_len, :] = piece[:, :HD]
            values[:prefix_len, :] = piece[:, HD:]

        if first:
            take(own_ref[...])
        else:
            pieces = (
                own_ref,
                partner_ref,
                low_ref.at[0],
                low_ref.at[1],
                high_ref.at[0],
                high_ref.at[1],
                far_ref,
            )
            for number, piece in enumerate(pieces):

                @pl.when(source == number)
                def _(piece=piece):
                    take(piece[...])

        keys[prefix_len:, :] = k_ref[...]
        values[prefix_len:, :] = v_ref[...]

    for head in range(HEADS_PER_STEP):
        key_grad, value_grad = one_head(
            q_ref, up_ref, out_ref, keys, values, half_grad, half_prob, head, answers, prefix_len
        )
        grads[source, :, :HD] += key_grad
        grads[source, :, HD:] += value_grad

    @pl.when((step == pl.num_programs(0) - 1) & (part == pl.num_programs(1) - 1))
    def _():
        def total(number):
            return jnp.concatenate(
                [grads[number, :, :HD] * HD**-0.5, grads[number, :, HD:]], axis=1
            )

        own_grad[...] = total(OWN)
        if not first:
            partner_grad[...] = total(PARTNER).astype(jnp.bfloat16)
            low_grad[0] = total(LOW).astype(jnp.bfloat16)
            low_grad[1] = total(LOW_PAIR).astype(jnp.bfloat16)
            high_grad[0] = total(HIGH).astype(jnp.bfloat16)
            high_grad[1] = total(HIGH_PAIR).astype(jnp.bfloat16)
            far_grad[...] = total(FAR).astype(jnp.bfloat16)


def attention(first, devices, me, prompts, pieces, query, keys, values, upstream, out):
    branches = prompts.shape[0]
    answers = query.shape[0] // branches
    width = query.shape[1]
    prefix_len = pieces[0].shape[0]
    part_width = HEADS_PER_STEP * HD
    steps = 1 if first else branches - 1

    def at(step, part, info, prompts):
        return branch_at(step, first, prompts, info[0], branches)

    wide = pl.BlockSpec((answers, part_width), lambda s, p, i, b: (at(s, p, i, b), p))
    narrow = pl.BlockSpec((answers, HD), lambda s, p, i, b: (at(s, p, i, b), 0))

    def whole(shape):
        return pl.BlockSpec(shape, lambda s, p, i, b: (0,) * len(shape))

    piece = (prefix_len, 2 * HD)
    in_specs = [whole(x.shape) for x in pieces] + [wide, narrow, narrow, wide]
    operands = [*pieces, query, keys, values, upstream]
    out_shape = [
        jax.ShapeDtypeStruct(query.shape, query.dtype),
        jax.ShapeDtypeStruct(piece, jnp.float32),
    ]
    out_specs = [wide, whole(piece)]
    aliases = {}
    if not first:
        in_specs.append(pl.BlockSpec(memory_space=pl.ANY))
        aliases = {2 + len(operands): 0}
        operands.append(out)
        for shape in (piece, (2, *piece), (2, *piece), piece):
            out_shape.append(jax.ShapeDtypeStruct(shape, jnp.bfloat16))
            out_specs.append(whole(shape))
    seen = prefix_len + (answers + BLOCK) // 2
    work = steps * answers * width
    return pl.pallas_call(
        functools.partial(attention_kernel, first, devices, branches),
        grid_spec=pltpu.PrefetchScalarGridSpec(
            num_scalar_prefetch=2,
            grid=(steps, width // part_width),
            in_specs=in_specs,
            out_specs=out_specs,
            scratch_shapes=[
                pltpu.VMEM((prefix_len + answers, HD), jnp.bfloat16),
                pltpu.VMEM((prefix_len + answers, HD), jnp.bfloat16),
                pltpu.VMEM((answers, prefix_len), jnp.bfloat16),
                pltpu.VMEM((answers, prefix_len), jnp.bfloat16),
                pltpu.VMEM((1 if first else SOURCES, prefix_len, 2 * HD), jnp.float32),
            ],
        ),
        out_shape=out_shape,
        input_output_aliases=aliases,
        compiler_params=pltpu.CompilerParams(dimension_semantics=("arbitrary", "arbitrary")),
        cost_estimate=pl.CostEstimate(
            flops=work * (4 * seen + 6 * prefix_len),
            bytes_accessed=6 * work,
            transcendentals=work // HD * seen,
        ),
        name="first_branch" if first else "other_branches",
    )(me, prompts, *operands)


def shards(prefix, kv_weight, ans_query, ans_kv, d_out, branch_prompt):
    prefix_len = prefix.shape[1]
    model_width = prefix.shape[2]
    columns = kv_weight.shape[2]
    if columns != HD:
        raise ValueError("one kv head")
    devices = lax.axis_size("dp")
    if devices % 2 or devices < 2 * REACH + 1:
        raise ValueError("dp size")
    flat_weight = kv_weight.reshape(kv_weight.shape[0], 2 * columns)
    own_kv = jnp.dot(prefix[0], flat_weight, preferred_element_type=jnp.float32).astype(
        jnp.bfloat16
    )
    me = lax.axis_index("dp").astype(jnp.int32).reshape(1)
    far = dp_permute(own_kv, far_of)
    partner = dp_permute(own_kv, lambda i: i ^ 1)
    pair = jnp.stack([own_kv, partner])
    low = dp_permute(pair, lambda i: i + 2)
    high = dp_permute(pair, lambda i: i - 2)
    answer_keys = ans_kv[:, 0]
    answer_values = ans_kv[:, 1]
    branch = functools.partial(attention, devices=devices, me=me, prompts=branch_prompt)
    out, own_grad = branch(
        True,
        pieces=[own_kv],
        query=ans_query,
        keys=answer_keys,
        values=answer_values,
        upstream=d_out,
        out=None,
    )
    out, more_grad, to_partner, to_low, to_high, to_far = branch(
        False,
        pieces=[own_kv, partner, low, high, far],
        query=ans_query,
        keys=answer_keys,
        values=answer_values,
        upstream=d_out,
        out=out,
    )
    from_far = dp_permute(to_far, far_of)
    from_high = dp_permute(to_low, lambda i: i - 2)
    from_low = dp_permute(to_high, lambda i: i + 2)

    def wide(x):
        return x.astype(jnp.float32)

    partner_sum = (wide(to_partner) + wide(from_high[1]) + wide(from_low[1])).astype(jnp.bfloat16)
    from_partner = dp_permute(partner_sum, lambda i: i ^ 1)
    kv_sum = own_grad + more_grad + wide(from_far) + wide(from_high[0]) + wide(from_low[0])
    kv_grad = (kv_sum + wide(from_partner)).astype(jnp.bfloat16)
    shares = lax.dot_general(
        kv_grad, flat_weight, (((1,), (1,)), ((), ())), preferred_element_type=jnp.float32
    ).astype(jnp.bfloat16)
    rows = sum_over_tensor(shares)
    return (out, rows.reshape(1, *rows.shape))


def sum_over_tensor(shares):
    count = lax.axis_size("tensor")
    index = lax.axis_index("tensor")
    if count & (count - 1):
        raise ValueError("tensor size")
    levels = count.bit_length() - 1
    rows = shares.shape[0] // count
    held = shares.reshape(*([2] * levels), rows, shares.shape[1])
    for level in range(levels):
        bit = 1 << level
        axis = levels - 1 - level
        mine = (index >> level) & 1
        keep = lax.dynamic_index_in_dim(held, mine, axis, keepdims=False)
        give = lax.dynamic_index_in_dim(held, 1 - mine, axis, keepdims=False)
        got = lax.ppermute(give, "tensor", [(i, i ^ bit) for i in range(count)])
        held = (keep.astype(jnp.float32) + got.astype(jnp.float32)).astype(jnp.bfloat16)
    return held


def solution(mesh):
    return jax.shard_map(
        shards,
        mesh=mesh,
        in_specs=(
            P("dp", None, None),
            P(None, None, "tensor"),
            P("dp", "tensor"),
            P("dp", None, "tensor"),
            P("dp", "tensor"),
            P("dp"),
        ),
        out_specs=(P("dp", "tensor"), P("dp", "tensor", None)),
        check_vma=False,
    )
```

time: 154 us -> 92.3 us (0.60)
  Pallas kernels: 0 us -> 34.4 us
  matrix products: 32 us -> 6.72 us
  local copies, waits for them, and re-layouts: 29.9 us -> 6.09 us
  other arithmetic: 21.2 us -> 4.62 us
  between operations: 14.3 us -> 0.79 us
  waiting for transfers between devices: 34.7 us -> 22.8 us
  starting transfers between devices: 20.9 us -> 16.4 us
    pallas_call x0 -> x2, Pallas kernels: none -> 34.4 us  [attention(): pl.pallas_call(functools.partial(attention_kernel, first, devices, branch...]
    reduce_scatter x1 -> x0, waiting for transfers between devices: 25 us -> none  [shards(): lax.psum_scatter(lax.dot_general(kv_grad, flat_weight, (((1,), (1,)), (()...]
    dot_general x11 -> x0, matrix products: 23.9 us -> none  [the longest x2 8.35 us: branch_pass(): jnp.einsum('hgak,khd->ahgd', prob_half, value_rows, preferred_element_typ...]
    ppermute x12 -> x10, waiting for transfers between devices: 9.63 us -> 22.8 us  [the longest x2 15.5 us: sum_over_tensor(): got = lax.ppermute(give, 'tensor', [(i, i ^ bit) for i in range(count)])]
    convert_element_type x2, other arithmetic: 13.2 us -> 2.65 us  [the longest x1 1.78 us: sum_over_tensor(): (keep.astype(jnp.float32) + got.astype(jnp.float32)).astype(jnp.bfloat16)]
    unnamed x17 -> x18, local copies, waits for them, and re-layouts: 10.6 us -> 3.6 us
    while x2 -> x0, local copies, waits for them, and re-layouts: 5.85 us -> none
    dynamic_slice x6 -> x0, local copies, waits for them, and re-layouts: 5.71 us -> none  [shards(): lax.map(one_branch, (queries, answer_kv, upstream, chosen))]
  transfers between devices with their start and end apart: 13 -> 10, of which waited for: 4 -> 4; matrix products, arithmetic and copies ran while one was open for 6% -> 3% of each run, Pallas kernels for 0% -> 18%
where the time goes in v1:
time: 92.3 us; the launch traced here: 91.9 us
  Pallas kernels  34.4 us (37%)
  waiting for transfers between devices  22.8 us (25%)
  starting transfers between devices  16.4 us (18%)
  matrix products  6.72 us (7%)
  local copies, waits for them, and re-layouts  6.09 us (7%)
  other arithmetic  4.62 us (5%)
    pallas_call x2, Pallas kernels, attention(): pl.pallas_call(functools.partial(attention_kernel, first, devices, branch...  34.4 us
    ppermute x2, waiting for transfers between devices, sum_over_tensor(): got = lax.ppermute(give, 'tensor', [(i, i ^ bit) for i in range(count)])  15.5 us
    ppermute x8, starting transfers between devices, dp_permute(): lax.ppermute(x, 'dp', [(i, target(i) % devices) for i in range(devices)])  14.8 us
    ppermute x8, waiting for transfers between devices, dp_permute(): lax.ppermute(x, 'dp', [(i, target(i) % devices) for i in range(devices)])  7.29 us
    dot_general x1, matrix products, shards(): lax.dot_general(kv_grad, flat_weight, (((1,), (1,)), ((), ())), preferred...  3.76 us
    unnamed x18, local copies, waits for them, and re-layouts  3.6 us
    dot_general x1, matrix products, shards(): jnp.dot(prefix[0], flat_weight, preferred_element_type=jnp.float32)  2.96 us
    reshape x1, other arithmetic, shards(): return (out, rows.reshape(1, *rows.shape))  1.95 us
  transfers between devices with their start and end apart: 10, of which 4 were waited for; matrix products, arithmetic and copies ran while one was open for 3% of the time, Pallas kernels for 18%

profile of v1, /device:TPU:0, one launch (start us, length us, event | category | flops | bytes accessed | tf_op | source)
XLA Modules:
  0.0 91.9 jit_solution(9724745897110433162)
XLA Ops:
  0.6 1.6 %copy-done = bf16[1,128,8192]{2,1,0:T(8,128)(2,1)S(1)} copy-done((bf16[1,128,8192]{2,1,0:T(8,128)(2,1)S(1)}, bf16[1,128,8192]{2,1,0:T(8,128)(2,1)}, u32[]{:S(2)}) %copy-start) | copy-done | bytes 2097176
  2.2 3.0 %fusion.7.refs_0_ = bf16[128,256]{1,0:T(8,128)(2,1)S(1)} fusion(bf16[1024,8,2,128]{3,2,1,0:T(2,128)(2,1)} %bitcast.59, bf16[1,128,8192]{2,1,0:T(8,128)(2,1)S(1)} %copy-done), kind=kOutput, calls=%fused_computation.9 | convolution fusion | flops 536903680 | bytes 6356992 | tf_op jit(solution)/shard_map/dot_general | solution.py:233
  5.2 3.0 %collective-permute-start = (bf16[128,256]{1,0:T(8,128)(2,1)S(1)}, bf16[128,256]{1,0:T(8,128)(2,1)S(1)}, u32[]{:S(2)}, u32[]{:S(2)}) collective-permute-start(bf16[128,256]{1,0:T(8,128)(2,1)S(1)} %fusion.7.refs_0_), channel_id=1, source_target_pairs={{0,4},{4,0},{8,12},{12,8},{16,20},{20,16},{24,28},{28,24},{1,5},{5... | collective-permute-start | bytes 196616 | tf_op jit(solution)/shard_map/ppermute | solution.py:20
  8.2 2.6 %collective-permute-start.3 = (bf16[128,256]{1,0:T(8,128)(2,1)S(1)}, bf16[128,256]{1,0:T(8,128)(2,1)S(1)}, u32[]{:S(2)}, u32[]{:S(2)}) collective-permute-start(bf16[128,256]{1,0:T(8,128)(2,1)S(1)} %fusion.7.refs_0_), channel_id=1, source_target_pairs={{0,20},{4,16},{8,28},{12,24},{16,4},{20,0},{24,12},{28,8},{1,21},{... | collective-permute-start | bytes 196616 | tf_op jit(solution)/shard_map/ppermute | solution.py:20
  10.8 0.7 fusion.18
  11.6 1.6 %collective-permute-start.1 = (bf16[2,128,256]{2,1,0:T(8,128)(2,1)S(1)}, bf16[2,128,256]{2,1,0:T(8,128)(2,1)S(1)}, u32[]{:S(2)}, u32[]{:S(2)}) collective-permute-start(bf16[2,128,256]{2,1,0:T(8,128)(2,1)S(1)} %pad_maximum_fusion), channel_id=1, source_target_pairs={{0,8},{4,12},{8,16},{12,20},{16,24},{20,28},{24,0},{28,4},{1,9},{5... | collective-permute-start | bytes 393224 | tf_op jit(solution)/shard_map/ppermute | solution.py:20
  13.2 2.2 %collective-permute-start.2 = (bf16[2,128,256]{2,1,0:T(8,128)(2,1)S(1)}, bf16[2,128,256]{2,1,0:T(8,128)(2,1)S(1)}, u32[]{:S(2)}, u32[]{:S(2)}) collective-permute-start(bf16[2,128,256]{2,1,0:T(8,128)(2,1)S(1)} %pad_maximum_fusion), channel_id=1, source_target_pairs={{0,24},{4,28},{8,0},{12,4},{16,8},{20,12},{24,16},{28,20},{1,25},{... | collective-permute-start | bytes 393224 | tf_op jit(solution)/shard_map/ppermute | solution.py:20
  15.5 0.9 copy_bitcast_fusion
  16.3 16.9 %first_branch.1 = (bf16[1024,1024]{1,0:T(8,128)(2,1)}, f32[128,256]{1,0:T(8,128)}) custom-call(s32[1]{0:T(128)} %bitcast.info, s32[2]{0:T(128)} %prompts.3, bf16[128,256]{1,0:T(8,128)(2,1)} %copy-done.3, bf16[1024,1024]{1,0:T(8,128)(2,1)} %refs_5_.1, bf16[1024,128]{1,0:T(8,128)(2,1)} %get-tuple-element.21.refs_2_.refs_6_, ...), custom_call_target="tpu_custom_call" | custom-call | flops 1342177280 | bytes 3145728 | tf_op jit(solution)/shard_map/first_branch/pallas_call | solution.py:196
  33.3 0.6 copy-done.8
  33.9 17.5 %other_branches.1 = (bf16[1024,1024]{1,0:T(8,128)(2,1)}, f32[128,256]{1,0:T(8,128)}, bf16[128,256]{1,0:T(8,128)(2,1)}, bf16[2,128,256]{2,1,0:T(8,128)(2,1)}, bf1...) custom-call(s32[1]{0:T(128)} %bitcast.info, s32[2]{0:T(128)} %prompts.3, ...), custom_call_target="tpu_custom_call", output_to_operand_aliasing={{0}: (11, {})} | custom-call | flops 1342177280 | bytes 3145728 | tf_op jit(solution)/shard_map/other_branches/pallas_call | solution.py:196
  51.5 3.8 %collective-permute-start.5 = (bf16[2,128,256]{2,1,0:T(8,128)(2,1)}, bf16[2,128,256]{2,1,0:T(8,128)(2,1)S(1)}, u32[]{:S(2)}, u32[]{:S(2)}) collective-permute-start(bf16[2,128,256]{2,1,0:T(8,128)(2,1)} %get-tuple-element.15), channel_id=1, source_target_pairs={{0,24},{4,28},{8,0},{12,4},{16,8},{20,12},{24,16},{28,20},{1,25},{... | collective-permute-start | bytes 393224 | tf_op jit(solution)/shard_map/ppermute | solution.py:20
  55.3 4.5 %collective-permute-done.6 = bf16[2,128,256]{2,1,0:T(8,128)(2,1)S(1)} collective-permute-done((bf16[2,128,256]{2,1,0:T(8,128)(2,1)}, bf16[2,128,256]{2,1,0:T(8,128)(2,1)S(1)}, u32[]{:S(2)}, u32[]{:S(2)}) %collective-permute-start.6) | collective-permute-done | bytes 131104 | tf_op jit(solution)/shard_map/ppermute | solution.py:20
  59.8 0.9 fusion.14
  60.7 1.6 %collective-permute-start.7 = (bf16[128,256]{1,0:T(8,128)(2,1)S(1)}, bf16[128,256]{1,0:T(8,128)(2,1)S(1)}, u32[]{:S(2)}, u32[]{:S(2)}) collective-permute-start(bf16[128,256]{1,0:T(8,128)(2,1)S(1)} %fusion.14), channel_id=1, source_target_pairs={{0,4},{4,0},{8,12},{12,8},{16,20},{20,16},{24,28},{28,24},{1,5},{5... | collective-permute-start | bytes 196616 | tf_op jit(solution)/shard_map/ppermute | solution.py:20
  62.2 2.8 %collective-permute-done.7 = bf16[128,256]{1,0:T(8,128)(2,1)S(1)} collective-permute-done((bf16[128,256]{1,0:T(8,128)(2,1)S(1)}, bf16[128,256]{1,0:T(8,128)(2,1)S(1)}, u32[]{:S(2)}, u32[]{:S(2)}) %collective-permute-start.7) | collective-permute-done | bytes 65568 | tf_op jit(solution)/shard_map/ppermute | solution.py:20
  65.0 3.8 %convolution_convert_fusion = bf16[128,8192]{1,0:T(8,128)(2,1)S(1)} fusion(bf16[1024,8,2,128]{3,2,1,0:T(2,128)(2,1)} %bitcast.60, bf16[128,256]{1,0:T(8,128)(2,1)S(1)} %collective-permute-done.7, bf16[128,256]{1,0:T(8,128)(2,1)S(1)} %collective-permute-done.4, f32[128,256]{1,0:T(8,128)S(1)} %copy-done.7, f32[128,256]{1,0:T(8,128)} %get-tuple-element.13, ...), kind=kOutput, calls=%fused_computation | convolution fusion | flops 538247168 | bytes 6815744 | tf_op jit(solution)/shard_map/dot_general | solution.py:274
  68.8 1.3 %copy-done.1 = bf16[128,8192]{1,0:T(8,128)(2,1)} copy-done((bf16[128,8192]{1,0:T(8,128)(2,1)}, bf16[128,8192]{1,0:T(8,128)(2,1)S(1)}, u32[]{:S(2)}) %copy-start.1) | copy-done | bytes 2097176
  70.3 2.8 %collective-permute-done.8 = bf16[2,32,8192]{2,1,0:T(8,128)(2,1)} collective-permute-done((bf16[2,32,8192]{2,1,0:T(8,128)(2,1)S(1)}, bf16[2,32,8192]{2,1,0:T(8,128)(2,1)}, u32[]{:S(2)}, u32[]{:S(2)}) %collective-permute-start.8) | collective-permute-done | bytes 1048608 | tf_op jit(solution)/shard_map/ppermute | solution.py:295
  73.0 1.8 %fusion.5 = bf16[2,32,8192]{2,1,0:T(8,128)(2,1)S(1)} fusion(bf16[2,32,8192]{2,1,0:T(8,128)(2,1)} %collective-permute-done.8, bf16[2,2,32,8192]{3,2,1,0:T(8,128)(2,1)} %bitcast.58, s32[]{:T(128)S(6)} %select_n.14), kind=kLoop, calls=%fused_computation.7 | loop fusion | flops 2097152 | bytes 3145732 | tf_op jit(solution)/shard_map/convert_element_type | solution.py:296
  74.8 0.8 dynamic-slice_bitcast_fusion.1
  75.7 1.5 %collective-permute-start.9 = (bf16[32,8192]{1,0:T(8,128)(2,1)}, bf16[32,8192]{1,0:T(8,128)(2,1)}, u32[]{:S(2)}, u32[]{:S(2)}) collective-permute-start(bf16[32,8192]{1,0:T(8,128)(2,1)} %dynamic-slice_bitcast_fusion.1), channel_id=1, source_target_pairs={{0,2},{1,3},{2,0},{3,1},{4,6},{5,7},{6,4},{7,5},{8,10},{9,11},{10,... | collective-permute-start | bytes 1572872 | tf_op jit(solution)/shard_map/ppermute | solution.py:295
  77.2 12.8 %collective-permute-done.9 = bf16[32,8192]{1,0:T(8,128)(2,1)} collective-permute-done((bf16[32,8192]{1,0:T(8,128)(2,1)}, bf16[32,8192]{1,0:T(8,128)(2,1)}, u32[]{:S(2)}, u32[]{:S(2)}) %collective-permute-start.9) | collective-permute-done | bytes 524320 | tf_op jit(solution)/shard_map/ppermute | solution.py:295
  89.9 2.0 %fusion.13 = bf16[1,32,8192]{2,1,0:T(8,128)(2,1)} fusion(bf16[32,8192]{1,0:T(8,128)(2,1)} %collective-permute-done.9, bf16[2,32,8192]{2,1,0:T(8,128)(2,1)S(1)} %fusion.5, s32[]{:T(128)S(6)} %select_n.16), kind=kLoop, calls=%fused_computation.13 | loop fusion | flops 1048576 | bytes 1572868 | tf_op jit(solution)/shard_map/reshape | solution.py:278
  (26 shorter events, 0.3 us)
Async XLA Ops:
  0.6 1.6 %copy-start = (bf16[1,128,8192]{2,1,0:T(8,128)(2,1)S(1)}, bf16[1,128,8192]{2,1,0:T(8,128)(2,1)}, u32[]{:S(2)}) copy-start(bf16[1,128,8192]{2,1,0:T(8,128)(2,1)} %param.6) | copy-start | bytes 6291460
  2.2 8.6 %copy-start.2 = (bf16[1024,2,128]{2,1,0:T(2,128)(2,1)S(1)}, bf16[1024,2,128]{2,1,0:T(2,128)(2,1)}, u32[]{:S(2)}) copy-start(bf16[1024,2,128]{2,1,0:T(2,128)(2,1)} %param.9) | copy-start | bytes 1572868
  5.2 11.1 %copy-start.3 = (bf16[128,256]{1,0:T(8,128)(2,1)}, bf16[128,256]{1,0:T(8,128)(2,1)S(1)}, u32[]{:S(2)}) copy-start(bf16[128,256]{1,0:T(8,128)(2,1)S(1)} %fusion.7.refs_0_) | copy-start | bytes 196612
  5.2 6.3 %collective-permute-start = (bf16[128,256]{1,0:T(8,128)(2,1)S(1)}, bf16[128,256]{1,0:T(8,128)(2,1)S(1)}, u32[]{:S(2)}, u32[]{:S(2)}) collective-permute-start(bf16[128,256]{1,0:T(8,128)(2,1)S(1)} %fusion.7.refs_0_), channel_id=1, source_target_pairs={{0,4},{4,0},{8,12},{12,8},{16,20},{20,16},{24,28},{28,24},{1,5},{5... | collective-permute-start | bytes 196616 | tf_op jit(solution)/shard_map/ppermute | solution.py:20
  8.2 25.0 %collective-permute-start.3 = (bf16[128,256]{1,0:T(8,128)(2,1)S(1)}, bf16[128,256]{1,0:T(8,128)(2,1)S(1)}, u32[]{:S(2)}, u32[]{:S(2)}) collective-permute-start(bf16[128,256]{1,0:T(8,128)(2,1)S(1)} %fusion.7.refs_0_), channel_id=1, source_target_pairs={{0,20},{4,16},{8,28},{12,24},{16,4},{20,0},{24,12},{28,8},{1,21},{... | collective-permute-start | bytes 196616 | tf_op jit(solution)/shard_map/ppermute | solution.py:20
  11.5 21.7 %copy-start.4 = (bf16[128,256]{1,0:T(8,128)(2,1)}, bf16[128,256]{1,0:T(8,128)(2,1)S(1)}, u32[]{:S(2)}) copy-start(bf16[128,256]{1,0:T(8,128)(2,1)S(1)} %collective-permute-done.refs_1_) | copy-start | bytes 196612
  11.6 21.7 %collective-permute-start.1 = (bf16[2,128,256]{2,1,0:T(8,128)(2,1)S(1)}, bf16[2,128,256]{2,1,0:T(8,128)(2,1)S(1)}, u32[]{:S(2)}, u32[]{:S(2)}) collective-permute-start(bf16[2,128,256]{2,1,0:T(8,128)(2,1)S(1)} %pad_maximum_fusion), channel_id=1, source_target_pairs={{0,8},{4,12},{8,16},{12,20},{16,24},{20,28},{24,0},{28,4},{1,9},{5... | collective-permute-start | bytes 393224 | tf_op jit(solution)/shard_map/ppermute | solution.py:20
  13.2 20.0 %collective-permute-start.2 = (bf16[2,128,256]{2,1,0:T(8,128)(2,1)S(1)}, bf16[2,128,256]{2,1,0:T(8,128)(2,1)S(1)}, u32[]{:S(2)}, u32[]{:S(2)}) collective-permute-start(bf16[2,128,256]{2,1,0:T(8,128)(2,1)S(1)} %pad_maximum_fusion), channel_id=1, source_target_pairs={{0,24},{4,28},{8,0},{12,4},{16,8},{20,12},{24,16},{28,20},{1,25},{... | collective-permute-start | bytes 393224 | tf_op jit(solution)/shard_map/ppermute | solution.py:20
  33.2 0.6 copy-start.8
  33.2 0.7 copy-start.5
  33.3 0.7 copy-start.6
  33.9 31.1 %copy-start.7 = (f32[128,256]{1,0:T(8,128)S(1)}, f32[128,256]{1,0:T(8,128)}, u32[]{:S(2)}) copy-start(f32[128,256]{1,0:T(8,128)} %get-tuple-element.12) | copy-start | bytes 393220
  51.5 8.3 %collective-permute-start.6 = (bf16[2,128,256]{2,1,0:T(8,128)(2,1)}, bf16[2,128,256]{2,1,0:T(8,128)(2,1)S(1)}, u32[]{:S(2)}, u32[]{:S(2)}) collective-permute-start(bf16[2,128,256]{2,1,0:T(8,128)(2,1)} %get-tuple-element.16), channel_id=1, source_target_pairs={{0,8},{4,12},{8,16},{12,20},{16,24},{20,28},{24,0},{28,4},{1,9},{5... | collective-permute-start | bytes 393224 | tf_op jit(solution)/shard_map/ppermute | solution.py:20
  51.5 8.3 %collective-permute-start.5 = (bf16[2,128,256]{2,1,0:T(8,128)(2,1)}, bf16[2,128,256]{2,1,0:T(8,128)(2,1)S(1)}, u32[]{:S(2)}, u32[]{:S(2)}) collective-permute-start(bf16[2,128,256]{2,1,0:T(8,128)(2,1)} %get-tuple-element.15), channel_id=1, source_target_pairs={{0,24},{4,28},{8,0},{12,4},{16,8},{20,12},{24,16},{28,20},{1,25},{... | collective-permute-start | bytes 393224 | tf_op jit(solution)/shard_map/ppermute | solution.py:20
  55.3 6.9 %collective-permute-start.4 = (bf16[128,256]{1,0:T(8,128)(2,1)}, bf16[128,256]{1,0:T(8,128)(2,1)S(1)}, u32[]{:S(2)}, u32[]{:S(2)}) collective-permute-start(bf16[128,256]{1,0:T(8,128)(2,1)} %get-tuple-element.14), channel_id=1, source_target_pairs={{0,20},{4,16},{8,28},{12,24},{16,4},{20,0},{24,12},{28,8},{1,21},{... | collective-permute-start | bytes 196616 | tf_op jit(solution)/shard_map/ppermute | solution.py:20
  60.7 4.3 %collective-permute-start.7 = (bf16[128,256]{1,0:T(8,128)(2,1)S(1)}, bf16[128,256]{1,0:T(8,128)(2,1)S(1)}, u32[]{:S(2)}, u32[]{:S(2)}) collective-permute-start(bf16[128,256]{1,0:T(8,128)(2,1)S(1)} %fusion.14), channel_id=1, source_target_pairs={{0,4},{4,0},{8,12},{12,8},{16,20},{20,16},{24,28},{28,24},{1,5},{5... | collective-permute-start | bytes 196616 | tf_op jit(solution)/shard_map/ppermute | solution.py:20
  68.8 1.3 %copy-start.1 = (bf16[128,8192]{1,0:T(8,128)(2,1)}, bf16[128,8192]{1,0:T(8,128)(2,1)S(1)}, u32[]{:S(2)}) copy-start(bf16[128,8192]{1,0:T(8,128)(2,1)S(1)} %convolution_convert_fusion) | copy-start | bytes 6291460
  70.2 2.9 %collective-permute-start.8 = (bf16[2,32,8192]{2,1,0:T(8,128)(2,1)S(1)}, bf16[2,32,8192]{2,1,0:T(8,128)(2,1)}, u32[]{:S(2)}, u32[]{:S(2)}) collective-permute-start(bf16[2,32,8192]{2,1,0:T(8,128)(2,1)S(1)} %dynamic-slice_bitcast_fusion), channel_id=1, source_target_pairs={{0,1},{1,0},{2,3},{3,2},{4,5},{5,4},{6,7},{7,6},{8,9},{9,8},{10,11... | collective-permute-start | bytes 3145736 | tf_op jit(solution)/shard_map/ppermute | solution.py:295
  75.7 14.3 %collective-permute-start.9 = (bf16[32,8192]{1,0:T(8,128)(2,1)}, bf16[32,8192]{1,0:T(8,128)(2,1)}, u32[]{:S(2)}, u32[]{:S(2)}) collective-permute-start(bf16[32,8192]{1,0:T(8,128)(2,1)} %dynamic-slice_bitcast_fusion.1), channel_id=1, source_target_pairs={{0,2},{1,3},{2,0},{3,1},{4,6},{5,7},{6,4},{7,5},{8,10},{9,11},{10,... | collective-permute-start | bytes 1572872 | tf_op jit(solution)/shard_map/ppermute | solution.py:295

commit v2 on v0

v2 whole, which is shorter than its diff:
```python
import functools
import math

import jax
import jax.numpy as jnp
from jax import lax
from jax.experimental import pallas as pl
from jax.experimental.pallas import tpu as pltpu
from jax.sharding import PartitionSpec as P

HD = 128
REACH = 3
BLOCK = 128
ROWS = 128
TALL = 4
TILE = 32
CHUNKS = 4
VMEM = 24 << 20
NOTES = 16
OWN, PARTNER, LOW, LOW_PAIR, HIGH, HIGH_PAIR, FAR = range(7)


def dp_permute(x, target):
    devices = lax.axis_size("dp")
    return lax.ppermute(x, "dp", [(i, target(i) % devices) for i in range(devices)])


def far_of(i):
    return i + REACH if i % 2 else i - REACH


def first_own(prompts, me, branches):
    own = jnp.int32(branches - 1)
    for slot in reversed(range(branches)):
        own = jnp.where(prompts[slot] == me, slot, own)
    return own


def other_branch(step, prompts, me, branches):
    own = first_own(prompts, me, branches)
    return step + jnp.where(step >= own, 1, 0)


def source_of(prompt, me, devices):
    rel = lax.rem(prompt - me + devices, devices)
    rel = jnp.where(rel > REACH, rel - devices, rel)
    odd = lax.rem(me, 2) == 1
    source = jnp.where(rel == 0, OWN, FAR)
    source = jnp.where(rel == -2, LOW, source)
    source = jnp.where(rel == 2, HIGH, source)
    source = jnp.where(rel == 1, jnp.where(odd, HIGH_PAIR, PARTNER), source)
    source = jnp.where(rel == -1, jnp.where(odd, PARTNER, LOW_PAIR), source)
    source = jnp.where(rel == 3, jnp.where(odd, FAR, HIGH_PAIR), source)
    source = jnp.where(rel == -3, jnp.where(odd, LOW_PAIR, FAR), source)
    return source


def contract(a, b, dim_a, dim_b):
    return lax.dot_general(
        a, b, (((dim_a,), (dim_b,)), ((), ())), preferred_element_type=jnp.float32
    )


def split_pairs(pairs, wide):
    rows = pairs.shape[0] // 2
    wide[...] = pairs.astype(jnp.float32)
    return [wide[pl.ds(at, rows, stride=2), :].astype(jnp.bfloat16) for at in range(2)]


def load_split(chunk, pairs, wide, split):
    size = wide.shape[1]
    keys, values = split_pairs(pairs[chunk * size : (chunk + 1) * size, :], wide.at[chunk % 2])
    split[chunk % 2, :, :HD] = keys
    split[chunk % 2, :, HD:] = values


def project_kernel(info, prompts, prefix_ref, weight_ref, out_ref, rows, pairs, wide, split, sems):
    depth = rows.shape[1] // CHUNKS
    copies = []
    for chunk in range(CHUNKS):
        deep = pl.ds(chunk * depth, depth)
        both = pl.ds(chunk * 2 * depth, 2 * depth)
        copies.append(
            (
                pltpu.make_async_copy(weight_ref.at[both, :], pairs.at[both, :], sems.at[0, chunk]),
                pltpu.make_async_copy(prefix_ref.at[:, deep], rows.at[:, deep], sems.at[1, chunk]),
            )
        )
    for pair in copies:
        for copy in pair:
            copy.start()
    total = jnp.zeros((rows.shape[0], out_ref.shape[1]), jnp.float32)
    for chunk in range(CHUNKS + 1):
        if chunk < CHUNKS:
            for copy in copies[chunk]:
                copy.wait()
            load_split(chunk, pairs, wide, split)
        if chunk:
            part = rows[:, (chunk - 1) * depth : chunk * depth]
            total += contract(part, split[(chunk - 1) % 2], 1, 0)
    out_ref[: rows.shape[0], :] = total.astype(out_ref.dtype)
    at = lax.broadcasted_iota(jnp.int32, (NOTES, out_ref.shape[1]), 0)
    notes = jnp.zeros(at.shape, jnp.float32)
    branches = prompts.shape[0]
    own = first_own(prompts, info[0], branches)
    for number in range(branches - 1):
        prompt = jnp.where(number >= own, prompts[number + 1], prompts[number])
        notes = jnp.where(at == number, prompt.astype(jnp.float32), notes)
    out_ref[rows.shape[0] :, :] = notes.astype(out_ref.dtype)


def project(me, prompts, prefix, kv_weight):
    prefix_len, model_width = prefix.shape
    there = pl.BlockSpec(memory_space=pl.ANY)
    return pl.pallas_call(
        project_kernel,
        in_specs=[pl.BlockSpec(memory_space=pltpu.SMEM)] * 2 + [there, there],
        out_specs=pl.BlockSpec(memory_space=pltpu.VMEM),
        out_shape=jax.ShapeDtypeStruct((prefix_len + NOTES, 2 * HD), jnp.bfloat16),
        scratch_shapes=[
            pltpu.VMEM(prefix.shape, jnp.bfloat16),
            pltpu.VMEM((2 * model_width, HD), jnp.bfloat16),
            pltpu.VMEM((2, 2 * model_width // CHUNKS, HD), jnp.float32),
            pltpu.VMEM((2, model_width // CHUNKS, 2 * HD), jnp.bfloat16),
            pltpu.SemaphoreType.DMA((2, CHUNKS)),
        ],
        cost_estimate=pl.CostEstimate(
            flops=4 * prefix_len * model_width * HD,
            bytes_accessed=2 * model_width * (prefix_len + 2 * HD),
            transcendentals=0,
        ),
        name="project",
    )(me, prompts, prefix, kv_weight.reshape(2 * model_width, HD))


def back_kernel(index, *refs):
    *grads, weight_ref, far_give, far_keep, near_give, near_keep, wide, split = refs
    depth = far_give.shape[1] // CHUNKS
    rows = far_give.shape[0]
    half, side = index[0] >> 1, index[0] & 1
    owners = (
        2 * (1 - half) + 1 - side,
        2 * (1 - half) + side,
        2 * half + 1 - side,
        2 * half + side,
    )
    parts = []
    for owner in owners:
        at = pl.ds(pl.multiple_of(owner * rows, rows), rows)
        total = grads[0][at, :].astype(jnp.float32)
        for grad in grads[1:]:
            total = total + grad[at, :].astype(jnp.float32)
        parts.append(total.astype(jnp.bfloat16))
    kv_grad = jnp.concatenate(parts, axis=0)
    for chunk in range(CHUNKS + 1):
        if chunk < CHUNKS:
            load_split(chunk, weight_ref, wide, split)
        if chunk:
            share = contract(kv_grad, split[(chunk - 1) % 2], 1, 1).astype(jnp.bfloat16)
            cols = pl.ds((chunk - 1) * depth, depth)
            for number, out in enumerate((far_give, far_keep, near_give, near_keep)):
                out[:, cols] = share[number * rows : (number + 1) * rows]


def back_shares(index, grads, kv_weight, count):
    model_width = kv_weight.shape[0]
    rows = grads[0].shape[0] // count
    here = pl.BlockSpec(memory_space=pltpu.VMEM)
    return pl.pallas_call(
        back_kernel,
        in_specs=[pl.BlockSpec(memory_space=pltpu.SMEM)]
        + [here] * (len(grads) + 1),
        out_specs=[here] * 4,
        out_shape=[jax.ShapeDtypeStruct((rows, model_width), jnp.bfloat16)] * 4,
        scratch_shapes=[
            pltpu.VMEM((2, 2 * model_width // CHUNKS, HD), jnp.float32),
            pltpu.VMEM((2, model_width // CHUNKS, 2 * HD), jnp.bfloat16),
        ],
        compiler_params=pltpu.CompilerParams(vmem_limit_bytes=VMEM),
        cost_estimate=pl.CostEstimate(
            flops=4 * grads[0].shape[0] * model_width * HD,
            bytes_accessed=2 * model_width * (grads[0].shape[0] + 2 * HD),
            transcendentals=0,
        ),
        name="back_shares",
    )(index, *grads, kv_weight.reshape(2 * model_width, HD))


def head_pass(heads, base, q_ref, up_ref, out_ref, keys, values, scratch, prefix_len):
    answers = keys.shape[0] - prefix_len
    scale = HD**-0.5 * math.log2(math.e)
    units = [(at, block) for at in range(0, len(heads), TALL) for block in range(answers // ROWS)]
    scores_at, probs_at, lead_at, half_grad, half_prob = scratch
    tall_rows = min(TALL, len(heads)) * ROWS

    def place(unit):
        at, block = units[unit]
        mine = range(at, min(at + TALL, len(heads)))
        return mine, block * ROWS, prefix_len + (block + 1) * ROWS

    def tall(ref, unit):
        mine, start, _ = place(unit)
        rows = pl.ds(pl.multiple_of(base + start, ROWS), ROWS)
        return jnp.concatenate(
            [ref[rows, heads[at] * HD : (heads[at] + 1) * HD] for at in mine], axis=0
        )

    def score(unit):
        seen = place(unit)[2]
        scores_at[unit % 2, :, :seen] = contract(tall(q_ref, unit), keys[:seen, :], 1, 1)

    def soften(unit):
        slot = unit % 2
        seen = place(unit)[2]
        for tile in range(tall_rows // TILE):
            rows = pl.ds(tile * TILE, TILE)
            first = tile * TILE % ROWS
            edge = seen - ROWS + first // BLOCK * BLOCK
            scores = scores_at[slot, rows, : edge + BLOCK]
            rows_at = lax.broadcasted_iota(jnp.int32, (TILE, BLOCK), 0) + first % BLOCK
            keys_at = lax.broadcasted_iota(jnp.int32, (TILE, BLOCK), 1)
            last = jnp.where(keys_at <= rows_at, scores[:, edge:], -jnp.inf)
            scores = jnp.concatenate([scores[:, :edge], last], axis=1)
            row_max = jnp.max(scores, axis=1, keepdims=True)
            exps = jnp.exp2((scores - row_max) * scale)
            probs = exps * (1.0 / jnp.sum(exps, axis=1, keepdims=True))
            lead_at[slot, rows, :] = probs[:, :prefix_len]
            probs_at[slot, rows, : edge + BLOCK] = probs.astype(jnp.bfloat16)
            if edge + BLOCK < seen:
                probs_at[slot, rows, edge + BLOCK : seen] = jnp.zeros(
                    (TILE, seen - edge - BLOCK), jnp.bfloat16
                )

    def finish(unit):
        slot = unit % 2
        mine, start, seen = place(unit)
        context = contract(probs_at[slot, :, :seen], values[:seen, :], 1, 0)
        upstream = tall(up_ref, unit)
        prob_grad = contract(upstream, values[:prefix_len, :], 1, 1)
        for number, head in enumerate(mine):
            out_ref[start : start + ROWS, head * HD : (head + 1) * HD] = context[
                number * ROWS : (number + 1) * ROWS
            ].astype(jnp.bfloat16)
        delta_row = jnp.sum(upstream.astype(jnp.float32) * context, axis=1, keepdims=True)
        score_grad = lead_at[slot] * (prob_grad - delta_row)
        at = pl.ds(unit * tall_rows, tall_rows)
        half_grad[at, :] = score_grad.astype(jnp.bfloat16)
        half_prob[at, :] = probs_at[slot, :, :prefix_len]

    score(0)
    for unit in range(len(units)):
        if unit + 1 < len(units):
            score(unit + 1)
        soften(unit)
        if unit:
            finish(unit - 1)
    finish(len(units) - 1)

    def gathered(ref):
        return jnp.concatenate([tall(ref, unit) for unit in range(len(units))], axis=0)

    key_grad = contract(half_grad[...], gathered(q_ref), 0, 0)
    value_grad = contract(half_prob[...], gathered(up_ref), 0, 0)
    return jnp.concatenate([key_grad * HD**-0.5, value_grad], axis=1)


def fill(keys, values, piece, kv_ref, base, wide):
    size = wide.shape[0]
    prefix_len = keys.shape[0] - size // 2
    keys[:prefix_len, :] = piece[:prefix_len, :HD]
    values[:prefix_len, :] = piece[:prefix_len, HD:]
    pairs = kv_ref[pl.ds(pl.multiple_of(2 * base, size), size), :]
    keys[prefix_len:, :], values[prefix_len:, :] = split_pairs(pairs, wide)


def branch_pass(heads, base, source, pieces, q_ref, kv_ref, up_ref, out_ref, buffers):
    wide, keys, values, *scratch = buffers
    prefix_len = keys.shape[0] - wide.shape[0] // 2
    if len(pieces) == 1:
        fill(keys, values, pieces[0], kv_ref, base, wide)
    else:
        for number, piece in enumerate(pieces):

            @pl.when(source == number)
            def _(piece=piece):
                fill(keys, values, piece, kv_ref, base, wide)

    return head_pass(heads, base, q_ref, up_ref, out_ref, keys, values, scratch, prefix_len)


def own_kernel(heads, answers, branches, later, info, prompts, own_ref, q_ref, kv_ref, up_ref, *refs):
    out_ref, own_grad, *buffers = refs[1:] if later else refs
    base = first_own(prompts, info[0], branches) * answers
    own_grad[...] = branch_pass(
        heads, base, None, [own_ref], q_ref, kv_ref, up_ref, out_ref, buffers
    )


def other_kernel(heads, answers, branches, devices, info, prompts, *refs):
    own_ref, partner_ref, low_ref, high_ref, far_ref = refs[:5]
    q_ref, kv_ref, up_ref, _, out_ref, own_grad, far_grad, grad_ref = refs[5:13]
    *buffers, own_total, far_total = refs[13:]
    step = pl.program_id(0)
    me = info[0]
    branch = other_branch(step, prompts, me, branches)
    source = source_of(prompts[branch], me, devices)
    pieces = [
        own_ref,
        partner_ref,
        low_ref.at[0],
        low_ref.at[1],
        high_ref.at[0],
        high_ref.at[1],
        far_ref,
    ]
    grad = branch_pass(
        heads, branch * answers, source, pieces, q_ref, kv_ref, up_ref, out_ref, buffers
    )
    own_part = jnp.where(source == OWN, grad, 0.0)
    far_part = jnp.where(source == FAR, grad, 0.0)
    grad_ref[step] = grad.astype(jnp.bfloat16)

    @pl.when(step == 0)
    def _():
        own_total[...] = own_part
        far_total[...] = far_part

    @pl.when(step > 0)
    def _():
        own_total[...] += own_part
        far_total[...] += far_part

    @pl.when(step == pl.num_programs(0) - 1)
    def _():
        own_grad[...] = own_total[...]
        far_grad[...] = far_total[...].astype(jnp.bfloat16)


def relay_kernel(branches, devices, info, prompts, grad_ref, got_ref, notes_ref, *outs):
    to_low, to_high, to_me = outs
    me = info[0]
    down, up = lax.rem(me + devices - 2, devices), lax.rem(me + 2, devices)
    low = high = kept = jnp.zeros(grad_ref.shape[1:], jnp.float32)
    notes = notes_ref[...].astype(jnp.float32)
    start = notes.shape[0] - NOTES
    for number in range(branches - 1):
        grad = grad_ref[number].astype(jnp.float32)
        prompt = prompts[other_branch(number, prompts, me, branches)]
        low = low + jnp.where(prompt == down, grad, 0.0)
        high = high + jnp.where(prompt == up, grad, 0.0)
        grad = got_ref[number].astype(jnp.float32)
        prompt = notes[start + number : start + number + 1, :]
        low = low + jnp.where(prompt == down.astype(jnp.float32), grad, 0.0)
        high = high + jnp.where(prompt == up.astype(jnp.float32), grad, 0.0)
        kept = kept + jnp.where(prompt == me.astype(jnp.float32), grad, 0.0)
    to_low[...] = low.astype(jnp.bfloat16)
    to_high[...] = high.astype(jnp.bfloat16)
    to_me[...] = kept


def relay(devices, me, prompts, grad, got, notes):
    branches = prompts.shape[0]
    here = pl.BlockSpec(memory_space=pltpu.VMEM)
    shape = grad.shape[1:]
    return pl.pallas_call(
        functools.partial(relay_kernel, branches, devices),
        grid_spec=pltpu.PrefetchScalarGridSpec(
            num_scalar_prefetch=2, grid=(1,), in_specs=[here] * 3, out_specs=[here] * 3
        ),
        out_shape=[
            jax.ShapeDtypeStruct(shape, jnp.bfloat16),
            jax.ShapeDtypeStruct(shape, jnp.bfloat16),
            jax.ShapeDtypeStruct(shape, jnp.float32),
        ],
        compiler_params=pltpu.CompilerParams(vmem_limit_bytes=VMEM),
        name="relay",
    )(me, prompts, grad, got, notes)


def attention(own, heads, devices, me, prompts, pieces, query, pairs, upstream, out):
    branches = prompts.shape[0]
    answers = query.shape[0] // branches
    prefix_len = pieces[0].shape[0] - NOTES
    width = len(heads) * HD
    steps = 1 if own else branches - 1

    def out_at(step, info, prompts):
        if own:
            return first_own(prompts, info[0], branches), heads[0] // len(heads)
        return other_branch(step, prompts, info[0], branches), 0

    here = pl.BlockSpec(memory_space=pltpu.VMEM)
    there = pl.BlockSpec(memory_space=pl.ANY)
    piece = (prefix_len, 2 * HD)
    operands = [*pieces, query, pairs, upstream]
    in_specs = [here] * len(operands)
    out_shape = [
        jax.ShapeDtypeStruct(query.shape, query.dtype),
        jax.ShapeDtypeStruct(piece, jnp.float32),
    ]
    out_specs = [pl.BlockSpec((answers, width), out_at), here]
    aliases = {}
    if out is not None:
        aliases = {2 + len(operands): 0}
        operands.append(out)
        in_specs.append(there)
    tall_rows = min(TALL, len(heads)) * ROWS
    all_rows = len(heads) * answers
    scratch = [
        pltpu.VMEM((2 * answers, HD), jnp.float32),
        pltpu.VMEM((prefix_len + answers, HD), jnp.bfloat16),
        pltpu.VMEM((prefix_len + answers, HD), jnp.bfloat16),
        pltpu.VMEM((2, tall_rows, prefix_len + answers), jnp.float32),
        pltpu.VMEM((2, tall_rows, prefix_len + answers), jnp.bfloat16),
        pltpu.VMEM((2, tall_rows, prefix_len), jnp.float32),
        pltpu.VMEM((all_rows, prefix_len), jnp.bfloat16),
        pltpu.VMEM((all_rows, prefix_len), jnp.bfloat16),
    ]
    if own:
        body = functools.partial(own_kernel, heads, answers, branches, out is not None)
    else:
        body = functools.partial(other_kernel, heads, answers, branches, devices)
        scratch += [pltpu.VMEM(piece, jnp.float32)] * 2
        for shape in (piece, (steps, *piece)):
            out_shape.append(jax.ShapeDtypeStruct(shape, jnp.bfloat16))
            out_specs.append(here)
    seen = prefix_len + (answers + BLOCK) // 2
    work = steps * answers * width
    return pl.pallas_call(
        body,
        grid_spec=pltpu.PrefetchScalarGridSpec(
            num_scalar_prefetch=2,
            grid=(steps,),
            in_specs=in_specs,
            out_specs=out_specs,
            scratch_shapes=scratch,
        ),
        out_shape=out_shape,
        input_output_aliases=aliases,
        compiler_params=pltpu.CompilerParams(
            dimension_semantics=("arbitrary",), vmem_limit_bytes=VMEM
        ),
        cost_estimate=pl.CostEstimate(
            flops=work * (4 * seen + 6 * prefix_len),
            bytes_accessed=6 * work,
            transcendentals=work // HD * seen,
        ),
        name="own_branch" if own else "other_branches",
    )(me, prompts, *operands)


def shards(prefix, kv_weight, ans_query, ans_kv, d_out, branch_prompt):
    columns = kv_weight.shape[2]
    if columns != HD:
        raise ValueError("one kv head")
    devices = lax.axis_size("dp")
    if devices % 2 or devices < 2 * REACH + 1:
        raise ValueError("dp size")
    if branch_prompt.shape[0] > NOTES or devices > 256:
        raise ValueError("notes size")
    me = lax.axis_index("dp").astype(jnp.int32).reshape(1)
    own_kv = project(me, branch_prompt, prefix[0], kv_weight)
    far = dp_permute(own_kv, far_of)
    partner = dp_permute(own_kv, lambda i: i ^ 1)
    pair = jnp.stack([own_kv, partner])
    low = dp_permute(pair, lambda i: i + 2)
    high = dp_permute(pair, lambda i: i - 2)
    branch = functools.partial(
        attention,
        devices=devices,
        me=me,
        prompts=branch_prompt,
        query=ans_query,
        pairs=ans_kv.reshape(2 * ans_kv.shape[0], HD),
        upstream=d_out,
    )
    heads = tuple(range(ans_query.shape[1] // HD))
    early, late = heads[: len(heads) // 2], heads[len(heads) // 2 :]
    out, early_grad = branch(own=True, heads=early, pieces=[own_kv], out=None)
    out, more_grad, to_far, grad = branch(
        own=False, heads=heads, pieces=[own_kv, partner, low, high, far], out=out
    )
    from_far = dp_permute(to_far, far_of)
    got = dp_permute(grad, lambda i: i ^ 1)
    out, late_grad = branch(own=True, heads=late, pieces=[own_kv], out=out)
    to_low, to_high, to_me = relay(devices, me, branch_prompt, grad, got, partner)
    from_high = dp_permute(to_low, lambda i: i - 2)
    from_low = dp_permute(to_high, lambda i: i + 2)
    grads = [early_grad, late_grad, more_grad, to_me, from_far, from_high, from_low]
    rows = project_back(grads, kv_weight)
    return (out, rows.reshape(1, *rows.shape))


def project_back(grads, kv_weight):
    count = lax.axis_size("tensor")
    if count != 4:
        raise ValueError("tensor size")
    index = lax.axis_index("tensor").astype(jnp.int32).reshape(1)
    far_give, far_keep, near_give, near_keep = back_shares(index, grads, kv_weight, count)

    def swap(x, bit):
        return lax.ppermute(x, "tensor", [(i, i ^ bit) for i in range(count)])

    def both(a, b):
        return a.astype(jnp.float32) + b.astype(jnp.float32)

    far_sum = both(far_keep, swap(far_give, 1)).astype(jnp.bfloat16)
    arrived = swap(far_sum, 2)
    got = swap(near_give, 1)
    mine = lax.optimization_barrier(both(near_keep, got).astype(jnp.bfloat16))
    return both(mine, arrived).astype(jnp.bfloat16)


def solution(mesh):
    return jax.shard_map(
        shards,
        mesh=mesh,
        in_specs=(
            P("dp", None, None),
            P(None, None, "tensor"),
            P("dp", "tensor"),
            P("dp", None, "tensor"),
            P("dp", "tensor"),
            P("dp"),
        ),
        out_specs=(P("dp", "tensor"), P("dp", "tensor", None)),
        check_vma=False,
    )
```

time: 154 us -> 65.2 us (0.42)
  matrix products: 32 us -> 0 us
  local copies, waits for them, and re-layouts: 29.9 us -> 4.08 us
  Pallas kernels: 0 us -> 20.9 us
  other arithmetic: 21.2 us -> 2.06 us
  between operations: 14.3 us -> 0.73 us
  waiting for transfers between devices: 34.7 us -> 21.3 us
  starting transfers between devices: 20.9 us -> 15.9 us
    dot_general x13 -> x0, matrix products: 32 us -> none  [the longest x2 8.35 us: branch_pass(): jnp.einsum('hgak,khd->ahgd', prob_half, value_rows, preferred_element_typ...]
    reduce_scatter x1 -> x0, waiting for transfers between devices: 25 us -> none  [shards(): lax.psum_scatter(lax.dot_general(kv_grad, flat_weight, (((1,), (1,)), (()...]
    pallas_call x0 -> x6, Pallas kernels: none -> 20.9 us  [the longest x3 12.2 us: attention(): pl.pallas_call(body, grid_spec=pltpu.PrefetchScalarGridSpec(num_scalar_pr...]
    convert_element_type x2, other arithmetic: 13.2 us -> 0.24 us  [the longest x1 0.12 us: project_back(): far_sum = both(far_keep, swap(far_give, 1)).astype(jnp.bfloat16)]
    ppermute x12 -> x11, waiting for transfers between devices: 9.63 us -> 21.3 us  [the longest x3 13.7 us: swap(): return lax.ppermute(x, 'tensor', [(i, i ^ bit) for i in range(count)])]
    unnamed x17 -> x16, local copies, waits for them, and re-layouts: 10.6 us -> 4.08 us
    while x2 -> x0, local copies, waits for them, and re-layouts: 5.85 us -> none
    dynamic_slice x6 -> x0, local copies, waits for them, and re-layouts: 5.71 us -> none  [shards(): lax.map(one_branch, (queries, answer_kv, upstream, chosen))]
  transfers between devices with their start and end apart: 13 -> 11, of which waited for: 4 -> 6; matrix products, arithmetic and copies ran while one was open for 6% -> 0% of each run, Pallas kernels for 0% -> 11%
where the time goes in v2:
time: 65.2 us; the launch traced here: 64.9 us
  waiting for transfers between devices  21.3 us (33%)
  Pallas kernels  20.9 us (32%)
  starting transfers between devices  15.9 us (24%)
  local copies, waits for them, and re-layouts  4.08 us (6%)
  other arithmetic  2.06 us (3%)
  between operations  0.73 us (1%)
    ppermute x3, waiting for transfers between devices, swap(): return lax.ppermute(x, 'tensor', [(i, i ^ bit) for i in range(count)])  13.7 us
    ppermute x8, starting transfers between devices, dp_permute(): lax.ppermute(x, 'dp', [(i, target(i) % devices) for i in range(devices)])  13.7 us
    pallas_call x3, Pallas kernels, attention(): pl.pallas_call(body, grid_spec=pltpu.PrefetchScalarGridSpec(num_scalar_pr...  12.2 us
    ppermute x8, waiting for transfers between devices, dp_permute(): lax.ppermute(x, 'dp', [(i, target(i) % devices) for i in range(devices)])  7.58 us
    pallas_call x1, Pallas kernels, project(): pl.pallas_call(project_kernel, in_specs=[pl.BlockSpec(memory_space=pltpu....  5.65 us
    unnamed x16, local copies, waits for them, and re-layouts  4.08 us
    pallas_call x1, Pallas kernels, back_shares(): pl.pallas_call(back_kernel, in_specs=[pl.BlockSpec(memory_space=pltpu.SME...  2.41 us
    ppermute x3, starting transfers between devices, swap(): return lax.ppermute(x, 'tensor', [(i, i ^ bit) for i in range(count)])  2.15 us
  transfers between devices with their start and end apart: 11, of which 6 were waited for; matrix products, arithmetic and copies ran while one was open for 0% of the time, Pallas kernels for 11%

profile of v2, /device:TPU:0, one launch (start us, length us, event | category | flops | bytes accessed | tf_op | source)
XLA Modules:
  0.0 64.9 jit_solution(6764547349956790386)
XLA Ops:
  0.7 5.6 %project.1.own_ref.refs_0_ = bf16[144,256]{1,0:T(8,128)(2,1)} custom-call(s32[1]{0:T(128)} %bitcast.info, s32[2]{0:T(128)} %prompts.9, bf16[128,8192]{1,0:T(8,128)(2,1)} %bitcast.16, bf16[16384,128]{1,0:T(8,128)(2,1)} %bitcast.9), custom_call_target="tpu_custom_call" | custom-call | flops 536870912 | bytes 6291456 | tf_op jit(solution)/shard_map/project/pallas_call | solution.py:115
  6.3 3.0 %collective-permute-start = (bf16[144,256]{1,0:T(8,128)(2,1)}, bf16[144,256]{1,0:T(8,128)(2,1)S(1)}, u32[]{:S(2)}, u32[]{:S(2)}) collective-permute-start(bf16[144,256]{1,0:T(8,128)(2,1)} %project.1.own_ref.refs_0_), channel_id=1, source_target_pairs={{0,4},{4,0},{8,12},{12,8},{16,20},{20,16},{24,28},{28,24},{1,5},{5... | collective-permute-start | bytes 221192 | tf_op jit(solution)/shard_map/ppermute | solution.py:25
  9.4 2.5 %collective-permute-done.refs_1_.notes_ref = bf16[144,256]{1,0:T(8,128)(2,1)S(1)} collective-permute-done((bf16[144,256]{1,0:T(8,128)(2,1)}, bf16[144,256]{1,0:T(8,128)(2,1)S(1)}, u32[]{:S(2)}, u32[]{:S(2)}) %collective-permute-start) | collective-permute-done | bytes 73760 | tf_op jit(solution)/shard_map/ppermute | solution.py:25
  11.9 0.9 %pad_maximum_fusion = bf16[2,144,256]{2,1,0:T(8,128)(2,1)S(1)} fusion(bf16[1,144,256]{2,1,0:T(8,128)(2,1)S(1)} %bitcast.15, bf16[1,144,256]{2,1,0:T(8,128)(2,1)} %bitcast.14), kind=kLoop, calls=%fused_computation.4 | loop fusion | flops 73728 | bytes 294912 | tf_op jit(solution)/shard_map/stack | solution.py:465
  12.8 4.2 %collective-permute-start.2 = (bf16[2,144,256]{2,1,0:T(8,128)(2,1)S(1)}, bf16[2,144,256]{2,1,0:T(8,128)(2,1)S(1)}, u32[]{:S(2)}, u32[]{:S(2)}) collective-permute-start(bf16[2,144,256]{2,1,0:T(8,128)(2,1)S(1)} %pad_maximum_fusion), channel_id=1, source_target_pairs={{0,24},{4,28},{8,0},{12,4},{16,8},{20,12},{24,16},{28,20},{1,25},{... | collective-permute-start | bytes 442376 | tf_op jit(solution)/shard_map/ppermute | solution.py:25
  17.0 1.9 %collective-permute-start.3 = (bf16[144,256]{1,0:T(8,128)(2,1)}, bf16[144,256]{1,0:T(8,128)(2,1)S(1)}, u32[]{:S(2)}, u32[]{:S(2)}) collective-permute-start(bf16[144,256]{1,0:T(8,128)(2,1)} %project.1.own_ref.refs_0_), channel_id=1, source_target_pairs={{0,20},{4,16},{8,28},{12,24},{16,4},{20,0},{24,12},{28,8},{1,21},{... | collective-permute-start | bytes 221192 | tf_op jit(solution)/shard_map/ppermute | solution.py:25
  18.9 1.6 %copy-done.1 = bf16[1024,1024]{1,0:T(8,128)(2,1)S(1)} copy-done((bf16[1024,1024]{1,0:T(8,128)(2,1)S(1)}, bf16[1024,1024]{1,0:T(8,128)(2,1)}, u32[]{:S(2)}) %copy-start.1) | copy-done | bytes 2097176
  20.5 0.9 %copy-done.5 = bf16[144,256]{1,0:T(8,128)(2,1)S(1)} copy-done((bf16[144,256]{1,0:T(8,128)(2,1)S(1)}, bf16[144,256]{1,0:T(8,128)(2,1)}, u32[]{:S(2)}) %copy-start.5) | copy-done | bytes 73752
  21.4 3.3 %own_branch.2 = (bf16[1024,1024]{1,0:T(8,128)(2,1)}, f32[128,256]{1,0:T(8,128)S(1)}) custom-call(s32[1]{0:T(128)} %bitcast.info, s32[2]{0:T(128)S(1)} %copy-done.7, bf16[144,256]{1,0:T(8,128)(2,1)S(1)} %copy-done.5, bf16[1024,1024]{1,0:T(8,128)(2,1)S(1)} %copy-done, bf16[2048,128]{1,0:T(8,128)(2,1)S(1)} %bitcast.11, bf16[1024,1024]{1,0:T(8,128)(2,1)S(1)} %copy-done.1), custom_call_target="tpu_custom_call" | custom-call | flops 671088640 | bytes 1572864 | tf_op jit(solution)/shard_map/own_branch/pallas_call | solution.py:429
  24.7 2.3 %collective-permute-done.3.refs_4_ = bf16[144,256]{1,0:T(8,128)(2,1)S(1)} collective-permute-done((bf16[144,256]{1,0:T(8,128)(2,1)}, bf16[144,256]{1,0:T(8,128)(2,1)S(1)}, u32[]{:S(2)}, u32[]{:S(2)}) %collective-permute-start.3) | collective-permute-done | bytes 73760 | tf_op jit(solution)/shard_map/ppermute | solution.py:25
  27.0 5.7 %other_branches.1 = (bf16[1024,1024]{1,0:T(8,128)(2,1)}, f32[128,256]{1,0:T(8,128)S(1)}, bf16[128,256]{1,0:T(8,128)(2,1)S(1)}, bf16[1,128,256]{2,1,0:T(8,128)(2,1)S(1)}) custom-call(s32[1]{0:T(128)} %bitcast.info, s32[2]{0:T(128)S(1)} %copy-done.7, bf16[144,256]{1,0:T(8,128)(2,1)S(1)} %copy-done.6, ...), custom_call_target="tpu_custom_call", output_to_operand_aliasing={{0}: (10, {})} | custom-call | flops 1342177280 | bytes 3145728 | tf_op jit(solution)/shard_map/other_branches/pallas_call | solution.py:429
  32.7 0.7 %collective-permute-start.4 = (bf16[1,128,256]{2,1,0:T(8,128)(2,1)S(1)}, bf16[1,128,256]{2,1,0:T(8,128)(2,1)S(1)}, u32[]{:S(2)}, u32[]{:S(2)}) collective-permute-start(bf16[1,128,256]{2,1,0:T(8,128)(2,1)S(1)} %get-tuple-element.23.grad_ref), channel_id=1, source_target_pairs={{0,4},{4,0},{8,12},{12,8},{16,20},{20,16},{24,28},{28,24},{1,5},{5... | collective-permute-start | bytes 196616 | tf_op jit(solution)/shard_map/ppermute | solution.py:25
  33.4 1.8 %collective-permute-start.5 = (bf16[128,256]{1,0:T(8,128)(2,1)S(1)}, bf16[128,256]{1,0:T(8,128)(2,1)S(1)}, u32[]{:S(2)}, u32[]{:S(2)}) collective-permute-start(bf16[128,256]{1,0:T(8,128)(2,1)S(1)} %get-tuple-element.25), channel_id=1, source_target_pairs={{0,20},{4,16},{8,28},{12,24},{16,4},{20,0},{24,12},{28,8},{1,21},{... | collective-permute-start | bytes 196616 | tf_op jit(solution)/shard_map/ppermute | solution.py:25
  35.2 2.5 %collective-permute-done.4.got_ref = bf16[1,128,256]{2,1,0:T(8,128)(2,1)S(1)} collective-permute-done((bf16[1,128,256]{2,1,0:T(8,128)(2,1)S(1)}, bf16[1,128,256]{2,1,0:T(8,128)(2,1)S(1)}, u32[]{:S(2)}, u32[]{:S(2)}) %collective-permute-start.4) | collective-permute-done | bytes 65568 | tf_op jit(solution)/shard_map/ppermute | solution.py:25
  37.7 0.6 relay.1
  38.3 1.1 %collective-permute-start.6 = (bf16[128,256]{1,0:T(8,128)(2,1)S(1)}, bf16[128,256]{1,0:T(8,128)(2,1)S(1)}, u32[]{:S(2)}, u32[]{:S(2)}) collective-permute-start(bf16[128,256]{1,0:T(8,128)(2,1)S(1)} %get-tuple-element.26), channel_id=1, source_target_pairs={{0,24},{4,28},{8,0},{12,4},{16,8},{20,12},{24,16},{28,20},{1,25},{... | collective-permute-start | bytes 196616 | tf_op jit(solution)/shard_map/ppermute | solution.py:25
  39.4 0.9 %collective-permute-start.7 = (bf16[128,256]{1,0:T(8,128)(2,1)S(1)}, bf16[128,256]{1,0:T(8,128)(2,1)S(1)}, u32[]{:S(2)}, u32[]{:S(2)}) collective-permute-start(bf16[128,256]{1,0:T(8,128)(2,1)S(1)} %get-tuple-element.27), channel_id=1, source_target_pairs={{0,8},{4,12},{8,16},{12,20},{16,24},{20,28},{24,0},{28,4},{1,9},{5... | collective-permute-start | bytes 196616 | tf_op jit(solution)/shard_map/ppermute | solution.py:25
  40.3 1.6 %copy-done.2 = bf16[1024,1024]{1,0:T(8,128)(2,1)S(1)} copy-done((bf16[1024,1024]{1,0:T(8,128)(2,1)S(1)}, bf16[1024,1024]{1,0:T(8,128)(2,1)}, u32[]{:S(2)}) %copy-start.2) | copy-done | bytes 2097176
  41.9 3.3 %own_branch.3 = (bf16[1024,1024]{1,0:T(8,128)(2,1)}, f32[128,256]{1,0:T(8,128)S(1)}) custom-call(s32[1]{0:T(128)} %bitcast.info, s32[2]{0:T(128)S(1)} %copy-done.7, bf16[144,256]{1,0:T(8,128)(2,1)S(1)} %copy-done.6, bf16[1024,1024]{1,0:T(8,128)(2,1)S(1)} %copy-done, bf16[2048,128]{1,0:T(8,128)(2,1)S(1)} %bitcast.13, ...), custom_call_target="tpu_custom_call", output_to_operand_aliasing={{0}: (6, {})} | custom-call | flops 671088640 | bytes 1572864 | tf_op jit(solution)/shard_map/own_branch/pallas_call | solution.py:429
  45.5 2.4 %back_shares.1 = (bf16[32,8192]{1,0:T(8,128)(2,1)S(1)}, bf16[32,8192]{1,0:T(8,128)(2,1)S(1)}, bf16[32,8192]{1,0:T(8,128)(2,1)S(1)}, bf16[32,8192]{1,0:T(8,128)(2,1)S(1)}) custom-call(s32[1]{0:T(128)} %bitcast.6.index, f32[128,256]{1,0:T(8,128)S(1)} %get-tuple-element.20.refs_0_, f32[128,256]{1,0:T(8,128)S(1)} %get-tuple-element.21.refs_1_, ...), custom_call_target="tpu_custom_call" | custom-call | flops 536870912 | bytes 6291456 | tf_op jit(solution)/shard_map/back_shares/pallas_call | solution.py:169
  48.5 1.4 %collective-permute-done.9 = bf16[32,8192]{1,0:T(8,128)(2,1)S(1)} collective-permute-done((bf16[32,8192]{1,0:T(8,128)(2,1)S(1)}, bf16[32,8192]{1,0:T(8,128)(2,1)S(1)}, u32[]{:S(2)}, u32[]{:S(2)}) %collective-permute-start.9) | collective-permute-done | bytes 524320 | tf_op jit(solution)/shard_map/ppermute | solution.py:502
  50.0 1.6 %collective-permute-start.10 = (bf16[32,8192]{1,0:T(8,128)(2,1)S(1)}, bf16[32,8192]{1,0:T(8,128)(2,1)S(1)}, u32[]{:S(2)}, u32[]{:S(2)}) collective-permute-start(bf16[32,8192]{1,0:T(8,128)(2,1)S(1)} %add_convert_fusion.1), channel_id=1, source_target_pairs={{0,2},{1,3},{2,0},{3,1},{4,6},{5,7},{6,4},{7,5},{8,10},{9,11},{10,... | collective-permute-start | bytes 1572872 | tf_op jit(solution)/shard_map/ppermute | solution.py:502
  51.7 12.3 %collective-permute-done.10 = bf16[32,8192]{1,0:T(8,128)(2,1)S(1)} collective-permute-done((bf16[32,8192]{1,0:T(8,128)(2,1)S(1)}, bf16[32,8192]{1,0:T(8,128)(2,1)S(1)}, u32[]{:S(2)}, u32[]{:S(2)}) %collective-permute-start.10) | collective-permute-done | bytes 524320 | tf_op jit(solution)/shard_map/ppermute | solution.py:502
  64.0 0.9 %fusion = bf16[1,32,8192]{2,1,0:T(8,128)(2,1)} fusion(bf16[32,8192]{1,0:T(8,128)(2,1)S(1)} %collective-permute-done.10, bf16[32,8192]{1,0:T(8,128)(2,1)S(1)} %add_convert_fusion.2), kind=kLoop, calls=%fused_computation.3 | loop fusion | flops 1048576 | bytes 1572864 | tf_op jit(solution)/shard_map/reshape | solution.py:491
  (24 shorter events, 1.1 us)
Async XLA Ops:
  0.6 18.3 %copy-start = (bf16[1024,1024]{1,0:T(8,128)(2,1)S(1)}, bf16[1024,1024]{1,0:T(8,128)(2,1)}, u32[]{:S(2)}) copy-start(bf16[1024,1024]{1,0:T(8,128)(2,1)} %q_ref.3) | copy-start | bytes 6291460
  0.6 18.3 %copy-start.4 = (bf16[1024,2,128]{2,1,0:T(2,128)(2,1)S(1)}, bf16[1024,2,128]{2,1,0:T(2,128)(2,1)}, u32[]{:S(2)}) copy-start(bf16[1024,2,128]{2,1,0:T(2,128)(2,1)} %param.9) | copy-start | bytes 1572868
  0.7 18.3 %copy-start.7 = (s32[2]{0:T(128)S(1)}, s32[2]{0:T(128)}, u32[]{:S(2)}) copy-start(s32[2]{0:T(128)} %prompts.9) | copy-start | bytes 28
  6.3 5.6 %collective-permute-start = (bf16[144,256]{1,0:T(8,128)(2,1)}, bf16[144,256]{1,0:T(8,128)(2,1)S(1)}, u32[]{:S(2)}, u32[]{:S(2)}) collective-permute-start(bf16[144,256]{1,0:T(8,128)(2,1)} %project.1.own_ref.refs_0_), channel_id=1, source_target_pairs={{0,4},{4,0},{8,12},{12,8},{16,20},{20,16},{24,28},{28,24},{1,5},{5... | collective-permute-start | bytes 221192 | tf_op jit(solution)/shard_map/ppermute | solution.py:25
  12.8 14.2 %collective-permute-start.2 = (bf16[2,144,256]{2,1,0:T(8,128)(2,1)S(1)}, bf16[2,144,256]{2,1,0:T(8,128)(2,1)S(1)}, u32[]{:S(2)}, u32[]{:S(2)}) collective-permute-start(bf16[2,144,256]{2,1,0:T(8,128)(2,1)S(1)} %pad_maximum_fusion), channel_id=1, source_target_pairs={{0,24},{4,28},{8,0},{12,4},{16,8},{20,12},{24,16},{28,20},{1,25},{... | collective-permute-start | bytes 442376 | tf_op jit(solution)/shard_map/ppermute | solution.py:25
  17.0 10.0 %collective-permute-start.1 = (bf16[2,144,256]{2,1,0:T(8,128)(2,1)S(1)}, bf16[2,144,256]{2,1,0:T(8,128)(2,1)S(1)}, u32[]{:S(2)}, u32[]{:S(2)}) collective-permute-start(bf16[2,144,256]{2,1,0:T(8,128)(2,1)S(1)} %pad_maximum_fusion), channel_id=1, source_target_pairs={{0,8},{4,12},{8,16},{12,20},{16,24},{20,28},{24,0},{28,4},{1,9},{5... | collective-permute-start | bytes 442376 | tf_op jit(solution)/shard_map/ppermute | solution.py:25
  17.0 10.0 %collective-permute-start.3 = (bf16[144,256]{1,0:T(8,128)(2,1)}, bf16[144,256]{1,0:T(8,128)(2,1)S(1)}, u32[]{:S(2)}, u32[]{:S(2)}) collective-permute-start(bf16[144,256]{1,0:T(8,128)(2,1)} %project.1.own_ref.refs_0_), channel_id=1, source_target_pairs={{0,20},{4,16},{8,28},{12,24},{16,4},{20,0},{24,12},{28,8},{1,21},{... | collective-permute-start | bytes 221192 | tf_op jit(solution)/shard_map/ppermute | solution.py:25
  18.9 1.6 %copy-start.1 = (bf16[1024,1024]{1,0:T(8,128)(2,1)S(1)}, bf16[1024,1024]{1,0:T(8,128)(2,1)}, u32[]{:S(2)}) copy-start(bf16[1024,1024]{1,0:T(8,128)(2,1)} %up_ref.3) | copy-start | bytes 6291460
  20.5 0.9 %copy-start.5 = (bf16[144,256]{1,0:T(8,128)(2,1)S(1)}, bf16[144,256]{1,0:T(8,128)(2,1)}, u32[]{:S(2)}) copy-start(bf16[144,256]{1,0:T(8,128)(2,1)} %project.1.own_ref.refs_0_) | copy-start | bytes 221188
  21.4 5.6 %copy-start.6 = (bf16[144,256]{1,0:T(8,128)(2,1)S(1)}, bf16[144,256]{1,0:T(8,128)(2,1)}, u32[]{:S(2)}) copy-start(bf16[144,256]{1,0:T(8,128)(2,1)} %project.1.own_ref.refs_0_) | copy-start | bytes 221188
  32.7 5.0 %collective-permute-start.4 = (bf16[1,128,256]{2,1,0:T(8,128)(2,1)S(1)}, bf16[1,128,256]{2,1,0:T(8,128)(2,1)S(1)}, u32[]{:S(2)}, u32[]{:S(2)}) collective-permute-start(bf16[1,128,256]{2,1,0:T(8,128)(2,1)S(1)} %get-tuple-element.23.grad_ref), channel_id=1, source_target_pairs={{0,4},{4,0},{8,12},{12,8},{16,20},{20,16},{24,28},{28,24},{1,5},{5... | collective-permute-start | bytes 196616 | tf_op jit(solution)/shard_map/ppermute | solution.py:25
  33.4 11.9 %collective-permute-start.5 = (bf16[128,256]{1,0:T(8,128)(2,1)S(1)}, bf16[128,256]{1,0:T(8,128)(2,1)S(1)}, u32[]{:S(2)}, u32[]{:S(2)}) collective-permute-start(bf16[128,256]{1,0:T(8,128)(2,1)S(1)} %get-tuple-element.25), channel_id=1, source_target_pairs={{0,20},{4,16},{8,28},{12,24},{16,4},{20,0},{24,12},{28,8},{1,21},{... | collective-permute-start | bytes 196616 | tf_op jit(solution)/shard_map/ppermute | solution.py:25
  38.3 7.0 %collective-permute-start.6 = (bf16[128,256]{1,0:T(8,128)(2,1)S(1)}, bf16[128,256]{1,0:T(8,128)(2,1)S(1)}, u32[]{:S(2)}, u32[]{:S(2)}) collective-permute-start(bf16[128,256]{1,0:T(8,128)(2,1)S(1)} %get-tuple-element.26), channel_id=1, source_target_pairs={{0,24},{4,28},{8,0},{12,4},{16,8},{20,12},{24,16},{28,20},{1,25},{... | collective-permute-start | bytes 196616 | tf_op jit(solution)/shard_map/ppermute | solution.py:25
  39.4 6.1 %collective-permute-start.7 = (bf16[128,256]{1,0:T(8,128)(2,1)S(1)}, bf16[128,256]{1,0:T(8,128)(2,1)S(1)}, u32[]{:S(2)}, u32[]{:S(2)}) collective-permute-start(bf16[128,256]{1,0:T(8,128)(2,1)S(1)} %get-tuple-element.27), channel_id=1, source_target_pairs={{0,8},{4,12},{8,16},{12,20},{16,24},{20,28},{24,0},{28,4},{1,9},{5... | collective-permute-start | bytes 196616 | tf_op jit(solution)/shard_map/ppermute | solution.py:25
  40.3 1.6 %copy-start.2 = (bf16[1024,1024]{1,0:T(8,128)(2,1)S(1)}, bf16[1024,1024]{1,0:T(8,128)(2,1)}, u32[]{:S(2)}) copy-start(bf16[1024,1024]{1,0:T(8,128)(2,1)} %up_ref.3) | copy-start | bytes 6291460
  41.9 3.5 %copy-start.3 = (bf16[8192,2,128]{2,1,0:T(2,128)(2,1)S(1)}, bf16[8192,2,128]{2,1,0:T(2,128)(2,1)}, u32[]{:S(2)}) copy-start(bf16[8192,2,128]{2,1,0:T(2,128)(2,1)} %param.7) | copy-start | bytes 12582916
  47.9 2.0 %collective-permute-start.9 = (bf16[32,8192]{1,0:T(8,128)(2,1)S(1)}, bf16[32,8192]{1,0:T(8,128)(2,1)S(1)}, u32[]{:S(2)}, u32[]{:S(2)}) collective-permute-start(bf16[32,8192]{1,0:T(8,128)(2,1)S(1)} %get-tuple-element.31), channel_id=1, source_target_pairs={{0,1},{1,0},{2,3},{3,2},{4,5},{5,4},{6,7},{7,6},{8,9},{9,8},{10,11... | collective-permute-start | bytes 1572872 | tf_op jit(solution)/shard_map/ppermute | solution.py:502
  48.0 3.6 %collective-permute-start.8 = (bf16[32,8192]{1,0:T(8,128)(2,1)S(1)}, bf16[32,8192]{1,0:T(8,128)(2,1)S(1)}, u32[]{:S(2)}, u32[]{:S(2)}) collective-permute-start(bf16[32,8192]{1,0:T(8,128)(2,1)S(1)} %get-tuple-element.29), channel_id=1, source_target_pairs={{0,1},{1,0},{2,3},{3,2},{4,5},{5,4},{6,7},{7,6},{8,9},{9,8},{10,11... | collective-permute-start | bytes 1572872 | tf_op jit(solution)/shard_map/ppermute | solution.py:502
  50.0 14.0 %collective-permute-start.10 = (bf16[32,8192]{1,0:T(8,128)(2,1)S(1)}, bf16[32,8192]{1,0:T(8,128)(2,1)S(1)}, u32[]{:S(2)}, u32[]{:S(2)}) collective-permute-start(bf16[32,8192]{1,0:T(8,128)(2,1)S(1)} %add_convert_fusion.1), channel_id=1, source_target_pairs={{0,2},{1,3},{2,0},{3,1},{4,6},{5,7},{6,4},{7,5},{8,10},{9,11},{10,... | collective-permute-start | bytes 1572872 | tf_op jit(solution)/shard_map/ppermute | solution.py:502

commit v3 on v2

--- a/solution.py
+++ b/solution.py
@@ -14,8 +14,9 @@
 ROWS = 128
 TALL = 4
 TILE = 32
-CHUNKS = 4
+CHUNKS = 8
 VMEM = 24 << 20
+PROJECT_VMEM = 60500000
 NOTES = 16
 OWN, PARTNER, LOW, LOW_PAIR, HIGH, HIGH_PAIR, FAR = range(7)
 
@@ -74,7 +75,9 @@
     split[chunk % 2, :, HD:] = values
 
 
-def project_kernel(info, prompts, prefix_ref, weight_ref, out_ref, rows, pairs, wide, split, sems):
+def project_kernel(
+    info, prompts, prefix_ref, weight_ref, out_ref, rows, pairs, wide, split, sems
+):
     depth = rows.shape[1] // CHUNKS
     copies = []
     for chunk in range(CHUNKS):
@@ -114,7 +117,7 @@
     there = pl.BlockSpec(memory_space=pl.ANY)
     return pl.pallas_call(
         project_kernel,
-        in_specs=[pl.BlockSpec(memory_space=pltpu.SMEM)] * 2 + [there, there],
+        in_specs=[pl.BlockSpec(memory_space=pltpu.SMEM)] * 2 + [there] * 2,
         out_specs=pl.BlockSpec(memory_space=pltpu.VMEM),
         out_shape=jax.ShapeDtypeStruct((prefix_len + NOTES, 2 * HD), jnp.bfloat16),
         scratch_shapes=[
@@ -124,6 +127,7 @@
             pltpu.VMEM((2, model_width // CHUNKS, 2 * HD), jnp.bfloat16),
             pltpu.SemaphoreType.DMA((2, CHUNKS)),
         ],
+        compiler_params=pltpu.CompilerParams(vmem_limit_bytes=PROJECT_VMEM),
         cost_estimate=pl.CostEstimate(
             flops=4 * prefix_len * model_width * HD,
             bytes_accessed=2 * model_width * (prefix_len + 2 * HD),
@@ -459,9 +463,10 @@
     if branch_prompt.shape[0] > NOTES or devices > 256:
         raise ValueError("notes size")
     me = lax.axis_index("dp").astype(jnp.int32).reshape(1)
+    answer_pairs = ans_kv.reshape(2 * ans_kv.shape[0], HD)
     own_kv = project(me, branch_prompt, prefix[0], kv_weight)
+    partner = dp_permute(own_kv, lambda i: i ^ 1)
     far = dp_permute(own_kv, far_of)
-    partner = dp_permute(own_kv, lambda i: i ^ 1)
     pair = jnp.stack([own_kv, partner])
     low = dp_permute(pair, lambda i: i + 2)
     high = dp_permute(pair, lambda i: i - 2)
@@ -471,7 +476,7 @@
         me=me,
         prompts=branch_prompt,
         query=ans_query,
-        pairs=ans_kv.reshape(2 * ans_kv.shape[0], HD),
+        pairs=answer_pairs,
         upstream=d_out,
     )
     heads = tuple(range(ans_query.shape[1] // HD))

time: 65.2 us -> 65.5 us (level)
  local copies, waits for them, and re-layouts: 4.08 us -> 2.51 us
  waiting for transfers between devices: 21.3 us -> 22.8 us
    unnamed x16, local copies, waits for them, and re-layouts: 4.08 us -> 2.51 us
    ppermute x8, waiting for transfers between devices: 7.58 us -> 9.11 us  [dp_permute(): lax.ppermute(x, 'dp', [(i, target(i) % devices) for i in range(devices)])]
where the time goes in v3:
time: 65.5 us; the launch traced here: 65.3 us
  waiting for transfers between devices  22.8 us (35%)
  Pallas kernels  21.3 us (33%)
  starting transfers between devices  15.9 us (24%)
  local copies, waits for them, and re-layouts  2.51 us (4%)
  other arithmetic  2.06 us (3%)
  between operations  0.74 us (1%)
    ppermute x8, starting transfers between devices, dp_permute(): lax.ppermute(x, 'dp', [(i, target(i) % devices) for i in range(devices)])  13.7 us
    ppermute x3, waiting for transfers between devices, swap(): return lax.ppermute(x, 'tensor', [(i, i ^ bit) for i in range(count)])  13.7 us
    pallas_call x3, Pallas kernels, attention(): pl.pallas_call(body, grid_spec=pltpu.PrefetchScalarGridSpec(num_scalar_pr...  12.4 us
    ppermute x8, waiting for transfers between devices, dp_permute(): lax.ppermute(x, 'dp', [(i, target(i) % devices) for i in range(devices)])  9.11 us
    pallas_call x1, Pallas kernels, project(): pl.pallas_call(project_kernel, in_specs=[pl.BlockSpec(memory_space=pltpu....  5.9 us
    unnamed x16, local copies, waits for them, and re-layouts  2.51 us
    pallas_call x1, Pallas kernels, back_shares(): pl.pallas_call(back_kernel, in_specs=[pl.BlockSpec(memory_space=pltpu.SME...  2.38 us
    ppermute x3, starting transfers between devices, swap(): return lax.ppermute(x, 'tensor', [(i, i ^ bit) for i in range(count)])  2.15 us
  transfers between devices with their start and end apart: 11, of which 6 were waited for; matrix products, arithmetic and copies ran while one was open for 0% of the time, Pallas kernels for 11%

profile of v3, /device:TPU:0, one launch (start us, length us, event | category | flops | bytes accessed | tf_op | source)
XLA Modules:
  0.0 65.3 jit_solution(10754106197802141002)
XLA Ops:
  0.7 5.9 %project.1.own_ref.refs_0_ = bf16[144,256]{1,0:T(8,128)(2,1)} custom-call(s32[1]{0:T(128)} %bitcast.info, s32[2]{0:T(128)} %prompts.9, bf16[128,8192]{1,0:T(8,128)(2,1)} %bitcast.16, bf16[16384,128]{1,0:T(8,128)(2,1)} %bitcast.9), custom_call_target="tpu_custom_call" | custom-call | flops 536870912 | bytes 6291456 | tf_op jit(solution)/shard_map/project/pallas_call | solution.py:118
  6.6 3.0 %collective-permute-start = (bf16[144,256]{1,0:T(8,128)(2,1)}, bf16[144,256]{1,0:T(8,128)(2,1)S(1)}, u32[]{:S(2)}, u32[]{:S(2)}) collective-permute-start(bf16[144,256]{1,0:T(8,128)(2,1)} %project.1.own_ref.refs_0_), channel_id=1, source_target_pairs={{0,4},{4,0},{8,12},{12,8},{16,20},{20,16},{24,28},{28,24},{1,5},{5... | collective-permute-start | bytes 221192 | tf_op jit(solution)/shard_map/ppermute | solution.py:26
  9.6 2.5 %collective-permute-done.refs_1_.notes_ref = bf16[144,256]{1,0:T(8,128)(2,1)S(1)} collective-permute-done((bf16[144,256]{1,0:T(8,128)(2,1)}, bf16[144,256]{1,0:T(8,128)(2,1)S(1)}, u32[]{:S(2)}, u32[]{:S(2)}) %collective-permute-start) | collective-permute-done | bytes 73760 | tf_op jit(solution)/shard_map/ppermute | solution.py:26
  12.2 0.9 %pad_maximum_fusion = bf16[2,144,256]{2,1,0:T(8,128)(2,1)S(1)} fusion(bf16[1,144,256]{2,1,0:T(8,128)(2,1)S(1)} %bitcast.15, bf16[1,144,256]{2,1,0:T(8,128)(2,1)} %bitcast.14), kind=kLoop, calls=%fused_computation.4 | loop fusion | flops 73728 | bytes 294912 | tf_op jit(solution)/shard_map/stack | solution.py:470
  13.1 4.2 %collective-permute-start.2 = (bf16[2,144,256]{2,1,0:T(8,128)(2,1)S(1)}, bf16[2,144,256]{2,1,0:T(8,128)(2,1)S(1)}, u32[]{:S(2)}, u32[]{:S(2)}) collective-permute-start(bf16[2,144,256]{2,1,0:T(8,128)(2,1)S(1)} %pad_maximum_fusion), channel_id=1, source_target_pairs={{0,24},{4,28},{8,0},{12,4},{16,8},{20,12},{24,16},{28,20},{1,25},{... | collective-permute-start | bytes 442376 | tf_op jit(solution)/shard_map/ppermute | solution.py:26
  17.2 1.9 %collective-permute-start.3 = (bf16[144,256]{1,0:T(8,128)(2,1)}, bf16[144,256]{1,0:T(8,128)(2,1)S(1)}, u32[]{:S(2)}, u32[]{:S(2)}) collective-permute-start(bf16[144,256]{1,0:T(8,128)(2,1)} %project.1.own_ref.refs_0_), channel_id=1, source_target_pairs={{0,20},{4,16},{8,28},{12,24},{16,4},{20,0},{24,12},{28,8},{1,21},{... | collective-permute-start | bytes 221192 | tf_op jit(solution)/shard_map/ppermute | solution.py:26
  19.2 0.9 %copy-done.5 = bf16[144,256]{1,0:T(8,128)(2,1)S(1)} copy-done((bf16[144,256]{1,0:T(8,128)(2,1)S(1)}, bf16[144,256]{1,0:T(8,128)(2,1)}, u32[]{:S(2)}) %copy-start.5) | copy-done | bytes 73752
  20.1 3.3 %own_branch.2 = (bf16[1024,1024]{1,0:T(8,128)(2,1)}, f32[128,256]{1,0:T(8,128)S(1)}) custom-call(s32[1]{0:T(128)} %bitcast.info, s32[2]{0:T(128)S(1)} %copy-done.7, bf16[144,256]{1,0:T(8,128)(2,1)S(1)} %copy-done.5, bf16[1024,1024]{1,0:T(8,128)(2,1)S(1)} %copy-done, bf16[2048,128]{1,0:T(8,128)(2,1)S(1)} %bitcast.11, bf16[1024,1024]{1,0:T(8,128)(2,1)S(1)} %copy-done.1), custom_call_target="tpu_custom_call" | custom-call | flops 671088640 | bytes 1572864 | tf_op jit(solution)/shard_map/own_branch/pallas_call | solution.py:433
  23.4 3.8 %collective-permute-done.3.refs_4_ = bf16[144,256]{1,0:T(8,128)(2,1)S(1)} collective-permute-done((bf16[144,256]{1,0:T(8,128)(2,1)}, bf16[144,256]{1,0:T(8,128)(2,1)S(1)}, u32[]{:S(2)}, u32[]{:S(2)}) %collective-permute-start.3) | collective-permute-done | bytes 73760 | tf_op jit(solution)/shard_map/ppermute | solution.py:26
  27.3 5.8 %other_branches.1 = (bf16[1024,1024]{1,0:T(8,128)(2,1)}, f32[128,256]{1,0:T(8,128)S(1)}, bf16[128,256]{1,0:T(8,128)(2,1)S(1)}, bf16[1,128,256]{2,1,0:T(8,128)(2,1)S(1)}) custom-call(s32[1]{0:T(128)} %bitcast.info, s32[2]{0:T(128)S(1)} %copy-done.7, bf16[144,256]{1,0:T(8,128)(2,1)S(1)} %copy-done.6, ...), custom_call_target="tpu_custom_call", output_to_operand_aliasing={{0}: (10, {})} | custom-call | flops 1342177280 | bytes 3145728 | tf_op jit(solution)/shard_map/other_branches/pallas_call | solution.py:433
  33.0 0.7 %collective-permute-start.4 = (bf16[1,128,256]{2,1,0:T(8,128)(2,1)S(1)}, bf16[1,128,256]{2,1,0:T(8,128)(2,1)S(1)}, u32[]{:S(2)}, u32[]{:S(2)}) collective-permute-start(bf16[1,128,256]{2,1,0:T(8,128)(2,1)S(1)} %get-tuple-element.23.grad_ref), channel_id=1, source_target_pairs={{0,4},{4,0},{8,12},{12,8},{16,20},{20,16},{24,28},{28,24},{1,5},{5... | collective-permute-start | bytes 196616 | tf_op jit(solution)/shard_map/ppermute | solution.py:26
  33.7 1.8 %collective-permute-start.5 = (bf16[128,256]{1,0:T(8,128)(2,1)S(1)}, bf16[128,256]{1,0:T(8,128)(2,1)S(1)}, u32[]{:S(2)}, u32[]{:S(2)}) collective-permute-start(bf16[128,256]{1,0:T(8,128)(2,1)S(1)} %get-tuple-element.25), channel_id=1, source_target_pairs={{0,20},{4,16},{8,28},{12,24},{16,4},{20,0},{24,12},{28,8},{1,21},{... | collective-permute-start | bytes 196616 | tf_op jit(solution)/shard_map/ppermute | solution.py:26
  35.5 2.5 %collective-permute-done.4.got_ref = bf16[1,128,256]{2,1,0:T(8,128)(2,1)S(1)} collective-permute-done((bf16[1,128,256]{2,1,0:T(8,128)(2,1)S(1)}, bf16[1,128,256]{2,1,0:T(8,128)(2,1)S(1)}, u32[]{:S(2)}, u32[]{:S(2)}) %collective-permute-start.4) | collective-permute-done | bytes 65568 | tf_op jit(solution)/shard_map/ppermute | solution.py:26
  38.0 0.6 relay.1
  38.6 1.1 %collective-permute-start.6 = (bf16[128,256]{1,0:T(8,128)(2,1)S(1)}, bf16[128,256]{1,0:T(8,128)(2,1)S(1)}, u32[]{:S(2)}, u32[]{:S(2)}) collective-permute-start(bf16[128,256]{1,0:T(8,128)(2,1)S(1)} %get-tuple-element.26), channel_id=1, source_target_pairs={{0,24},{4,28},{8,0},{12,4},{16,8},{20,12},{24,16},{28,20},{1,25},{... | collective-permute-start | bytes 196616 | tf_op jit(solution)/shard_map/ppermute | solution.py:26
  39.8 0.9 %collective-permute-start.7 = (bf16[128,256]{1,0:T(8,128)(2,1)S(1)}, bf16[128,256]{1,0:T(8,128)(2,1)S(1)}, u32[]{:S(2)}, u32[]{:S(2)}) collective-permute-start(bf16[128,256]{1,0:T(8,128)(2,1)S(1)} %get-tuple-element.27), channel_id=1, source_target_pairs={{0,8},{4,12},{8,16},{12,20},{16,24},{20,28},{24,0},{28,4},{1,9},{5... | collective-permute-start | bytes 196616 | tf_op jit(solution)/shard_map/ppermute | solution.py:26
  40.7 1.6 %copy-done.2 = bf16[1024,1024]{1,0:T(8,128)(2,1)S(1)} copy-done((bf16[1024,1024]{1,0:T(8,128)(2,1)S(1)}, bf16[1024,1024]{1,0:T(8,128)(2,1)}, u32[]{:S(2)}) %copy-start.2) | copy-done | bytes 2097176
  42.3 3.3 %own_branch.3 = (bf16[1024,1024]{1,0:T(8,128)(2,1)}, f32[128,256]{1,0:T(8,128)S(1)}) custom-call(s32[1]{0:T(128)} %bitcast.info, s32[2]{0:T(128)S(1)} %copy-done.7, bf16[144,256]{1,0:T(8,128)(2,1)S(1)} %copy-done.6, bf16[1024,1024]{1,0:T(8,128)(2,1)S(1)} %copy-done, bf16[2048,128]{1,0:T(8,128)(2,1)S(1)} %bitcast.13, ...), custom_call_target="tpu_custom_call", output_to_operand_aliasing={{0}: (6, {})} | custom-call | flops 671088640 | bytes 1572864 | tf_op jit(solution)/shard_map/own_branch/pallas_call | solution.py:433
  45.8 2.4 %back_shares.1 = (bf16[32,8192]{1,0:T(8,128)(2,1)S(1)}, bf16[32,8192]{1,0:T(8,128)(2,1)S(1)}, bf16[32,8192]{1,0:T(8,128)(2,1)S(1)}, bf16[32,8192]{1,0:T(8,128)(2,1)S(1)}) custom-call(s32[1]{0:T(128)} %bitcast.6.index, f32[128,256]{1,0:T(8,128)S(1)} %get-tuple-element.20.refs_0_, f32[128,256]{1,0:T(8,128)S(1)} %get-tuple-element.21.refs_1_, ...), custom_call_target="tpu_custom_call" | custom-call | flops 536870912 | bytes 6291456 | tf_op jit(solution)/shard_map/back_shares/pallas_call | solution.py:173
  48.3 0.5 collective-permute-start.8
  48.8 1.4 %collective-permute-done.9 = bf16[32,8192]{1,0:T(8,128)(2,1)S(1)} collective-permute-done((bf16[32,8192]{1,0:T(8,128)(2,1)S(1)}, bf16[32,8192]{1,0:T(8,128)(2,1)S(1)}, u32[]{:S(2)}, u32[]{:S(2)}) %collective-permute-start.9) | collective-permute-done | bytes 524320 | tf_op jit(solution)/shard_map/ppermute | solution.py:507
  50.3 1.6 %collective-permute-start.10 = (bf16[32,8192]{1,0:T(8,128)(2,1)S(1)}, bf16[32,8192]{1,0:T(8,128)(2,1)S(1)}, u32[]{:S(2)}, u32[]{:S(2)}) collective-permute-start(bf16[32,8192]{1,0:T(8,128)(2,1)S(1)} %add_convert_fusion.1), channel_id=1, source_target_pairs={{0,2},{1,3},{2,0},{3,1},{4,6},{5,7},{6,4},{7,5},{8,10},{9,11},{10,... | collective-permute-start | bytes 1572872 | tf_op jit(solution)/shard_map/ppermute | solution.py:507
  52.0 12.3 %collective-permute-done.10 = bf16[32,8192]{1,0:T(8,128)(2,1)S(1)} collective-permute-done((bf16[32,8192]{1,0:T(8,128)(2,1)S(1)}, bf16[32,8192]{1,0:T(8,128)(2,1)S(1)}, u32[]{:S(2)}, u32[]{:S(2)}) %collective-permute-start.10) | collective-permute-done | bytes 524320 | tf_op jit(solution)/shard_map/ppermute | solution.py:507
  64.4 0.9 %fusion = bf16[1,32,8192]{2,1,0:T(8,128)(2,1)} fusion(bf16[32,8192]{1,0:T(8,128)(2,1)S(1)} %collective-permute-done.10, bf16[32,8192]{1,0:T(8,128)(2,1)S(1)} %add_convert_fusion.2), kind=kLoop, calls=%fused_computation.3 | loop fusion | flops 1048576 | bytes 1572864 | tf_op jit(solution)/shard_map/reshape | solution.py:496
  (24 shorter events, 0.6 us)
Async XLA Ops:
  0.6 18.6 %copy-start = (bf16[1024,1024]{1,0:T(8,128)(2,1)S(1)}, bf16[1024,1024]{1,0:T(8,128)(2,1)}, u32[]{:S(2)}) copy-start(bf16[1024,1024]{1,0:T(8,128)(2,1)} %q_ref.3) | copy-start | bytes 6291460
  0.6 18.5 %copy-start.1 = (bf16[1024,1024]{1,0:T(8,128)(2,1)S(1)}, bf16[1024,1024]{1,0:T(8,128)(2,1)}, u32[]{:S(2)}) copy-start(bf16[1024,1024]{1,0:T(8,128)(2,1)} %up_ref.3) | copy-start | bytes 6291460
  0.7 18.5 %copy-start.4 = (bf16[1024,2,128]{2,1,0:T(2,128)(2,1)S(1)}, bf16[1024,2,128]{2,1,0:T(2,128)(2,1)}, u32[]{:S(2)}) copy-start(bf16[1024,2,128]{2,1,0:T(2,128)(2,1)} %param.9) | copy-start | bytes 1572868
  0.7 18.5 %copy-start.7 = (s32[2]{0:T(128)S(1)}, s32[2]{0:T(128)}, u32[]{:S(2)}) copy-start(s32[2]{0:T(128)} %prompts.9) | copy-start | bytes 28
  6.6 5.6 %collective-permute-start = (bf16[144,256]{1,0:T(8,128)(2,1)}, bf16[144,256]{1,0:T(8,128)(2,1)S(1)}, u32[]{:S(2)}, u32[]{:S(2)}) collective-permute-start(bf16[144,256]{1,0:T(8,128)(2,1)} %project.1.own_ref.refs_0_), channel_id=1, source_target_pairs={{0,4},{4,0},{8,12},{12,8},{16,20},{20,16},{24,28},{28,24},{1,5},{5... | collective-permute-start | bytes 221192 | tf_op jit(solution)/shard_map/ppermute | solution.py:26
  13.1 14.2 %collective-permute-start.2 = (bf16[2,144,256]{2,1,0:T(8,128)(2,1)S(1)}, bf16[2,144,256]{2,1,0:T(8,128)(2,1)S(1)}, u32[]{:S(2)}, u32[]{:S(2)}) collective-permute-start(bf16[2,144,256]{2,1,0:T(8,128)(2,1)S(1)} %pad_maximum_fusion), channel_id=1, source_target_pairs={{0,24},{4,28},{8,0},{12,4},{16,8},{20,12},{24,16},{28,20},{1,25},{... | collective-permute-start | bytes 442376 | tf_op jit(solution)/shard_map/ppermute | solution.py:26
  17.2 10.0 %collective-permute-start.1 = (bf16[2,144,256]{2,1,0:T(8,128)(2,1)S(1)}, bf16[2,144,256]{2,1,0:T(8,128)(2,1)S(1)}, u32[]{:S(2)}, u32[]{:S(2)}) collective-permute-start(bf16[2,144,256]{2,1,0:T(8,128)(2,1)S(1)} %pad_maximum_fusion), channel_id=1, source_target_pairs={{0,8},{4,12},{8,16},{12,20},{16,24},{20,28},{24,0},{28,4},{1,9},{5... | collective-permute-start | bytes 442376 | tf_op jit(solution)/shard_map/ppermute | solution.py:26
  17.2 10.0 %collective-permute-start.3 = (bf16[144,256]{1,0:T(8,128)(2,1)}, bf16[144,256]{1,0:T(8,128)(2,1)S(1)}, u32[]{:S(2)}, u32[]{:S(2)}) collective-permute-start(bf16[144,256]{1,0:T(8,128)(2,1)} %project.1.own_ref.refs_0_), channel_id=1, source_target_pairs={{0,20},{4,16},{8,28},{12,24},{16,4},{20,0},{24,12},{28,8},{1,21},{... | collective-permute-start | bytes 221192 | tf_op jit(solution)/shard_map/ppermute | solution.py:26
  19.2 0.9 %copy-start.5 = (bf16[144,256]{1,0:T(8,128)(2,1)S(1)}, bf16[144,256]{1,0:T(8,128)(2,1)}, u32[]{:S(2)}) copy-start(bf16[144,256]{1,0:T(8,128)(2,1)} %project.1.own_ref.refs_0_) | copy-start | bytes 221188
  20.1 7.2 %copy-start.6 = (bf16[144,256]{1,0:T(8,128)(2,1)S(1)}, bf16[144,256]{1,0:T(8,128)(2,1)}, u32[]{:S(2)}) copy-start(bf16[144,256]{1,0:T(8,128)(2,1)} %project.1.own_ref.refs_0_) | copy-start | bytes 221188
  33.0 5.0 %collective-permute-start.4 = (bf16[1,128,256]{2,1,0:T(8,128)(2,1)S(1)}, bf16[1,128,256]{2,1,0:T(8,128)(2,1)S(1)}, u32[]{:S(2)}, u32[]{:S(2)}) collective-permute-start(bf16[1,128,256]{2,1,0:T(8,128)(2,1)S(1)} %get-tuple-element.23.grad_ref), channel_id=1, source_target_pairs={{0,4},{4,0},{8,12},{12,8},{16,20},{20,16},{24,28},{28,24},{1,5},{5... | collective-permute-start | bytes 196616 | tf_op jit(solution)/shard_map/ppermute | solution.py:26
  33.7 11.9 %collective-permute-start.5 = (bf16[128,256]{1,0:T(8,128)(2,1)S(1)}, bf16[128,256]{1,0:T(8,128)(2,1)S(1)}, u32[]{:S(2)}, u32[]{:S(2)}) collective-permute-start(bf16[128,256]{1,0:T(8,128)(2,1)S(1)} %get-tuple-element.25), channel_id=1, source_target_pairs={{0,20},{4,16},{8,28},{12,24},{16,4},{20,0},{24,12},{28,8},{1,21},{... | collective-permute-start | bytes 196616 | tf_op jit(solution)/shard_map/ppermute | solution.py:26
  38.6 7.0 %collective-permute-start.6 = (bf16[128,256]{1,0:T(8,128)(2,1)S(1)}, bf16[128,256]{1,0:T(8,128)(2,1)S(1)}, u32[]{:S(2)}, u32[]{:S(2)}) collective-permute-start(bf16[128,256]{1,0:T(8,128)(2,1)S(1)} %get-tuple-element.26), channel_id=1, source_target_pairs={{0,24},{4,28},{8,0},{12,4},{16,8},{20,12},{24,16},{28,20},{1,25},{... | collective-permute-start | bytes 196616 | tf_op jit(solution)/shard_map/ppermute | solution.py:26
  39.8 6.1 %collective-permute-start.7 = (bf16[128,256]{1,0:T(8,128)(2,1)S(1)}, bf16[128,256]{1,0:T(8,128)(2,1)S(1)}, u32[]{:S(2)}, u32[]{:S(2)}) collective-permute-start(bf16[128,256]{1,0:T(8,128)(2,1)S(1)} %get-tuple-element.27), channel_id=1, source_target_pairs={{0,8},{4,12},{8,16},{12,20},{16,24},{20,28},{24,0},{28,4},{1,9},{5... | collective-permute-start | bytes 196616 | tf_op jit(solution)/shard_map/ppermute | solution.py:26
  40.7 1.6 %copy-start.2 = (bf16[1024,1024]{1,0:T(8,128)(2,1)S(1)}, bf16[1024,1024]{1,0:T(8,128)(2,1)}, u32[]{:S(2)}) copy-start(bf16[1024,1024]{1,0:T(8,128)(2,1)} %up_ref.3) | copy-start | bytes 6291460
  42.3 3.5 %copy-start.3 = (bf16[8192,2,128]{2,1,0:T(2,128)(2,1)S(1)}, bf16[8192,2,128]{2,1,0:T(2,128)(2,1)}, u32[]{:S(2)}) copy-start(bf16[8192,2,128]{2,1,0:T(2,128)(2,1)} %param.7) | copy-start | bytes 12582916
  48.2 2.0 %collective-permute-start.9 = (bf16[32,8192]{1,0:T(8,128)(2,1)S(1)}, bf16[32,8192]{1,0:T(8,128)(2,1)S(1)}, u32[]{:S(2)}, u32[]{:S(2)}) collective-permute-start(bf16[32,8192]{1,0:T(8,128)(2,1)S(1)} %get-tuple-element.31), channel_id=1, source_target_pairs={{0,1},{1,0},{2,3},{3,2},{4,5},{5,4},{6,7},{7,6},{8,9},{9,8},{10,11... | collective-permute-start | bytes 1572872 | tf_op jit(solution)/shard_map/ppermute | solution.py:507
  48.3 3.6 %collective-permute-start.8 = (bf16[32,8192]{1,0:T(8,128)(2,1)S(1)}, bf16[32,8192]{1,0:T(8,128)(2,1)S(1)}, u32[]{:S(2)}, u32[]{:S(2)}) collective-permute-start(bf16[32,8192]{1,0:T(8,128)(2,1)S(1)} %get-tuple-element.29), channel_id=1, source_target_pairs={{0,1},{1,0},{2,3},{3,2},{4,5},{5,4},{6,7},{7,6},{8,9},{9,8},{10,11... | collective-permute-start | bytes 1572872 | tf_op jit(solution)/shard_map/ppermute | solution.py:507
  50.3 14.0 %collective-permute-start.10 = (bf16[32,8192]{1,0:T(8,128)(2,1)S(1)}, bf16[32,8192]{1,0:T(8,128)(2,1)S(1)}, u32[]{:S(2)}, u32[]{:S(2)}) collective-permute-start(bf16[32,8192]{1,0:T(8,128)(2,1)S(1)} %add_convert_fusion.1), channel_id=1, source_target_pairs={{0,2},{1,3},{2,0},{3,1},{4,6},{5,7},{6,4},{7,5},{8,10},{9,11},{10,... | collective-permute-start | bytes 1572872 | tf_op jit(solution)/shard_map/ppermute | solution.py:507

commit v4 on v3

--- a/solution.py
+++ b/solution.py
@@ -16,7 +16,8 @@
 TILE = 32
 CHUNKS = 8
 VMEM = 24 << 20
-PROJECT_VMEM = 60500000
+PARTS = 2
+PROJECT_VMEM = 54500000
 NOTES = 16
 OWN, PARTNER, LOW, LOW_PAIR, HIGH, HIGH_PAIR, FAR = range(7)
 
@@ -75,9 +76,7 @@
     split[chunk % 2, :, HD:] = values
 
 
-def project_kernel(
-    info, prompts, prefix_ref, weight_ref, out_ref, rows, pairs, wide, split, sems
-):
+def project_kernel(prefix_ref, weight_ref, out_ref, rows, pairs, wide, split, sems):
     depth = rows.shape[1] // CHUNKS
     copies = []
     for chunk in range(CHUNKS):
@@ -101,25 +100,17 @@
         if chunk:
             part = rows[:, (chunk - 1) * depth : chunk * depth]
             total += contract(part, split[(chunk - 1) % 2], 1, 0)
-    out_ref[: rows.shape[0], :] = total.astype(out_ref.dtype)
-    at = lax.broadcasted_iota(jnp.int32, (NOTES, out_ref.shape[1]), 0)
-    notes = jnp.zeros(at.shape, jnp.float32)
-    branches = prompts.shape[0]
-    own = first_own(prompts, info[0], branches)
-    for number in range(branches - 1):
-        prompt = jnp.where(number >= own, prompts[number + 1], prompts[number])
-        notes = jnp.where(at == number, prompt.astype(jnp.float32), notes)
-    out_ref[rows.shape[0] :, :] = notes.astype(out_ref.dtype)
-
-
-def project(me, prompts, prefix, kv_weight):
+    out_ref[...] = total.astype(out_ref.dtype)
+
+
+def project(prefix, kv_weight):
     prefix_len, model_width = prefix.shape
     there = pl.BlockSpec(memory_space=pl.ANY)
     return pl.pallas_call(
         project_kernel,
-        in_specs=[pl.BlockSpec(memory_space=pltpu.SMEM)] * 2 + [there] * 2,
+        in_specs=[there] * 2,
         out_specs=pl.BlockSpec(memory_space=pltpu.VMEM),
-        out_shape=jax.ShapeDtypeStruct((prefix_len + NOTES, 2 * HD), jnp.bfloat16),
+        out_shape=jax.ShapeDtypeStruct((prefix_len, 2 * HD), jnp.bfloat16),
         scratch_shapes=[
             pltpu.VMEM(prefix.shape, jnp.bfloat16),
             pltpu.VMEM((2 * model_width, HD), jnp.bfloat16),
@@ -134,12 +125,13 @@
             transcendentals=0,
         ),
         name="project",
-    )(me, prompts, prefix, kv_weight.reshape(2 * model_width, HD))
-
-
-def back_kernel(index, *refs):
+    )(prefix, kv_weight.reshape(2 * model_width, HD))
+
+
+def back_kernel(part, index, *refs):
     *grads, weight_ref, far_give, far_keep, near_give, near_keep, wide, split = refs
-    depth = far_give.shape[1] // CHUNKS
+    depth = split.shape[1]
+    chunks = far_give.shape[1] // depth
     rows = far_give.shape[0]
     half, side = index[0] >> 1, index[0] & 1
     owners = (
@@ -156,34 +148,34 @@
             total = total + grad[at, :].astype(jnp.float32)
         parts.append(total.astype(jnp.bfloat16))
     kv_grad = jnp.concatenate(parts, axis=0)
-    for chunk in range(CHUNKS + 1):
-        if chunk < CHUNKS:
-            load_split(chunk, weight_ref, wide, split)
+    for chunk in range(chunks + 1):
+        if chunk < chunks:
+            load_split(part * chunks + chunk, weight_ref, wide, split)
         if chunk:
-            share = contract(kv_grad, split[(chunk - 1) % 2], 1, 1).astype(jnp.bfloat16)
+            share = contract(kv_grad, split[(part * chunks + chunk - 1) % 2], 1, 1).astype(jnp.bfloat16)
             cols = pl.ds((chunk - 1) * depth, depth)
             for number, out in enumerate((far_give, far_keep, near_give, near_keep)):
                 out[:, cols] = share[number * rows : (number + 1) * rows]
 
 
-def back_shares(index, grads, kv_weight, count):
+def back_shares(index, grads, kv_weight, count, part):
     model_width = kv_weight.shape[0]
     rows = grads[0].shape[0] // count
     here = pl.BlockSpec(memory_space=pltpu.VMEM)
     return pl.pallas_call(
-        back_kernel,
+        functools.partial(back_kernel, part),
         in_specs=[pl.BlockSpec(memory_space=pltpu.SMEM)]
         + [here] * (len(grads) + 1),
         out_specs=[here] * 4,
-        out_shape=[jax.ShapeDtypeStruct((rows, model_width), jnp.bfloat16)] * 4,
+        out_shape=[jax.ShapeDtypeStruct((rows, model_width // PARTS), jnp.bfloat16)] * 4,
         scratch_shapes=[
             pltpu.VMEM((2, 2 * model_width // CHUNKS, HD), jnp.float32),
             pltpu.VMEM((2, model_width // CHUNKS, 2 * HD), jnp.bfloat16),
         ],
         compiler_params=pltpu.CompilerParams(vmem_limit_bytes=VMEM),
         cost_estimate=pl.CostEstimate(
-            flops=4 * grads[0].shape[0] * model_width * HD,
-            bytes_accessed=2 * model_width * (grads[0].shape[0] + 2 * HD),
+            flops=4 * grads[0].shape[0] * model_width * HD // PARTS,
+            bytes_accessed=2 * model_width * (grads[0].shape[0] + 2 * HD) // PARTS,
             transcendentals=0,
         ),
         name="back_shares",
@@ -271,8 +263,8 @@
 def fill(keys, values, piece, kv_ref, base, wide):
     size = wide.shape[0]
     prefix_len = keys.shape[0] - size // 2
-    keys[:prefix_len, :] = piece[:prefix_len, :HD]
-    values[:prefix_len, :] = piece[:prefix_len, HD:]
+    keys[:prefix_len, :] = piece[:, :HD]
+    values[:prefix_len, :] = piece[:, HD:]
     pairs = kv_ref[pl.ds(pl.multiple_of(2 * base, size), size), :]
     keys[prefix_len:, :], values[prefix_len:, :] = split_pairs(pairs, wide)
 
@@ -322,7 +314,10 @@
     )
     own_part = jnp.where(source == OWN, grad, 0.0)
     far_part = jnp.where(source == FAR, grad, 0.0)
-    grad_ref[step] = grad.astype(jnp.bfloat16)
+    prefix_len = grad.shape[0]
+    grad_ref[step, :prefix_len, :] = grad.astype(jnp.bfloat16)
+    prompt = prompts[branch].astype(jnp.float32)
+    grad_ref[step, prefix_len:, :] = jnp.full((NOTES, grad.shape[1]), prompt).astype(jnp.bfloat16)
 
     @pl.when(step == 0)
     def _():
@@ -340,20 +335,19 @@
         far_grad[...] = far_total[...].astype(jnp.bfloat16)
 
 
-def relay_kernel(branches, devices, info, prompts, grad_ref, got_ref, notes_ref, *outs):
+def relay_kernel(branches, devices, info, prompts, grad_ref, got_ref, *outs):
     to_low, to_high, to_me = outs
     me = info[0]
     down, up = lax.rem(me + devices - 2, devices), lax.rem(me + 2, devices)
-    low = high = kept = jnp.zeros(grad_ref.shape[1:], jnp.float32)
-    notes = notes_ref[...].astype(jnp.float32)
-    start = notes.shape[0] - NOTES
+    low = high = kept = jnp.zeros(to_me.shape, jnp.float32)
+    prefix_len = to_me.shape[0]
     for number in range(branches - 1):
-        grad = grad_ref[number].astype(jnp.float32)
+        grad = grad_ref[number, :prefix_len, :].astype(jnp.float32)
         prompt = prompts[other_branch(number, prompts, me, branches)]
         low = low + jnp.where(prompt == down, grad, 0.0)
         high = high + jnp.where(prompt == up, grad, 0.0)
-        grad = got_ref[number].astype(jnp.float32)
-        prompt = notes[start + number : start + number + 1, :]
+        grad = got_ref[number, :prefix_len, :].astype(jnp.float32)
+        prompt = got_ref[number, prefix_len : prefix_len + NOTES, :].astype(jnp.float32)[:1]
         low = low + jnp.where(prompt == down.astype(jnp.float32), grad, 0.0)
         high = high + jnp.where(prompt == up.astype(jnp.float32), grad, 0.0)
         kept = kept + jnp.where(prompt == me.astype(jnp.float32), grad, 0.0)
@@ -362,14 +356,14 @@
     to_me[...] = kept
 
 
-def relay(devices, me, prompts, grad, got, notes):
+def relay(devices, me, prompts, grad, got):
     branches = prompts.shape[0]
     here = pl.BlockSpec(memory_space=pltpu.VMEM)
-    shape = grad.shape[1:]
+    shape = (grad.shape[1] - NOTES, grad.shape[2])
     return pl.pallas_call(
         functools.partial(relay_kernel, branches, devices),
         grid_spec=pltpu.PrefetchScalarGridSpec(
-            num_scalar_prefetch=2, grid=(1,), in_specs=[here] * 3, out_specs=[here] * 3
+            num_scalar_prefetch=2, grid=(1,), in_specs=[here] * 2, out_specs=[here] * 3
         ),
         out_shape=[
             jax.ShapeDtypeStruct(shape, jnp.bfloat16),
@@ -378,13 +372,13 @@
         ],
         compiler_params=pltpu.CompilerParams(vmem_limit_bytes=VMEM),
         name="relay",
-    )(me, prompts, grad, got, notes)
+    )(me, prompts, grad, got)
 
 
 def attention(own, heads, devices, me, prompts, pieces, query, pairs, upstream, out):
     branches = prompts.shape[0]
     answers = query.shape[0] // branches
-    prefix_len = pieces[0].shape[0] - NOTES
+    prefix_len = pieces[0].shape[0]
     width = len(heads) * HD
     steps = 1 if own else branches - 1
 
@@ -425,7 +419,7 @@
     else:
         body = functools.partial(other_kernel, heads, answers, branches, devices)
         scratch += [pltpu.VMEM(piece, jnp.float32)] * 2
-        for shape in (piece, (steps, *piece)):
+        for shape in (piece, (steps, prefix_len + NOTES, 2 * HD)):
             out_shape.append(jax.ShapeDtypeStruct(shape, jnp.bfloat16))
             out_specs.append(here)
     seen = prefix_len + (answers + BLOCK) // 2
@@ -460,11 +454,11 @@
     devices = lax.axis_size("dp")
     if devices % 2 or devices < 2 * REACH + 1:
         raise ValueError("dp size")
-    if branch_prompt.shape[0] > NOTES or devices > 256:
+    if devices > 256:
         raise ValueError("notes size")
     me = lax.axis_index("dp").astype(jnp.int32).reshape(1)
     answer_pairs = ans_kv.reshape(2 * ans_kv.shape[0], HD)
-    own_kv = project(me, branch_prompt, prefix[0], kv_weight)
+    own_kv = project(prefix[0], kv_weight)
     partner = dp_permute(own_kv, lambda i: i ^ 1)
     far = dp_permute(own_kv, far_of)
     pair = jnp.stack([own_kv, partner])
@@ -488,7 +482,7 @@
     from_far = dp_permute(to_far, far_of)
     got = dp_permute(grad, lambda i: i ^ 1)
     out, late_grad = branch(own=True, heads=late, pieces=[own_kv], out=out)
-    to_low, to_high, to_me = relay(devices, me, branch_prompt, grad, got, partner)
+    to_low, to_high, to_me = relay(devices, me, branch_prompt, grad, got)
     from_high = dp_permute(to_low, lambda i: i - 2)
     from_low = dp_permute(to_high, lambda i: i + 2)
     grads = [early_grad, late_grad, more_grad, to_me, from_far, from_high, from_low]
@@ -501,19 +495,22 @@
     if count != 4:
         raise ValueError("tensor size")
     index = lax.axis_index("tensor").astype(jnp.int32).reshape(1)
-    far_give, far_keep, near_give, near_keep = back_shares(index, grads, kv_weight, count)
 
     def swap(x, bit):
         return lax.ppermute(x, "tensor", [(i, i ^ bit) for i in range(count)])
 
     def both(a, b):
-        return a.astype(jnp.float32) + b.astype(jnp.float32)
-
-    far_sum = both(far_keep, swap(far_give, 1)).astype(jnp.bfloat16)
-    arrived = swap(far_sum, 2)
-    got = swap(near_give, 1)
-    mine = lax.optimization_barrier(both(near_keep, got).astype(jnp.bfloat16))
-    return both(mine, arrived).astype(jnp.bfloat16)
+        return (a.astype(jnp.float32) + b.astype(jnp.float32)).astype(jnp.bfloat16)
+
+    shares = [back_shares(index, grads, kv_weight, count, part) for part in range(PARTS)]
+    arrived, mine = [], []
+    for far_give, far_keep, _, _ in shares:
+        got = swap(far_give, 1)
+        arrived.append(swap(both(far_keep, got), 2))
+    for _, _, near_give, near_keep in shares:
+        got = swap(near_give, 1)
+        mine.append(lax.optimization_barrier(both(near_keep, got)))
+    return jnp.concatenate([both(a, b) for a, b in zip(mine, arrived)], axis=1)
 
 
 def solution(mesh):

time: 65.5 us -> 61.1 us (0.933)
  waiting for transfers between devices: 22.8 us -> 18.4 us
  starting transfers between devices: 15.9 us -> 17.5 us
  Pallas kernels: 21.3 us -> 19.8 us
  other arithmetic: 2.06 us -> 1.24 us
  local copies, waits for them, and re-layouts: 2.51 us -> 3.19 us
    ppermute x3 -> x6, waiting for transfers between devices: 13.7 us -> 10.9 us  [swap(): return lax.ppermute(x, 'tensor', [(i, i ^ bit) for i in range(count)])]
    ppermute x3 -> x6, starting transfers between devices: 2.15 us -> 3.89 us  [swap(): return lax.ppermute(x, 'tensor', [(i, i ^ bit) for i in range(count)])]
    ppermute x8, waiting for transfers between devices: 9.11 us -> 7.49 us  [dp_permute(): lax.ppermute(x, 'dp', [(i, target(i) % devices) for i in range(devices)])]
    pallas_call x2 -> x3, Pallas kernels: 8.28 us -> 6.82 us  [the longest x1 4.22 us: project(): pl.pallas_call(project_kernel, in_specs=[there] * 2, out_specs=pl.BlockSp...]
    another operation x1, other arithmetic: 0.9 us -> 0.01 us  [shards(): pair = jnp.stack([own_kv, partner])]
    unnamed x16 -> x12, local copies, waits for them, and re-layouts: 2.51 us -> 3.19 us
  transfers between devices with their start and end apart: 11 -> 14, of which waited for: 6 -> 6; matrix products, arithmetic and copies ran while one was open for 0% -> 1% of each run, Pallas kernels for 11% -> 14%
where the time goes in v4:
time: 61.1 us; the launch traced here: 61 us
  Pallas kernels  19.8 us (32%)
  waiting for transfers between devices  18.4 us (30%)
  starting transfers between devices  17.5 us (29%)
  local copies, waits for them, and re-layouts  3.19 us (5%)
  other arithmetic  1.24 us (2%)
  between operations  0.76 us (1%)
    ppermute x8, starting transfers between devices, dp_permute(): lax.ppermute(x, 'dp', [(i, target(i) % devices) for i in range(devices)])  13.6 us
    pallas_call x3, Pallas kernels, attention(): pl.pallas_call(body, grid_spec=pltpu.PrefetchScalarGridSpec(num_scalar_pr...  12.4 us
    ppermute x6, waiting for transfers between devices, swap(): return lax.ppermute(x, 'tensor', [(i, i ^ bit) for i in range(count)])  10.9 us
    ppermute x8, waiting for transfers between devices, dp_permute(): lax.ppermute(x, 'dp', [(i, target(i) % devices) for i in range(devices)])  7.49 us
    pallas_call x1, Pallas kernels, project(): pl.pallas_call(project_kernel, in_specs=[there] * 2, out_specs=pl.BlockSp...  4.22 us
    ppermute x6, starting transfers between devices, swap(): return lax.ppermute(x, 'tensor', [(i, i ^ bit) for i in range(count)])  3.89 us
    unnamed x12, local copies, waits for them, and re-layouts  3.19 us
    pallas_call x2, Pallas kernels, back_shares(): pl.pallas_call(functools.partial(back_kernel, part), in_specs=[pl.BlockSp...  2.6 us
  transfers between devices with their start and end apart: 14, of which 6 were waited for; matrix products, arithmetic and copies ran while one was open for 1% of the time, Pallas kernels for 14%

profile of v4, /device:TPU:0, one launch (start us, length us, event | category | flops | bytes accessed | tf_op | source)
XLA Modules:
  0.0 61.0 jit_solution(15987282872791179807)
XLA Ops:
  0.7 4.2 %project.1.own_ref.refs_0_ = bf16[128,256]{1,0:T(8,128)(2,1)S(1)} custom-call(bf16[128,8192]{1,0:T(8,128)(2,1)} %bitcast.17, bf16[16384,128]{1,0:T(8,128)(2,1)} %bitcast.9), custom_call_target="tpu_custom_call" | custom-call | flops 536870912 | bytes 6291456 | tf_op jit(solution)/shard_map/project/pallas_call | solution.py:109
  4.9 3.0 %collective-permute-start = (bf16[128,256]{1,0:T(8,128)(2,1)S(1)}, bf16[128,256]{1,0:T(8,128)(2,1)S(1)}, u32[]{:S(2)}, u32[]{:S(2)}) collective-permute-start(bf16[128,256]{1,0:T(8,128)(2,1)S(1)} %project.1.own_ref.refs_0_), channel_id=1, source_target_pairs={{0,4},{4,0},{8,12},{12,8},{16,20},{20,16},{24,28},{28,24},{1,5},{5... | collective-permute-start | bytes 196616 | tf_op jit(solution)/shard_map/ppermute | solution.py:27
  7.9 2.2 %collective-permute-done.refs_1_ = bf16[128,256]{1,0:T(8,128)(2,1)S(1)} collective-permute-done((bf16[128,256]{1,0:T(8,128)(2,1)S(1)}, bf16[128,256]{1,0:T(8,128)(2,1)S(1)}, u32[]{:S(2)}, u32[]{:S(2)}) %collective-permute-start) | collective-permute-done | bytes 65568 | tf_op jit(solution)/shard_map/ppermute | solution.py:27
  10.2 4.2 %collective-permute-start.2 = (bf16[2,128,256]{2,1,0:T(8,128)(2,1)S(1)}, bf16[2,128,256]{2,1,0:T(8,128)(2,1)S(1)}, u32[]{:S(2)}, u32[]{:S(2)}) collective-permute-start(bf16[2,128,256]{2,1,0:T(8,128)(2,1)S(1)} %pad_maximum_fusion), channel_id=1, source_target_pairs={{0,24},{4,28},{8,0},{12,4},{16,8},{20,12},{24,16},{28,20},{1,25},{... | collective-permute-start | bytes 393224 | tf_op jit(solution)/shard_map/ppermute | solution.py:27
  14.4 1.9 %collective-permute-start.3 = (bf16[128,256]{1,0:T(8,128)(2,1)S(1)}, bf16[128,256]{1,0:T(8,128)(2,1)S(1)}, u32[]{:S(2)}, u32[]{:S(2)}) collective-permute-start(bf16[128,256]{1,0:T(8,128)(2,1)S(1)} %project.1.own_ref.refs_0_), channel_id=1, source_target_pairs={{0,20},{4,16},{8,28},{12,24},{16,4},{20,0},{24,12},{28,8},{1,21},{... | collective-permute-start | bytes 196616 | tf_op jit(solution)/shard_map/ppermute | solution.py:27
  16.3 1.6 %copy-done.2 = bf16[1024,1024]{1,0:T(8,128)(2,1)S(1)} copy-done((bf16[1024,1024]{1,0:T(8,128)(2,1)S(1)}, bf16[1024,1024]{1,0:T(8,128)(2,1)}, u32[]{:S(2)}) %copy-start.2) | copy-done | bytes 2097176
  17.9 3.3 %own_branch.2 = (bf16[1024,1024]{1,0:T(8,128)(2,1)}, f32[128,256]{1,0:T(8,128)S(1)}) custom-call(s32[1]{0:T(128)} %bitcast.info, s32[2]{0:T(128)S(1)} %copy-done.5, bf16[128,256]{1,0:T(8,128)(2,1)S(1)} %project.1.own_ref.refs_0_, bf16[1024,1024]{1,0:T(8,128)(2,1)S(1)} %copy-done.1, bf16[2048,128]{1,0:T(8,128)(2,1)S(1)} %bitcast.12, ...), custom_call_target="tpu_custom_call" | custom-call | flops 671088640 | bytes 1572864 | tf_op jit(solution)/shard_map/own_branch/pallas_call | solution.py:427
  21.2 2.4 %collective-permute-done.3.refs_4_ = bf16[128,256]{1,0:T(8,128)(2,1)S(1)} collective-permute-done((bf16[128,256]{1,0:T(8,128)(2,1)S(1)}, bf16[128,256]{1,0:T(8,128)(2,1)S(1)}, u32[]{:S(2)}, u32[]{:S(2)}) %collective-permute-start.3) | collective-permute-done | bytes 65568 | tf_op jit(solution)/shard_map/ppermute | solution.py:27
  23.6 5.7 %other_branches.1 = (bf16[1024,1024]{1,0:T(8,128)(2,1)}, f32[128,256]{1,0:T(8,128)S(1)}, bf16[128,256]{1,0:T(8,128)(2,1)S(1)}, bf16[1,144,256]{2,1,0:T(8,128)(2,1)S(1)}) custom-call(s32[1]{0:T(128)} %bitcast.info, s32[2]{0:T(128)S(1)} %copy-done.5, bf16[128,256]{1,0:T(8,128)(2,1)S(1)} %project.1.own_ref.refs_0_, ...), custom_call_target="tpu_custom_call", output_to_operand_aliasing={{0}: (10, {})} | custom-call | flops 1342177280 | bytes 3145728 | tf_op jit(solution)/shard_map/other_branches/pallas_call | solution.py:427
  29.4 0.7 %collective-permute-start.4 = (bf16[1,144,256]{2,1,0:T(8,128)(2,1)S(1)}, bf16[1,144,256]{2,1,0:T(8,128)(2,1)S(1)}, u32[]{:S(2)}, u32[]{:S(2)}) collective-permute-start(bf16[1,144,256]{2,1,0:T(8,128)(2,1)S(1)} %get-tuple-element.27.grad_ref), channel_id=1, source_target_pairs={{0,4},{4,0},{8,12},{12,8},{16,20},{20,16},{24,28},{28,24},{1,5},{5... | collective-permute-start | bytes 221192 | tf_op jit(solution)/shard_map/ppermute | solution.py:27
  30.0 1.7 %collective-permute-start.5 = (bf16[128,256]{1,0:T(8,128)(2,1)S(1)}, bf16[128,256]{1,0:T(8,128)(2,1)S(1)}, u32[]{:S(2)}, u32[]{:S(2)}) collective-permute-start(bf16[128,256]{1,0:T(8,128)(2,1)S(1)} %get-tuple-element.29), channel_id=1, source_target_pairs={{0,20},{4,16},{8,28},{12,24},{16,4},{20,0},{24,12},{28,8},{1,21},{... | collective-permute-start | bytes 196616 | tf_op jit(solution)/shard_map/ppermute | solution.py:27
  31.7 2.7 %collective-permute-done.4.got_ref = bf16[1,144,256]{2,1,0:T(8,128)(2,1)S(1)} collective-permute-done((bf16[1,144,256]{2,1,0:T(8,128)(2,1)S(1)}, bf16[1,144,256]{2,1,0:T(8,128)(2,1)S(1)}, u32[]{:S(2)}, u32[]{:S(2)}) %collective-permute-start.4) | collective-permute-done | bytes 73760 | tf_op jit(solution)/shard_map/ppermute | solution.py:27
  34.4 0.6 relay.1
  35.0 1.1 %collective-permute-start.6 = (bf16[128,256]{1,0:T(8,128)(2,1)S(1)}, bf16[128,256]{1,0:T(8,128)(2,1)S(1)}, u32[]{:S(2)}, u32[]{:S(2)}) collective-permute-start(bf16[128,256]{1,0:T(8,128)(2,1)S(1)} %get-tuple-element.30), channel_id=1, source_target_pairs={{0,24},{4,28},{8,0},{12,4},{16,8},{20,12},{24,16},{28,20},{1,25},{... | collective-permute-start | bytes 196616 | tf_op jit(solution)/shard_map/ppermute | solution.py:27
  36.2 0.9 %collective-permute-start.7 = (bf16[128,256]{1,0:T(8,128)(2,1)S(1)}, bf16[128,256]{1,0:T(8,128)(2,1)S(1)}, u32[]{:S(2)}, u32[]{:S(2)}) collective-permute-start(bf16[128,256]{1,0:T(8,128)(2,1)S(1)} %get-tuple-element.31), channel_id=1, source_target_pairs={{0,8},{4,12},{8,16},{12,20},{16,24},{20,28},{24,0},{28,4},{1,9},{5... | collective-permute-start | bytes 196616 | tf_op jit(solution)/shard_map/ppermute | solution.py:27
  37.1 1.6 %copy-done.3 = bf16[1024,1024]{1,0:T(8,128)(2,1)S(1)} copy-done((bf16[1024,1024]{1,0:T(8,128)(2,1)S(1)}, bf16[1024,1024]{1,0:T(8,128)(2,1)}, u32[]{:S(2)}) %copy-start.3) | copy-done | bytes 2097176
  38.7 3.3 %own_branch.3 = (bf16[1024,1024]{1,0:T(8,128)(2,1)}, f32[128,256]{1,0:T(8,128)S(1)}) custom-call(s32[1]{0:T(128)} %bitcast.info, s32[2]{0:T(128)S(1)} %copy-done.5, bf16[128,256]{1,0:T(8,128)(2,1)S(1)} %project.1.own_ref.refs_0_, bf16[1024,1024]{1,0:T(8,128)(2,1)S(1)} %copy-done.1, bf16[2048,128]{1,0:T(8,128)(2,1)S(1)} %bitcast.14, ...), custom_call_target="tpu_custom_call", output_to_operand_aliasing={{0}: (6, {})} | custom-call | flops 671088640 | bytes 1572864 | tf_op jit(solution)/shard_map/own_branch/pallas_call | solution.py:427
  42.2 1.3 %back_shares.3 = (bf16[32,4096]{1,0:T(8,128)(2,1)S(1)}, bf16[32,4096]{1,0:T(8,128)(2,1)S(1)}, bf16[32,4096]{1,0:T(8,128)(2,1)S(1)}, bf16[32,4096]{1,0:T(8,128)(2,1)S(1)}) custom-call(s32[1]{0:T(128)} %bitcast.6.index, f32[128,256]{1,0:T(8,128)S(1)} %get-tuple-element.24.refs_0_, f32[128,256]{1,0:T(8,128)S(1)} %get-tuple-element.25.refs_1_, ...), custom_call_target="tpu_custom_call" | custom-call | flops 268435456 | bytes 3145728 | tf_op jit(solution)/shard_map/back_shares/pallas_call | solution.py:165
  44.1 1.3 %back_shares.2 = (bf16[32,4096]{1,0:T(8,128)(2,1)S(1)}, bf16[32,4096]{1,0:T(8,128)(2,1)S(1)}, bf16[32,4096]{1,0:T(8,128)(2,1)S(1)}, bf16[32,4096]{1,0:T(8,128)(2,1)S(1)}) custom-call(s32[1]{0:T(128)} %bitcast.6.index, f32[128,256]{1,0:T(8,128)S(1)} %get-tuple-element.24.refs_0_, f32[128,256]{1,0:T(8,128)S(1)} %get-tuple-element.25.refs_1_, ...), custom_call_target="tpu_custom_call" | custom-call | flops 268435456 | bytes 3145728 | tf_op jit(solution)/shard_map/back_shares/pallas_call | solution.py:165
  46.1 1.6 %collective-permute-start.13 = (bf16[32,4096]{1,0:T(8,128)(2,1)S(1)}, bf16[32,4096]{1,0:T(8,128)(2,1)S(1)}, u32[]{:S(2)}, u32[]{:S(2)}) collective-permute-start(bf16[32,4096]{1,0:T(8,128)(2,1)S(1)} %add_convert_fusion.1), channel_id=1, source_target_pairs={{0,2},{1,3},{2,0},{3,1},{4,6},{5,7},{6,4},{7,5},{8,10},{9,11},{10,... | collective-permute-start | bytes 786440 | tf_op jit(solution)/shard_map/ppermute | solution.py:500
  47.9 1.2 %collective-permute-start.10 = (bf16[32,4096]{1,0:T(8,128)(2,1)S(1)}, bf16[32,4096]{1,0:T(8,128)(2,1)S(1)}, u32[]{:S(2)}, u32[]{:S(2)}) collective-permute-start(bf16[32,4096]{1,0:T(8,128)(2,1)S(1)} %add_convert_fusion.4), channel_id=1, source_target_pairs={{0,2},{1,3},{2,0},{3,1},{4,6},{5,7},{6,4},{7,5},{8,10},{9,11},{10,... | collective-permute-start | bytes 786440 | tf_op jit(solution)/shard_map/ppermute | solution.py:500
  49.1 6.3 %collective-permute-done.13 = bf16[32,4096]{1,0:T(8,128)(2,1)S(1)} collective-permute-done((bf16[32,4096]{1,0:T(8,128)(2,1)S(1)}, bf16[32,4096]{1,0:T(8,128)(2,1)S(1)}, u32[]{:S(2)}, u32[]{:S(2)}) %collective-permute-start.13) | collective-permute-done | bytes 262176 | tf_op jit(solution)/shard_map/ppermute | solution.py:500
  55.4 4.7 %collective-permute-done.10 = bf16[32,4096]{1,0:T(8,128)(2,1)S(1)} collective-permute-done((bf16[32,4096]{1,0:T(8,128)(2,1)S(1)}, bf16[32,4096]{1,0:T(8,128)(2,1)S(1)}, u32[]{:S(2)}, u32[]{:S(2)}) %collective-permute-start.10) | collective-permute-done | bytes 262176 | tf_op jit(solution)/shard_map/ppermute | solution.py:500
  60.1 0.8 %maximum_bitcast_fusion = bf16[1,32,8192]{2,1,0:T(8,128)(2,1)} fusion(bf16[32,4096]{1,0:T(8,128)(2,1)S(1)} %add_convert_fusion, bf16[32,4096]{1,0:T(8,128)(2,1)S(1)} %add_convert_fusion.3), kind=kLoop, calls=%fused_computation | loop fusion | flops 1048576 | bytes 1048576 | tf_op jit(solution)/shard_map/reshape | solution.py:490
  (31 shorter events, 1.8 us)
Async XLA Ops:
  0.6 15.7 %copy-start.1 = (bf16[1024,1024]{1,0:T(8,128)(2,1)S(1)}, bf16[1024,1024]{1,0:T(8,128)(2,1)}, u32[]{:S(2)}) copy-start(bf16[1024,1024]{1,0:T(8,128)(2,1)} %q_ref.3) | copy-start | bytes 6291460
  0.6 15.7 %copy-start.4 = (bf16[1024,2,128]{2,1,0:T(2,128)(2,1)S(1)}, bf16[1024,2,128]{2,1,0:T(2,128)(2,1)}, u32[]{:S(2)}) copy-start(bf16[1024,2,128]{2,1,0:T(2,128)(2,1)} %param.9) | copy-start | bytes 1572868
  0.7 15.7 %copy-start.5 = (s32[2]{0:T(128)S(1)}, s32[2]{0:T(128)}, u32[]{:S(2)}) copy-start(s32[2]{0:T(128)} %prompts.7) | copy-start | bytes 28
  4.9 5.3 %collective-permute-start = (bf16[128,256]{1,0:T(8,128)(2,1)S(1)}, bf16[128,256]{1,0:T(8,128)(2,1)S(1)}, u32[]{:S(2)}, u32[]{:S(2)}) collective-permute-start(bf16[128,256]{1,0:T(8,128)(2,1)S(1)} %project.1.own_ref.refs_0_), channel_id=1, source_target_pairs={{0,4},{4,0},{8,12},{12,8},{16,20},{20,16},{24,28},{28,24},{1,5},{5... | collective-permute-start | bytes 196616 | tf_op jit(solution)/shard_map/ppermute | solution.py:27
  10.2 13.4 %collective-permute-start.2 = (bf16[2,128,256]{2,1,0:T(8,128)(2,1)S(1)}, bf16[2,128,256]{2,1,0:T(8,128)(2,1)S(1)}, u32[]{:S(2)}, u32[]{:S(2)}) collective-permute-start(bf16[2,128,256]{2,1,0:T(8,128)(2,1)S(1)} %pad_maximum_fusion), channel_id=1, source_target_pairs={{0,24},{4,28},{8,0},{12,4},{16,8},{20,12},{24,16},{28,20},{1,25},{... | collective-permute-start | bytes 393224 | tf_op jit(solution)/shard_map/ppermute | solution.py:27
  14.4 9.2 %collective-permute-start.1 = (bf16[2,128,256]{2,1,0:T(8,128)(2,1)S(1)}, bf16[2,128,256]{2,1,0:T(8,128)(2,1)S(1)}, u32[]{:S(2)}, u32[]{:S(2)}) collective-permute-start(bf16[2,128,256]{2,1,0:T(8,128)(2,1)S(1)} %pad_maximum_fusion), channel_id=1, source_target_pairs={{0,8},{4,12},{8,16},{12,20},{16,24},{20,28},{24,0},{28,4},{1,9},{5... | collective-permute-start | bytes 393224 | tf_op jit(solution)/shard_map/ppermute | solution.py:27
  14.4 9.2 %collective-permute-start.3 = (bf16[128,256]{1,0:T(8,128)(2,1)S(1)}, bf16[128,256]{1,0:T(8,128)(2,1)S(1)}, u32[]{:S(2)}, u32[]{:S(2)}) collective-permute-start(bf16[128,256]{1,0:T(8,128)(2,1)S(1)} %project.1.own_ref.refs_0_), channel_id=1, source_target_pairs={{0,20},{4,16},{8,28},{12,24},{16,4},{20,0},{24,12},{28,8},{1,21},{... | collective-permute-start | bytes 196616 | tf_op jit(solution)/shard_map/ppermute | solution.py:27
  16.3 1.6 %copy-start.2 = (bf16[1024,1024]{1,0:T(8,128)(2,1)S(1)}, bf16[1024,1024]{1,0:T(8,128)(2,1)}, u32[]{:S(2)}) copy-start(bf16[1024,1024]{1,0:T(8,128)(2,1)} %up_ref.3) | copy-start | bytes 6291460
  29.4 5.1 %collective-permute-start.4 = (bf16[1,144,256]{2,1,0:T(8,128)(2,1)S(1)}, bf16[1,144,256]{2,1,0:T(8,128)(2,1)S(1)}, u32[]{:S(2)}, u32[]{:S(2)}) collective-permute-start(bf16[1,144,256]{2,1,0:T(8,128)(2,1)S(1)} %get-tuple-element.27.grad_ref), channel_id=1, source_target_pairs={{0,4},{4,0},{8,12},{12,8},{16,20},{20,16},{24,28},{28,24},{1,5},{5... | collective-permute-start | bytes 221192 | tf_op jit(solution)/shard_map/ppermute | solution.py:27
  30.0 12.0 %collective-permute-start.5 = (bf16[128,256]{1,0:T(8,128)(2,1)S(1)}, bf16[128,256]{1,0:T(8,128)(2,1)S(1)}, u32[]{:S(2)}, u32[]{:S(2)}) collective-permute-start(bf16[128,256]{1,0:T(8,128)(2,1)S(1)} %get-tuple-element.29), channel_id=1, source_target_pairs={{0,20},{4,16},{8,28},{12,24},{16,4},{20,0},{24,12},{28,8},{1,21},{... | collective-permute-start | bytes 196616 | tf_op jit(solution)/shard_map/ppermute | solution.py:27
  35.0 7.0 %collective-permute-start.6 = (bf16[128,256]{1,0:T(8,128)(2,1)S(1)}, bf16[128,256]{1,0:T(8,128)(2,1)S(1)}, u32[]{:S(2)}, u32[]{:S(2)}) collective-permute-start(bf16[128,256]{1,0:T(8,128)(2,1)S(1)} %get-tuple-element.30), channel_id=1, source_target_pairs={{0,24},{4,28},{8,0},{12,4},{16,8},{20,12},{24,16},{28,20},{1,25},{... | collective-permute-start | bytes 196616 | tf_op jit(solution)/shard_map/ppermute | solution.py:27
  36.2 6.1 %collective-permute-start.7 = (bf16[128,256]{1,0:T(8,128)(2,1)S(1)}, bf16[128,256]{1,0:T(8,128)(2,1)S(1)}, u32[]{:S(2)}, u32[]{:S(2)}) collective-permute-start(bf16[128,256]{1,0:T(8,128)(2,1)S(1)} %get-tuple-element.31), channel_id=1, source_target_pairs={{0,8},{4,12},{8,16},{12,20},{16,24},{20,28},{24,0},{28,4},{1,9},{5... | collective-permute-start | bytes 196616 | tf_op jit(solution)/shard_map/ppermute | solution.py:27
  37.1 1.6 %copy-start.3 = (bf16[1024,1024]{1,0:T(8,128)(2,1)S(1)}, bf16[1024,1024]{1,0:T(8,128)(2,1)}, u32[]{:S(2)}) copy-start(bf16[1024,1024]{1,0:T(8,128)(2,1)} %up_ref.3) | copy-start | bytes 6291460
  38.7 3.5 %copy-start = (bf16[8192,2,128]{2,1,0:T(2,128)(2,1)S(1)}, bf16[8192,2,128]{2,1,0:T(2,128)(2,1)}, u32[]{:S(2)}) copy-start(bf16[8192,2,128]{2,1,0:T(2,128)(2,1)} %param.7) | copy-start | bytes 12582916
  43.5 2.5 %collective-permute-start.12 = (bf16[32,4096]{1,0:T(8,128)(2,1)S(1)}, bf16[32,4096]{1,0:T(8,128)(2,1)S(1)}, u32[]{:S(2)}, u32[]{:S(2)}) collective-permute-start(bf16[32,4096]{1,0:T(8,128)(2,1)S(1)} %get-tuple-element.39), channel_id=1, source_target_pairs={{0,1},{1,0},{2,3},{3,2},{4,5},{5,4},{6,7},{7,6},{8,9},{9,8},{10,11... | collective-permute-start | bytes 786440 | tf_op jit(solution)/shard_map/ppermute | solution.py:500
  43.6 4.0 %collective-permute-start.11 = (bf16[32,4096]{1,0:T(8,128)(2,1)S(1)}, bf16[32,4096]{1,0:T(8,128)(2,1)S(1)}, u32[]{:S(2)}, u32[]{:S(2)}) collective-permute-start(bf16[32,4096]{1,0:T(8,128)(2,1)S(1)} %get-tuple-element.37), channel_id=1, source_target_pairs={{0,1},{1,0},{2,3},{3,2},{4,5},{5,4},{6,7},{7,6},{8,9},{9,8},{10,11... | collective-permute-start | bytes 786440 | tf_op jit(solution)/shard_map/ppermute | solution.py:500
  45.4 2.3 %collective-permute-start.8 = (bf16[32,4096]{1,0:T(8,128)(2,1)S(1)}, bf16[32,4096]{1,0:T(8,128)(2,1)S(1)}, u32[]{:S(2)}, u32[]{:S(2)}) collective-permute-start(bf16[32,4096]{1,0:T(8,128)(2,1)S(1)} %get-tuple-element.33), channel_id=1, source_target_pairs={{0,1},{1,0},{2,3},{3,2},{4,5},{5,4},{6,7},{7,6},{8,9},{9,8},{10,11... | collective-permute-start | bytes 786440 | tf_op jit(solution)/shard_map/ppermute | solution.py:500
  45.6 2.2 %collective-permute-start.9 = (bf16[32,4096]{1,0:T(8,128)(2,1)S(1)}, bf16[32,4096]{1,0:T(8,128)(2,1)S(1)}, u32[]{:S(2)}, u32[]{:S(2)}) collective-permute-start(bf16[32,4096]{1,0:T(8,128)(2,1)S(1)} %get-tuple-element.35), channel_id=1, source_target_pairs={{0,1},{1,0},{2,3},{3,2},{4,5},{5,4},{6,7},{7,6},{8,9},{9,8},{10,11... | collective-permute-start | bytes 786440 | tf_op jit(solution)/shard_map/ppermute | solution.py:500
  46.1 9.2 %collective-permute-start.13 = (bf16[32,4096]{1,0:T(8,128)(2,1)S(1)}, bf16[32,4096]{1,0:T(8,128)(2,1)S(1)}, u32[]{:S(2)}, u32[]{:S(2)}) collective-permute-start(bf16[32,4096]{1,0:T(8,128)(2,1)S(1)} %add_convert_fusion.1), channel_id=1, source_target_pairs={{0,2},{1,3},{2,0},{3,1},{4,6},{5,7},{6,4},{7,5},{8,10},{9,11},{10,... | collective-permute-start | bytes 786440 | tf_op jit(solution)/shard_map/ppermute | solution.py:500
  47.9 12.2 %collective-permute-start.10 = (bf16[32,4096]{1,0:T(8,128)(2,1)S(1)}, bf16[32,4096]{1,0:T(8,128)(2,1)S(1)}, u32[]{:S(2)}, u32[]{:S(2)}) collective-permute-start(bf16[32,4096]{1,0:T(8,128)(2,1)S(1)} %add_convert_fusion.4), channel_id=1, source_target_pairs={{0,2},{1,3},{2,0},{3,1},{4,6},{5,7},{6,4},{7,5},{8,10},{9,11},{10,... | collective-permute-start | bytes 786440 | tf_op jit(solution)/shard_map/ppermute | solution.py:500

commit v5 on v4

--- a/solution.py
+++ b/solution.py
@@ -19,7 +19,7 @@
 PARTS = 2
 PROJECT_VMEM = 54500000
 NOTES = 16
-OWN, PARTNER, LOW, LOW_PAIR, HIGH, HIGH_PAIR, FAR = range(7)
+OWN, PARTNER, LOW, LOW_PAIR, HIGH, HIGH_PAIR, FAR, SOURCES = range(8)
 
 
 def dp_permute(x, target):
@@ -293,22 +293,13 @@
 
 
 def other_kernel(heads, answers, branches, devices, info, prompts, *refs):
-    own_ref, partner_ref, low_ref, high_ref, far_ref = refs[:5]
-    q_ref, kv_ref, up_ref, _, out_ref, own_grad, far_grad, grad_ref = refs[5:13]
-    *buffers, own_total, far_total = refs[13:]
+    pieces = refs[:SOURCES]
+    q_ref, kv_ref, up_ref, _, out_ref, own_grad, far_grad, grad_ref = refs[SOURCES : SOURCES + 8]
+    *buffers, own_total, far_total = refs[SOURCES + 8 :]
     step = pl.program_id(0)
     me = info[0]
     branch = other_branch(step, prompts, me, branches)
     source = source_of(prompts[branch], me, devices)
-    pieces = [
-        own_ref,
-        partner_ref,
-        low_ref.at[0],
-        low_ref.at[1],
-        high_ref.at[0],
-        high_ref.at[1],
-        far_ref,
-    ]
     grad = branch_pass(
         heads, branch * answers, source, pieces, q_ref, kv_ref, up_ref, out_ref, buffers
     )
@@ -461,9 +452,10 @@
     own_kv = project(prefix[0], kv_weight)
     partner = dp_permute(own_kv, lambda i: i ^ 1)
     far = dp_permute(own_kv, far_of)
-    pair = jnp.stack([own_kv, partner])
-    low = dp_permute(pair, lambda i: i + 2)
-    high = dp_permute(pair, lambda i: i - 2)
+    low = dp_permute(own_kv, lambda i: i + 2)
+    high = dp_permute(own_kv, lambda i: i - 2)
+    low_pair = dp_permute(partner, lambda i: i + 2)
+    high_pair = dp_permute(partner, lambda i: i - 2)
     branch = functools.partial(
         attention,
         devices=devices,
@@ -477,7 +469,7 @@
     early, late = heads[: len(heads) // 2], heads[len(heads) // 2 :]
     out, early_grad = branch(own=True, heads=early, pieces=[own_kv], out=None)
     out, more_grad, to_far, grad = branch(
-        own=False, heads=heads, pieces=[own_kv, partner, low, high, far], out=out
+        own=False, heads=heads, pieces=[own_kv, partner, low, low_pair, high, high_pair, far], out=out
     )
     from_far = dp_permute(to_far, far_of)
     got = dp_permute(grad, lambda i: i ^ 1)

time: 61.1 us -> 60.2 us (0.985)
  waiting for transfers between devices: 18.4 us -> 16.5 us
  starting transfers between devices: 17.5 us -> 18.5 us
    ppermute x8 -> x10, waiting for transfers between devices: 7.49 us -> 5.57 us  [dp_permute(): lax.ppermute(x, 'dp', [(i, target(i) % devices) for i in range(devices)])]
    ppermute x8 -> x10, starting transfers between devices: 13.6 us -> 14.7 us  [dp_permute(): lax.ppermute(x, 'dp', [(i, target(i) % devices) for i in range(devices)])]
  transfers between devices with their start and end apart: 14 -> 16, of which waited for: 6 -> 5; matrix products, arithmetic and copies ran while one was open for 1% -> 1% of each run, Pallas kernels for 14% -> 14%
where the time goes in v5:
time: 60.2 us; the launch traced here: 60.1 us
  Pallas kernels  19.8 us (33%)
  starting transfers between devices  18.5 us (31%)
  waiting for transfers between devices  16.5 us (27%)
  local copies, waits for them, and re-layouts  3.19 us (5%)
  other arithmetic  1.23 us (2%)
  between operations  0.78 us (1%)
    ppermute x10, starting transfers between devices, dp_permute(): lax.ppermute(x, 'dp', [(i, target(i) % devices) for i in range(devices)])  14.7 us
    pallas_call x3, Pallas kernels, attention(): pl.pallas_call(body, grid_spec=pltpu.PrefetchScalarGridSpec(num_scalar_pr...  12.4 us
    ppermute x6, waiting for transfers between devices, swap(): return lax.ppermute(x, 'tensor', [(i, i ^ bit) for i in range(count)])  10.9 us
    ppermute x10, waiting for transfers between devices, dp_permute(): lax.ppermute(x, 'dp', [(i, target(i) % devices) for i in range(devices)])  5.57 us
    pallas_call x1, Pallas kernels, project(): pl.pallas_call(project_kernel, in_specs=[there] * 2, out_specs=pl.BlockSp...  4.22 us
    ppermute x6, starting transfers between devices, swap(): return lax.ppermute(x, 'tensor', [(i, i ^ bit) for i in range(count)])  3.89 us
    unnamed x12, local copies, waits for them, and re-layouts  3.19 us
    pallas_call x2, Pallas kernels, back_shares(): pl.pallas_call(functools.partial(back_kernel, part), in_specs=[pl.BlockSp...  2.61 us
  transfers between devices with their start and end apart: 16, of which 5 were waited for; matrix products, arithmetic and copies ran while one was open for 1% of the time, Pallas kernels for 14%

profile of v5, /device:TPU:0, one launch (start us, length us, event | category | flops | bytes accessed | tf_op | source)
XLA Modules:
  0.0 60.1 jit_solution(57506085746188793)
XLA Ops:
  0.7 4.2 %project.1.own_ref.refs_0_ = bf16[128,256]{1,0:T(8,128)(2,1)S(1)} custom-call(bf16[128,8192]{1,0:T(8,128)(2,1)} %bitcast.13, bf16[16384,128]{1,0:T(8,128)(2,1)} %bitcast.7), custom_call_target="tpu_custom_call" | custom-call | flops 536870912 | bytes 6291456 | tf_op jit(solution)/shard_map/project/pallas_call | solution.py:109
  4.9 3.0 %collective-permute-start = (bf16[128,256]{1,0:T(8,128)(2,1)S(1)}, bf16[128,256]{1,0:T(8,128)(2,1)S(1)}, u32[]{:S(2)}, u32[]{:S(2)}) collective-permute-start(bf16[128,256]{1,0:T(8,128)(2,1)S(1)} %project.1.own_ref.refs_0_), channel_id=1, source_target_pairs={{0,4},{4,0},{8,12},{12,8},{16,20},{20,16},{24,28},{28,24},{1,5},{5... | collective-permute-start | bytes 196616 | tf_op jit(solution)/shard_map/ppermute | solution.py:27
  7.9 2.6 %collective-permute-start.5 = (bf16[128,256]{1,0:T(8,128)(2,1)S(1)}, bf16[128,256]{1,0:T(8,128)(2,1)S(1)}, u32[]{:S(2)}, u32[]{:S(2)}) collective-permute-start(bf16[128,256]{1,0:T(8,128)(2,1)S(1)} %project.1.own_ref.refs_0_), channel_id=1, source_target_pairs={{0,20},{4,16},{8,28},{12,24},{16,4},{20,0},{24,12},{28,8},{1,21},{... | collective-permute-start | bytes 196616 | tf_op jit(solution)/shard_map/ppermute | solution.py:27
  10.5 1.4 %collective-permute-start.3 = (bf16[128,256]{1,0:T(8,128)(2,1)S(1)}, bf16[128,256]{1,0:T(8,128)(2,1)S(1)}, u32[]{:S(2)}, u32[]{:S(2)}) collective-permute-start(bf16[128,256]{1,0:T(8,128)(2,1)S(1)} %project.1.own_ref.refs_0_), channel_id=1, source_target_pairs={{0,24},{4,28},{8,0},{12,4},{16,8},{20,12},{24,16},{28,20},{1,25},{... | collective-permute-start | bytes 196616 | tf_op jit(solution)/shard_map/ppermute | solution.py:27
  11.8 0.7 %collective-permute-start.1 = (bf16[128,256]{1,0:T(8,128)(2,1)S(1)}, bf16[128,256]{1,0:T(8,128)(2,1)S(1)}, u32[]{:S(2)}, u32[]{:S(2)}) collective-permute-start(bf16[128,256]{1,0:T(8,128)(2,1)S(1)} %project.1.own_ref.refs_0_), channel_id=1, source_target_pairs={{0,8},{4,12},{8,16},{12,20},{16,24},{20,28},{24,0},{28,4},{1,9},{5... | collective-permute-start | bytes 196616 | tf_op jit(solution)/shard_map/ppermute | solution.py:27
  12.5 3.1 %collective-permute-start.4 = (bf16[128,256]{1,0:T(8,128)(2,1)S(1)}, bf16[128,256]{1,0:T(8,128)(2,1)S(1)}, u32[]{:S(2)}, u32[]{:S(2)}) collective-permute-start(bf16[128,256]{1,0:T(8,128)(2,1)S(1)} %collective-permute-done.refs_1_), channel_id=1, source_target_pairs={{0,24},{4,28},{8,0},{12,4},{16,8},{20,12},{24,16},{28,20},{1,25},{... | collective-permute-start | bytes 196616 | tf_op jit(solution)/shard_map/ppermute | solution.py:27
  15.7 1.6 %copy-done.2 = bf16[1024,1024]{1,0:T(8,128)(2,1)S(1)} copy-done((bf16[1024,1024]{1,0:T(8,128)(2,1)S(1)}, bf16[1024,1024]{1,0:T(8,128)(2,1)}, u32[]{:S(2)}) %copy-start.2) | copy-done | bytes 2097176
  17.3 3.3 %own_branch.2 = (bf16[1024,1024]{1,0:T(8,128)(2,1)}, f32[128,256]{1,0:T(8,128)S(1)}) custom-call(s32[1]{0:T(128)} %bitcast.info, s32[2]{0:T(128)S(1)} %copy-done.5, bf16[128,256]{1,0:T(8,128)(2,1)S(1)} %project.1.own_ref.refs_0_, bf16[1024,1024]{1,0:T(8,128)(2,1)S(1)} %copy-done.1, bf16[2048,128]{1,0:T(8,128)(2,1)S(1)} %bitcast.10, ...), custom_call_target="tpu_custom_call" | custom-call | flops 671088640 | bytes 1572864 | tf_op jit(solution)/shard_map/own_branch/pallas_call | solution.py:418
  20.6 1.1 %collective-permute-done.2.refs_3_ = bf16[128,256]{1,0:T(8,128)(2,1)S(1)} collective-permute-done((bf16[128,256]{1,0:T(8,128)(2,1)S(1)}, bf16[128,256]{1,0:T(8,128)(2,1)S(1)}, u32[]{:S(2)}, u32[]{:S(2)}) %collective-permute-start.2) | collective-permute-done | bytes 65568 | tf_op jit(solution)/shard_map/ppermute | solution.py:27
  21.7 5.7 %other_branches.1 = (bf16[1024,1024]{1,0:T(8,128)(2,1)}, f32[128,256]{1,0:T(8,128)S(1)}, bf16[128,256]{1,0:T(8,128)(2,1)S(1)}, bf16[1,144,256]{2,1,0:T(8,128)(2,1)S(1)}) custom-call(s32[1]{0:T(128)} %bitcast.info, s32[2]{0:T(128)S(1)} %copy-done.5, bf16[128,256]{1,0:T(8,128)(2,1)S(1)} %project.1.own_ref.refs_0_, ...), custom_call_target="tpu_custom_call", output_to_operand_aliasing={{0}: (12, {})} | custom-call | flops 1342177280 | bytes 3145728 | tf_op jit(solution)/shard_map/other_branches/pallas_call | solution.py:418
  27.5 1.5 %collective-permute-start.6 = (bf16[1,144,256]{2,1,0:T(8,128)(2,1)S(1)}, bf16[1,144,256]{2,1,0:T(8,128)(2,1)S(1)}, u32[]{:S(2)}, u32[]{:S(2)}) collective-permute-start(bf16[1,144,256]{2,1,0:T(8,128)(2,1)S(1)} %get-tuple-element.27.grad_ref), channel_id=1, source_target_pairs={{0,4},{4,0},{8,12},{12,8},{16,20},{20,16},{24,28},{28,24},{1,5},{5... | collective-permute-start | bytes 221192 | tf_op jit(solution)/shard_map/ppermute | solution.py:27
  29.2 3.3 %collective-permute-done.6.got_ref = bf16[1,144,256]{2,1,0:T(8,128)(2,1)S(1)} collective-permute-done((bf16[1,144,256]{2,1,0:T(8,128)(2,1)S(1)}, bf16[1,144,256]{2,1,0:T(8,128)(2,1)S(1)}, u32[]{:S(2)}, u32[]{:S(2)}) %collective-permute-start.6) | collective-permute-done | bytes 73760 | tf_op jit(solution)/shard_map/ppermute | solution.py:27
  32.5 0.6 %relay.1 = (bf16[128,256]{1,0:T(8,128)(2,1)S(1)}, bf16[128,256]{1,0:T(8,128)(2,1)S(1)}, f32[128,256]{1,0:T(8,128)S(1)}) custom-call(s32[1]{0:T(128)} %bitcast.info, s32[2]{0:T(128)S(1)} %copy-done.5, bf16[1,144,256]{2,1,0:T(8,128)(2,1)S(1)} %get-tuple-element.27.grad_ref, bf16[1,144,256]{2,1,0:T(8,128)(2,1)S(1)} %collective-permute-done.6.got_ref), custom_call_target="tpu_custom_call" | custom-call | tf_op jit(solution)/shard_map/relay/pallas_call | solution.py:354
  33.1 2.2 %collective-permute-start.8 = (bf16[128,256]{1,0:T(8,128)(2,1)S(1)}, bf16[128,256]{1,0:T(8,128)(2,1)S(1)}, u32[]{:S(2)}, u32[]{:S(2)}) collective-permute-start(bf16[128,256]{1,0:T(8,128)(2,1)S(1)} %get-tuple-element.30), channel_id=1, source_target_pairs={{0,24},{4,28},{8,0},{12,4},{16,8},{20,12},{24,16},{28,20},{1,25},{... | collective-permute-start | bytes 196616 | tf_op jit(solution)/shard_map/ppermute | solution.py:27
  35.3 1.6 %copy-done.3 = bf16[1024,1024]{1,0:T(8,128)(2,1)S(1)} copy-done((bf16[1024,1024]{1,0:T(8,128)(2,1)S(1)}, bf16[1024,1024]{1,0:T(8,128)(2,1)}, u32[]{:S(2)}) %copy-start.3) | copy-done | bytes 2097176
  36.9 3.3 %own_branch.3 = (bf16[1024,1024]{1,0:T(8,128)(2,1)}, f32[128,256]{1,0:T(8,128)S(1)}) custom-call(s32[1]{0:T(128)} %bitcast.info, s32[2]{0:T(128)S(1)} %copy-done.5, bf16[128,256]{1,0:T(8,128)(2,1)S(1)} %project.1.own_ref.refs_0_, bf16[1024,1024]{1,0:T(8,128)(2,1)S(1)} %copy-done.1, bf16[2048,128]{1,0:T(8,128)(2,1)S(1)} %bitcast.12, ...), custom_call_target="tpu_custom_call", output_to_operand_aliasing={{0}: (6, {})} | custom-call | flops 671088640 | bytes 1572864 | tf_op jit(solution)/shard_map/own_branch/pallas_call | solution.py:418
  40.2 1.1 %collective-permute-done.9.refs_6_ = bf16[128,256]{1,0:T(8,128)(2,1)S(1)} collective-permute-done((bf16[128,256]{1,0:T(8,128)(2,1)S(1)}, bf16[128,256]{1,0:T(8,128)(2,1)S(1)}, u32[]{:S(2)}, u32[]{:S(2)}) %collective-permute-start.9) | collective-permute-done | bytes 65568 | tf_op jit(solution)/shard_map/ppermute | solution.py:27
  41.3 1.3 %back_shares.3 = (bf16[32,4096]{1,0:T(8,128)(2,1)S(1)}, bf16[32,4096]{1,0:T(8,128)(2,1)S(1)}, bf16[32,4096]{1,0:T(8,128)(2,1)S(1)}, bf16[32,4096]{1,0:T(8,128)(2,1)S(1)}) custom-call(s32[1]{0:T(128)} %bitcast.4.index, f32[128,256]{1,0:T(8,128)S(1)} %get-tuple-element.24.refs_0_, f32[128,256]{1,0:T(8,128)S(1)} %get-tuple-element.25.refs_1_, ...), custom_call_target="tpu_custom_call" | custom-call | flops 268435456 | bytes 3145728 | tf_op jit(solution)/shard_map/back_shares/pallas_call | solution.py:165
  43.2 1.3 %back_shares.2 = (bf16[32,4096]{1,0:T(8,128)(2,1)S(1)}, bf16[32,4096]{1,0:T(8,128)(2,1)S(1)}, bf16[32,4096]{1,0:T(8,128)(2,1)S(1)}, bf16[32,4096]{1,0:T(8,128)(2,1)S(1)}) custom-call(s32[1]{0:T(128)} %bitcast.4.index, f32[128,256]{1,0:T(8,128)S(1)} %get-tuple-element.24.refs_0_, f32[128,256]{1,0:T(8,128)S(1)} %get-tuple-element.25.refs_1_, ...), custom_call_target="tpu_custom_call" | custom-call | flops 268435456 | bytes 3145728 | tf_op jit(solution)/shard_map/back_shares/pallas_call | solution.py:165
  45.2 1.6 %collective-permute-start.15 = (bf16[32,4096]{1,0:T(8,128)(2,1)S(1)}, bf16[32,4096]{1,0:T(8,128)(2,1)S(1)}, u32[]{:S(2)}, u32[]{:S(2)}) collective-permute-start(bf16[32,4096]{1,0:T(8,128)(2,1)S(1)} %add_convert_fusion.1), channel_id=1, source_target_pairs={{0,2},{1,3},{2,0},{3,1},{4,6},{5,7},{6,4},{7,5},{8,10},{9,11},{10,... | collective-permute-start | bytes 786440 | tf_op jit(solution)/shard_map/ppermute | solution.py:492
  47.0 1.2 %collective-permute-start.12 = (bf16[32,4096]{1,0:T(8,128)(2,1)S(1)}, bf16[32,4096]{1,0:T(8,128)(2,1)S(1)}, u32[]{:S(2)}, u32[]{:S(2)}) collective-permute-start(bf16[32,4096]{1,0:T(8,128)(2,1)S(1)} %add_convert_fusion.4), channel_id=1, source_target_pairs={{0,2},{1,3},{2,0},{3,1},{4,6},{5,7},{6,4},{7,5},{8,10},{9,11},{10,... | collective-permute-start | bytes 786440 | tf_op jit(solution)/shard_map/ppermute | solution.py:492
  48.2 6.3 %collective-permute-done.15 = bf16[32,4096]{1,0:T(8,128)(2,1)S(1)} collective-permute-done((bf16[32,4096]{1,0:T(8,128)(2,1)S(1)}, bf16[32,4096]{1,0:T(8,128)(2,1)S(1)}, u32[]{:S(2)}, u32[]{:S(2)}) %collective-permute-start.15) | collective-permute-done | bytes 262176 | tf_op jit(solution)/shard_map/ppermute | solution.py:492
  54.5 4.7 %collective-permute-done.12 = bf16[32,4096]{1,0:T(8,128)(2,1)S(1)} collective-permute-done((bf16[32,4096]{1,0:T(8,128)(2,1)S(1)}, bf16[32,4096]{1,0:T(8,128)(2,1)S(1)}, u32[]{:S(2)}, u32[]{:S(2)}) %collective-permute-start.12) | collective-permute-done | bytes 262176 | tf_op jit(solution)/shard_map/ppermute | solution.py:492
  59.2 0.8 %maximum_bitcast_fusion = bf16[1,32,8192]{2,1,0:T(8,128)(2,1)} fusion(bf16[32,4096]{1,0:T(8,128)(2,1)S(1)} %add_convert_fusion, bf16[32,4096]{1,0:T(8,128)(2,1)S(1)} %add_convert_fusion.3), kind=kLoop, calls=%fused_computation | loop fusion | flops 1048576 | bytes 1048576 | tf_op jit(solution)/shard_map/reshape | solution.py:482
  (34 shorter events, 1.8 us)
Async XLA Ops:
  0.6 15.0 %copy-start.1 = (bf16[1024,1024]{1,0:T(8,128)(2,1)S(1)}, bf16[1024,1024]{1,0:T(8,128)(2,1)}, u32[]{:S(2)}) copy-start(bf16[1024,1024]{1,0:T(8,128)(2,1)} %q_ref.3) | copy-start | bytes 6291460
  0.6 15.0 %copy-start.4 = (bf16[1024,2,128]{2,1,0:T(2,128)(2,1)S(1)}, bf16[1024,2,128]{2,1,0:T(2,128)(2,1)}, u32[]{:S(2)}) copy-start(bf16[1024,2,128]{2,1,0:T(2,128)(2,1)} %param.9) | copy-start | bytes 1572868
  0.7 15.0 %copy-start.5 = (s32[2]{0:T(128)S(1)}, s32[2]{0:T(128)}, u32[]{:S(2)}) copy-start(s32[2]{0:T(128)} %prompts.7) | copy-start | bytes 28
  4.9 7.6 %collective-permute-start = (bf16[128,256]{1,0:T(8,128)(2,1)S(1)}, bf16[128,256]{1,0:T(8,128)(2,1)S(1)}, u32[]{:S(2)}, u32[]{:S(2)}) collective-permute-start(bf16[128,256]{1,0:T(8,128)(2,1)S(1)} %project.1.own_ref.refs_0_), channel_id=1, source_target_pairs={{0,4},{4,0},{8,12},{12,8},{16,20},{20,16},{24,28},{28,24},{1,5},{5... | collective-permute-start | bytes 196616 | tf_op jit(solution)/shard_map/ppermute | solution.py:27
  7.9 12.7 %collective-permute-start.5 = (bf16[128,256]{1,0:T(8,128)(2,1)S(1)}, bf16[128,256]{1,0:T(8,128)(2,1)S(1)}, u32[]{:S(2)}, u32[]{:S(2)}) collective-permute-start(bf16[128,256]{1,0:T(8,128)(2,1)S(1)} %project.1.own_ref.refs_0_), channel_id=1, source_target_pairs={{0,20},{4,16},{8,28},{12,24},{16,4},{20,0},{24,12},{28,8},{1,21},{... | collective-permute-start | bytes 196616 | tf_op jit(solution)/shard_map/ppermute | solution.py:27
  10.5 10.1 %collective-permute-start.3 = (bf16[128,256]{1,0:T(8,128)(2,1)S(1)}, bf16[128,256]{1,0:T(8,128)(2,1)S(1)}, u32[]{:S(2)}, u32[]{:S(2)}) collective-permute-start(bf16[128,256]{1,0:T(8,128)(2,1)S(1)} %project.1.own_ref.refs_0_), channel_id=1, source_target_pairs={{0,24},{4,28},{8,0},{12,4},{16,8},{20,12},{24,16},{28,20},{1,25},{... | collective-permute-start | bytes 196616 | tf_op jit(solution)/shard_map/ppermute | solution.py:27
  11.8 8.8 %collective-permute-start.1 = (bf16[128,256]{1,0:T(8,128)(2,1)S(1)}, bf16[128,256]{1,0:T(8,128)(2,1)S(1)}, u32[]{:S(2)}, u32[]{:S(2)}) collective-permute-start(bf16[128,256]{1,0:T(8,128)(2,1)S(1)} %project.1.own_ref.refs_0_), channel_id=1, source_target_pairs={{0,8},{4,12},{8,16},{12,20},{16,24},{20,28},{24,0},{28,4},{1,9},{5... | collective-permute-start | bytes 196616 | tf_op jit(solution)/shard_map/ppermute | solution.py:27
  12.5 8.1 %collective-permute-start.4 = (bf16[128,256]{1,0:T(8,128)(2,1)S(1)}, bf16[128,256]{1,0:T(8,128)(2,1)S(1)}, u32[]{:S(2)}, u32[]{:S(2)}) collective-permute-start(bf16[128,256]{1,0:T(8,128)(2,1)S(1)} %collective-permute-done.refs_1_), channel_id=1, source_target_pairs={{0,24},{4,28},{8,0},{12,4},{16,8},{20,12},{24,16},{28,20},{1,25},{... | collective-permute-start | bytes 196616 | tf_op jit(solution)/shard_map/ppermute | solution.py:27
  15.7 6.1 %collective-permute-start.2 = (bf16[128,256]{1,0:T(8,128)(2,1)S(1)}, bf16[128,256]{1,0:T(8,128)(2,1)S(1)}, u32[]{:S(2)}, u32[]{:S(2)}) collective-permute-start(bf16[128,256]{1,0:T(8,128)(2,1)S(1)} %collective-permute-done.refs_1_), channel_id=1, source_target_pairs={{0,8},{4,12},{8,16},{12,20},{16,24},{20,28},{24,0},{28,4},{1,9},{5... | collective-permute-start | bytes 196616 | tf_op jit(solution)/shard_map/ppermute | solution.py:27
  15.7 1.6 %copy-start.2 = (bf16[1024,1024]{1,0:T(8,128)(2,1)S(1)}, bf16[1024,1024]{1,0:T(8,128)(2,1)}, u32[]{:S(2)}) copy-start(bf16[1024,1024]{1,0:T(8,128)(2,1)} %up_ref.3) | copy-start | bytes 6291460
  27.5 5.0 %collective-permute-start.6 = (bf16[1,144,256]{2,1,0:T(8,128)(2,1)S(1)}, bf16[1,144,256]{2,1,0:T(8,128)(2,1)S(1)}, u32[]{:S(2)}, u32[]{:S(2)}) collective-permute-start(bf16[1,144,256]{2,1,0:T(8,128)(2,1)S(1)} %get-tuple-element.27.grad_ref), channel_id=1, source_target_pairs={{0,4},{4,0},{8,12},{12,8},{16,20},{20,16},{24,28},{28,24},{1,5},{5... | collective-permute-start | bytes 221192 | tf_op jit(solution)/shard_map/ppermute | solution.py:27
  29.0 11.2 %collective-permute-start.7 = (bf16[128,256]{1,0:T(8,128)(2,1)S(1)}, bf16[128,256]{1,0:T(8,128)(2,1)S(1)}, u32[]{:S(2)}, u32[]{:S(2)}) collective-permute-start(bf16[128,256]{1,0:T(8,128)(2,1)S(1)} %get-tuple-element.29), channel_id=1, source_target_pairs={{0,20},{4,16},{8,28},{12,24},{16,4},{20,0},{24,12},{28,8},{1,21},{... | collective-permute-start | bytes 196616 | tf_op jit(solution)/shard_map/ppermute | solution.py:27
  33.1 7.1 %collective-permute-start.8 = (bf16[128,256]{1,0:T(8,128)(2,1)S(1)}, bf16[128,256]{1,0:T(8,128)(2,1)S(1)}, u32[]{:S(2)}, u32[]{:S(2)}) collective-permute-start(bf16[128,256]{1,0:T(8,128)(2,1)S(1)} %get-tuple-element.30), channel_id=1, source_target_pairs={{0,24},{4,28},{8,0},{12,4},{16,8},{20,12},{24,16},{28,20},{1,25},{... | collective-permute-start | bytes 196616 | tf_op jit(solution)/shard_map/ppermute | solution.py:27
  35.3 6.1 %collective-permute-start.9 = (bf16[128,256]{1,0:T(8,128)(2,1)S(1)}, bf16[128,256]{1,0:T(8,128)(2,1)S(1)}, u32[]{:S(2)}, u32[]{:S(2)}) collective-permute-start(bf16[128,256]{1,0:T(8,128)(2,1)S(1)} %get-tuple-element.31), channel_id=1, source_target_pairs={{0,8},{4,12},{8,16},{12,20},{16,24},{20,28},{24,0},{28,4},{1,9},{5... | collective-permute-start | bytes 196616 | tf_op jit(solution)/shard_map/ppermute | solution.py:27
  35.3 1.6 %copy-start.3 = (bf16[1024,1024]{1,0:T(8,128)(2,1)S(1)}, bf16[1024,1024]{1,0:T(8,128)(2,1)}, u32[]{:S(2)}) copy-start(bf16[1024,1024]{1,0:T(8,128)(2,1)} %up_ref.3) | copy-start | bytes 6291460
  36.9 4.5 %copy-start = (bf16[8192,2,128]{2,1,0:T(2,128)(2,1)S(1)}, bf16[8192,2,128]{2,1,0:T(2,128)(2,1)}, u32[]{:S(2)}) copy-start(bf16[8192,2,128]{2,1,0:T(2,128)(2,1)} %param.7) | copy-start | bytes 12582916
  42.6 2.5 %collective-permute-start.14 = (bf16[32,4096]{1,0:T(8,128)(2,1)S(1)}, bf16[32,4096]{1,0:T(8,128)(2,1)S(1)}, u32[]{:S(2)}, u32[]{:S(2)}) collective-permute-start(bf16[32,4096]{1,0:T(8,128)(2,1)S(1)} %get-tuple-element.39), channel_id=1, source_target_pairs={{0,1},{1,0},{2,3},{3,2},{4,5},{5,4},{6,7},{7,6},{8,9},{9,8},{10,11... | collective-permute-start | bytes 786440 | tf_op jit(solution)/shard_map/ppermute | solution.py:492
  42.7 4.0 %collective-permute-start.13 = (bf16[32,4096]{1,0:T(8,128)(2,1)S(1)}, bf16[32,4096]{1,0:T(8,128)(2,1)S(1)}, u32[]{:S(2)}, u32[]{:S(2)}) collective-permute-start(bf16[32,4096]{1,0:T(8,128)(2,1)S(1)} %get-tuple-element.37), channel_id=1, source_target_pairs={{0,1},{1,0},{2,3},{3,2},{4,5},{5,4},{6,7},{7,6},{8,9},{9,8},{10,11... | collective-permute-start | bytes 786440 | tf_op jit(solution)/shard_map/ppermute | solution.py:492
  44.5 2.3 %collective-permute-start.10 = (bf16[32,4096]{1,0:T(8,128)(2,1)S(1)}, bf16[32,4096]{1,0:T(8,128)(2,1)S(1)}, u32[]{:S(2)}, u32[]{:S(2)}) collective-permute-start(bf16[32,4096]{1,0:T(8,128)(2,1)S(1)} %get-tuple-element.33), channel_id=1, source_target_pairs={{0,1},{1,0},{2,3},{3,2},{4,5},{5,4},{6,7},{7,6},{8,9},{9,8},{10,11... | collective-permute-start | bytes 786440 | tf_op jit(solution)/shard_map/ppermute | solution.py:492
  44.7 2.2 %collective-permute-start.11 = (bf16[32,4096]{1,0:T(8,128)(2,1)S(1)}, bf16[32,4096]{1,0:T(8,128)(2,1)S(1)}, u32[]{:S(2)}, u32[]{:S(2)}) collective-permute-start(bf16[32,4096]{1,0:T(8,128)(2,1)S(1)} %get-tuple-element.35), channel_id=1, source_target_pairs={{0,1},{1,0},{2,3},{3,2},{4,5},{5,4},{6,7},{7,6},{8,9},{9,8},{10,11... | collective-permute-start | bytes 786440 | tf_op jit(solution)/shard_map/ppermute | solution.py:492
  45.2 9.2 %collective-permute-start.15 = (bf16[32,4096]{1,0:T(8,128)(2,1)S(1)}, bf16[32,4096]{1,0:T(8,128)(2,1)S(1)}, u32[]{:S(2)}, u32[]{:S(2)}) collective-permute-start(bf16[32,4096]{1,0:T(8,128)(2,1)S(1)} %add_convert_fusion.1), channel_id=1, source_target_pairs={{0,2},{1,3},{2,0},{3,1},{4,6},{5,7},{6,4},{7,5},{8,10},{9,11},{10,... | collective-permute-start | bytes 786440 | tf_op jit(solution)/shard_map/ppermute | solution.py:492
  47.0 12.2 %collective-permute-start.12 = (bf16[32,4096]{1,0:T(8,128)(2,1)S(1)}, bf16[32,4096]{1,0:T(8,128)(2,1)S(1)}, u32[]{:S(2)}, u32[]{:S(2)}) collective-permute-start(bf16[32,4096]{1,0:T(8,128)(2,1)S(1)} %add_convert_fusion.4), channel_id=1, source_target_pairs={{0,2},{1,3},{2,0},{3,1},{4,6},{5,7},{6,4},{7,5},{8,10},{9,11},{10,... | collective-permute-start | bytes 786440 | tf_op jit(solution)/shard_map/ppermute | solution.py:492

commit v6 on v5

--- a/solution.py
+++ b/solution.py
@@ -15,6 +15,7 @@
 TALL = 4
 TILE = 32
 CHUNKS = 8
+BACK_CHUNKS = 2
 VMEM = 24 << 20
 PARTS = 2
 PROJECT_VMEM = 54500000
@@ -169,8 +170,8 @@
         out_specs=[here] * 4,
         out_shape=[jax.ShapeDtypeStruct((rows, model_width // PARTS), jnp.bfloat16)] * 4,
         scratch_shapes=[
-            pltpu.VMEM((2, 2 * model_width // CHUNKS, HD), jnp.float32),
-            pltpu.VMEM((2, model_width // CHUNKS, 2 * HD), jnp.bfloat16),
+            pltpu.VMEM((2, 2 * model_width // BACK_CHUNKS, HD), jnp.float32),
+            pltpu.VMEM((2, model_width // BACK_CHUNKS, 2 * HD), jnp.bfloat16),
         ],
         compiler_params=pltpu.CompilerParams(vmem_limit_bytes=VMEM),
         cost_estimate=pl.CostEstimate(

time: 60.2 us -> 59.9 us (level)
  no operation moved by 1% of the time
where the time goes in v6:
time: 59.9 us; the launch traced here: 59.7 us
  Pallas kernels  19.5 us (33%)
  starting transfers between devices  18.5 us (31%)
  waiting for transfers between devices  16.5 us (28%)
  local copies, waits for them, and re-layouts  3.19 us (5%)
  other arithmetic  1.23 us (2%)
  between operations  0.78 us (1%)
    ppermute x10, starting transfers between devices, dp_permute(): lax.ppermute(x, 'dp', [(i, target(i) % devices) for i in range(devices)])  14.7 us
    pallas_call x3, Pallas kernels, attention(): pl.pallas_call(body, grid_spec=pltpu.PrefetchScalarGridSpec(num_scalar_pr...  12.4 us
    ppermute x6, waiting for transfers between devices, swap(): return lax.ppermute(x, 'tensor', [(i, i ^ bit) for i in range(count)])  10.9 us
    ppermute x10, waiting for transfers between devices, dp_permute(): lax.ppermute(x, 'dp', [(i, target(i) % devices) for i in range(devices)])  5.57 us
    pallas_call x1, Pallas kernels, project(): pl.pallas_call(project_kernel, in_specs=[there] * 2, out_specs=pl.BlockSp...  4.22 us
    ppermute x6, starting transfers between devices, swap(): return lax.ppermute(x, 'tensor', [(i, i ^ bit) for i in range(count)])  3.89 us
    unnamed x12, local copies, waits for them, and re-layouts  3.19 us
    pallas_call x2, Pallas kernels, back_shares(): pl.pallas_call(functools.partial(back_kernel, part), in_specs=[pl.BlockSp...  2.26 us
  transfers between devices with their start and end apart: 16, of which 5 were waited for; matrix products, arithmetic and copies ran while one was open for 1% of the time, Pallas kernels for 14%

profile of v6, /device:TPU:0, one launch (start us, length us, event | category | flops | bytes accessed | tf_op | source)
XLA Modules:
  0.0 59.7 jit_solution(9907637864972262364)
XLA Ops:
  0.7 4.2 %project.1.own_ref.refs_0_ = bf16[128,256]{1,0:T(8,128)(2,1)S(1)} custom-call(bf16[128,8192]{1,0:T(8,128)(2,1)} %bitcast.13, bf16[16384,128]{1,0:T(8,128)(2,1)} %bitcast.7), custom_call_target="tpu_custom_call" | custom-call | flops 536870912 | bytes 6291456 | tf_op jit(solution)/shard_map/project/pallas_call | solution.py:110
  4.9 3.0 %collective-permute-start = (bf16[128,256]{1,0:T(8,128)(2,1)S(1)}, bf16[128,256]{1,0:T(8,128)(2,1)S(1)}, u32[]{:S(2)}, u32[]{:S(2)}) collective-permute-start(bf16[128,256]{1,0:T(8,128)(2,1)S(1)} %project.1.own_ref.refs_0_), channel_id=1, source_target_pairs={{0,4},{4,0},{8,12},{12,8},{16,20},{20,16},{24,28},{28,24},{1,5},{5... | collective-permute-start | bytes 196616 | tf_op jit(solution)/shard_map/ppermute | solution.py:28
  7.9 2.6 %collective-permute-start.5 = (bf16[128,256]{1,0:T(8,128)(2,1)S(1)}, bf16[128,256]{1,0:T(8,128)(2,1)S(1)}, u32[]{:S(2)}, u32[]{:S(2)}) collective-permute-start(bf16[128,256]{1,0:T(8,128)(2,1)S(1)} %project.1.own_ref.refs_0_), channel_id=1, source_target_pairs={{0,20},{4,16},{8,28},{12,24},{16,4},{20,0},{24,12},{28,8},{1,21},{... | collective-permute-start | bytes 196616 | tf_op jit(solution)/shard_map/ppermute | solution.py:28
  10.5 1.4 %collective-permute-start.3 = (bf16[128,256]{1,0:T(8,128)(2,1)S(1)}, bf16[128,256]{1,0:T(8,128)(2,1)S(1)}, u32[]{:S(2)}, u32[]{:S(2)}) collective-permute-start(bf16[128,256]{1,0:T(8,128)(2,1)S(1)} %project.1.own_ref.refs_0_), channel_id=1, source_target_pairs={{0,24},{4,28},{8,0},{12,4},{16,8},{20,12},{24,16},{28,20},{1,25},{... | collective-permute-start | bytes 196616 | tf_op jit(solution)/shard_map/ppermute | solution.py:28
  11.8 0.7 %collective-permute-start.1 = (bf16[128,256]{1,0:T(8,128)(2,1)S(1)}, bf16[128,256]{1,0:T(8,128)(2,1)S(1)}, u32[]{:S(2)}, u32[]{:S(2)}) collective-permute-start(bf16[128,256]{1,0:T(8,128)(2,1)S(1)} %project.1.own_ref.refs_0_), channel_id=1, source_target_pairs={{0,8},{4,12},{8,16},{12,20},{16,24},{20,28},{24,0},{28,4},{1,9},{5... | collective-permute-start | bytes 196616 | tf_op jit(solution)/shard_map/ppermute | solution.py:28
  12.5 3.1 %collective-permute-start.4 = (bf16[128,256]{1,0:T(8,128)(2,1)S(1)}, bf16[128,256]{1,0:T(8,128)(2,1)S(1)}, u32[]{:S(2)}, u32[]{:S(2)}) collective-permute-start(bf16[128,256]{1,0:T(8,128)(2,1)S(1)} %collective-permute-done.refs_1_), channel_id=1, source_target_pairs={{0,24},{4,28},{8,0},{12,4},{16,8},{20,12},{24,16},{28,20},{1,25},{... | collective-permute-start | bytes 196616 | tf_op jit(solution)/shard_map/ppermute | solution.py:28
  15.7 1.6 %copy-done.2 = bf16[1024,1024]{1,0:T(8,128)(2,1)S(1)} copy-done((bf16[1024,1024]{1,0:T(8,128)(2,1)S(1)}, bf16[1024,1024]{1,0:T(8,128)(2,1)}, u32[]{:S(2)}) %copy-start.2) | copy-done | bytes 2097176
  17.3 3.3 %own_branch.2 = (bf16[1024,1024]{1,0:T(8,128)(2,1)}, f32[128,256]{1,0:T(8,128)S(1)}) custom-call(s32[1]{0:T(128)} %bitcast.info, s32[2]{0:T(128)S(1)} %copy-done.5, bf16[128,256]{1,0:T(8,128)(2,1)S(1)} %project.1.own_ref.refs_0_, bf16[1024,1024]{1,0:T(8,128)(2,1)S(1)} %copy-done.1, bf16[2048,128]{1,0:T(8,128)(2,1)S(1)} %bitcast.10, ...), custom_call_target="tpu_custom_call" | custom-call | flops 671088640 | bytes 1572864 | tf_op jit(solution)/shard_map/own_branch/pallas_call | solution.py:419
  20.6 1.1 %collective-permute-done.2.refs_3_ = bf16[128,256]{1,0:T(8,128)(2,1)S(1)} collective-permute-done((bf16[128,256]{1,0:T(8,128)(2,1)S(1)}, bf16[128,256]{1,0:T(8,128)(2,1)S(1)}, u32[]{:S(2)}, u32[]{:S(2)}) %collective-permute-start.2) | collective-permute-done | bytes 65568 | tf_op jit(solution)/shard_map/ppermute | solution.py:28
  21.7 5.7 %other_branches.1 = (bf16[1024,1024]{1,0:T(8,128)(2,1)}, f32[128,256]{1,0:T(8,128)S(1)}, bf16[128,256]{1,0:T(8,128)(2,1)S(1)}, bf16[1,144,256]{2,1,0:T(8,128)(2,1)S(1)}) custom-call(s32[1]{0:T(128)} %bitcast.info, s32[2]{0:T(128)S(1)} %copy-done.5, bf16[128,256]{1,0:T(8,128)(2,1)S(1)} %project.1.own_ref.refs_0_, ...), custom_call_target="tpu_custom_call", output_to_operand_aliasing={{0}: (12, {})} | custom-call | flops 1342177280 | bytes 3145728 | tf_op jit(solution)/shard_map/other_branches/pallas_call | solution.py:419
  27.5 1.5 %collective-permute-start.6 = (bf16[1,144,256]{2,1,0:T(8,128)(2,1)S(1)}, bf16[1,144,256]{2,1,0:T(8,128)(2,1)S(1)}, u32[]{:S(2)}, u32[]{:S(2)}) collective-permute-start(bf16[1,144,256]{2,1,0:T(8,128)(2,1)S(1)} %get-tuple-element.27.grad_ref), channel_id=1, source_target_pairs={{0,4},{4,0},{8,12},{12,8},{16,20},{20,16},{24,28},{28,24},{1,5},{5... | collective-permute-start | bytes 221192 | tf_op jit(solution)/shard_map/ppermute | solution.py:28
  29.2 3.3 %collective-permute-done.6.got_ref = bf16[1,144,256]{2,1,0:T(8,128)(2,1)S(1)} collective-permute-done((bf16[1,144,256]{2,1,0:T(8,128)(2,1)S(1)}, bf16[1,144,256]{2,1,0:T(8,128)(2,1)S(1)}, u32[]{:S(2)}, u32[]{:S(2)}) %collective-permute-start.6) | collective-permute-done | bytes 73760 | tf_op jit(solution)/shard_map/ppermute | solution.py:28
  32.5 0.6 %relay.1 = (bf16[128,256]{1,0:T(8,128)(2,1)S(1)}, bf16[128,256]{1,0:T(8,128)(2,1)S(1)}, f32[128,256]{1,0:T(8,128)S(1)}) custom-call(s32[1]{0:T(128)} %bitcast.info, s32[2]{0:T(128)S(1)} %copy-done.5, bf16[1,144,256]{2,1,0:T(8,128)(2,1)S(1)} %get-tuple-element.27.grad_ref, bf16[1,144,256]{2,1,0:T(8,128)(2,1)S(1)} %collective-permute-done.6.got_ref), custom_call_target="tpu_custom_call" | custom-call | tf_op jit(solution)/shard_map/relay/pallas_call | solution.py:355
  33.1 2.2 %collective-permute-start.8 = (bf16[128,256]{1,0:T(8,128)(2,1)S(1)}, bf16[128,256]{1,0:T(8,128)(2,1)S(1)}, u32[]{:S(2)}, u32[]{:S(2)}) collective-permute-start(bf16[128,256]{1,0:T(8,128)(2,1)S(1)} %get-tuple-element.30), channel_id=1, source_target_pairs={{0,24},{4,28},{8,0},{12,4},{16,8},{20,12},{24,16},{28,20},{1,25},{... | collective-permute-start | bytes 196616 | tf_op jit(solution)/shard_map/ppermute | solution.py:28
  35.3 1.6 %copy-done.3 = bf16[1024,1024]{1,0:T(8,128)(2,1)S(1)} copy-done((bf16[1024,1024]{1,0:T(8,128)(2,1)S(1)}, bf16[1024,1024]{1,0:T(8,128)(2,1)}, u32[]{:S(2)}) %copy-start.3) | copy-done | bytes 2097176
  36.9 3.3 %own_branch.3 = (bf16[1024,1024]{1,0:T(8,128)(2,1)}, f32[128,256]{1,0:T(8,128)S(1)}) custom-call(s32[1]{0:T(128)} %bitcast.info, s32[2]{0:T(128)S(1)} %copy-done.5, bf16[128,256]{1,0:T(8,128)(2,1)S(1)} %project.1.own_ref.refs_0_, bf16[1024,1024]{1,0:T(8,128)(2,1)S(1)} %copy-done.1, bf16[2048,128]{1,0:T(8,128)(2,1)S(1)} %bitcast.12, ...), custom_call_target="tpu_custom_call", output_to_operand_aliasing={{0}: (6, {})} | custom-call | flops 671088640 | bytes 1572864 | tf_op jit(solution)/shard_map/own_branch/pallas_call | solution.py:419
  40.2 1.1 %collective-permute-done.9.refs_6_ = bf16[128,256]{1,0:T(8,128)(2,1)S(1)} collective-permute-done((bf16[128,256]{1,0:T(8,128)(2,1)S(1)}, bf16[128,256]{1,0:T(8,128)(2,1)S(1)}, u32[]{:S(2)}, u32[]{:S(2)}) %collective-permute-start.9) | collective-permute-done | bytes 65568 | tf_op jit(solution)/shard_map/ppermute | solution.py:28
  41.3 1.1 %back_shares.3 = (bf16[32,4096]{1,0:T(8,128)(2,1)S(1)}, bf16[32,4096]{1,0:T(8,128)(2,1)S(1)}, bf16[32,4096]{1,0:T(8,128)(2,1)S(1)}, bf16[32,4096]{1,0:T(8,128)(2,1)S(1)}) custom-call(s32[1]{0:T(128)} %bitcast.4.index, f32[128,256]{1,0:T(8,128)S(1)} %get-tuple-element.24.refs_0_, f32[128,256]{1,0:T(8,128)S(1)} %get-tuple-element.25.refs_1_, ...), custom_call_target="tpu_custom_call" | custom-call | flops 268435456 | bytes 3145728 | tf_op jit(solution)/shard_map/back_shares/pallas_call | solution.py:166
  43.1 1.1 %back_shares.2 = (bf16[32,4096]{1,0:T(8,128)(2,1)S(1)}, bf16[32,4096]{1,0:T(8,128)(2,1)S(1)}, bf16[32,4096]{1,0:T(8,128)(2,1)S(1)}, bf16[32,4096]{1,0:T(8,128)(2,1)S(1)}) custom-call(s32[1]{0:T(128)} %bitcast.4.index, f32[128,256]{1,0:T(8,128)S(1)} %get-tuple-element.24.refs_0_, f32[128,256]{1,0:T(8,128)S(1)} %get-tuple-element.25.refs_1_, ...), custom_call_target="tpu_custom_call" | custom-call | flops 268435456 | bytes 3145728 | tf_op jit(solution)/shard_map/back_shares/pallas_call | solution.py:166
  44.8 1.6 %collective-permute-start.15 = (bf16[32,4096]{1,0:T(8,128)(2,1)S(1)}, bf16[32,4096]{1,0:T(8,128)(2,1)S(1)}, u32[]{:S(2)}, u32[]{:S(2)}) collective-permute-start(bf16[32,4096]{1,0:T(8,128)(2,1)S(1)} %add_convert_fusion.1), channel_id=1, source_target_pairs={{0,2},{1,3},{2,0},{3,1},{4,6},{5,7},{6,4},{7,5},{8,10},{9,11},{10,... | collective-permute-start | bytes 786440 | tf_op jit(solution)/shard_map/ppermute | solution.py:493
  46.7 1.2 %collective-permute-start.12 = (bf16[32,4096]{1,0:T(8,128)(2,1)S(1)}, bf16[32,4096]{1,0:T(8,128)(2,1)S(1)}, u32[]{:S(2)}, u32[]{:S(2)}) collective-permute-start(bf16[32,4096]{1,0:T(8,128)(2,1)S(1)} %add_convert_fusion.4), channel_id=1, source_target_pairs={{0,2},{1,3},{2,0},{3,1},{4,6},{5,7},{6,4},{7,5},{8,10},{9,11},{10,... | collective-permute-start | bytes 786440 | tf_op jit(solution)/shard_map/ppermute | solution.py:493
  47.8 6.3 %collective-permute-done.15 = bf16[32,4096]{1,0:T(8,128)(2,1)S(1)} collective-permute-done((bf16[32,4096]{1,0:T(8,128)(2,1)S(1)}, bf16[32,4096]{1,0:T(8,128)(2,1)S(1)}, u32[]{:S(2)}, u32[]{:S(2)}) %collective-permute-start.15) | collective-permute-done | bytes 262176 | tf_op jit(solution)/shard_map/ppermute | solution.py:493
  54.2 4.7 %collective-permute-done.12 = bf16[32,4096]{1,0:T(8,128)(2,1)S(1)} collective-permute-done((bf16[32,4096]{1,0:T(8,128)(2,1)S(1)}, bf16[32,4096]{1,0:T(8,128)(2,1)S(1)}, u32[]{:S(2)}, u32[]{:S(2)}) %collective-permute-start.12) | collective-permute-done | bytes 262176 | tf_op jit(solution)/shard_map/ppermute | solution.py:493
  58.9 0.8 %maximum_bitcast_fusion = bf16[1,32,8192]{2,1,0:T(8,128)(2,1)} fusion(bf16[32,4096]{1,0:T(8,128)(2,1)S(1)} %add_convert_fusion, bf16[32,4096]{1,0:T(8,128)(2,1)S(1)} %add_convert_fusion.3), kind=kLoop, calls=%fused_computation | loop fusion | flops 1048576 | bytes 1048576 | tf_op jit(solution)/shard_map/reshape | solution.py:483
  (34 shorter events, 1.8 us)
Async XLA Ops:
  0.6 15.0 %copy-start.1 = (bf16[1024,1024]{1,0:T(8,128)(2,1)S(1)}, bf16[1024,1024]{1,0:T(8,128)(2,1)}, u32[]{:S(2)}) copy-start(bf16[1024,1024]{1,0:T(8,128)(2,1)} %q_ref.3) | copy-start | bytes 6291460
  0.6 15.0 %copy-start.4 = (bf16[1024,2,128]{2,1,0:T(2,128)(2,1)S(1)}, bf16[1024,2,128]{2,1,0:T(2,128)(2,1)}, u32[]{:S(2)}) copy-start(bf16[1024,2,128]{2,1,0:T(2,128)(2,1)} %param.9) | copy-start | bytes 1572868
  0.7 15.0 %copy-start.5 = (s32[2]{0:T(128)S(1)}, s32[2]{0:T(128)}, u32[]{:S(2)}) copy-start(s32[2]{0:T(128)} %prompts.7) | copy-start | bytes 28
  4.9 7.6 %collective-permute-start = (bf16[128,256]{1,0:T(8,128)(2,1)S(1)}, bf16[128,256]{1,0:T(8,128)(2,1)S(1)}, u32[]{:S(2)}, u32[]{:S(2)}) collective-permute-start(bf16[128,256]{1,0:T(8,128)(2,1)S(1)} %project.1.own_ref.refs_0_), channel_id=1, source_target_pairs={{0,4},{4,0},{8,12},{12,8},{16,20},{20,16},{24,28},{28,24},{1,5},{5... | collective-permute-start | bytes 196616 | tf_op jit(solution)/shard_map/ppermute | solution.py:28
  7.9 12.7 %collective-permute-start.5 = (bf16[128,256]{1,0:T(8,128)(2,1)S(1)}, bf16[128,256]{1,0:T(8,128)(2,1)S(1)}, u32[]{:S(2)}, u32[]{:S(2)}) collective-permute-start(bf16[128,256]{1,0:T(8,128)(2,1)S(1)} %project.1.own_ref.refs_0_), channel_id=1, source_target_pairs={{0,20},{4,16},{8,28},{12,24},{16,4},{20,0},{24,12},{28,8},{1,21},{... | collective-permute-start | bytes 196616 | tf_op jit(solution)/shard_map/ppermute | solution.py:28
  10.5 10.1 %collective-permute-start.3 = (bf16[128,256]{1,0:T(8,128)(2,1)S(1)}, bf16[128,256]{1,0:T(8,128)(2,1)S(1)}, u32[]{:S(2)}, u32[]{:S(2)}) collective-permute-start(bf16[128,256]{1,0:T(8,128)(2,1)S(1)} %project.1.own_ref.refs_0_), channel_id=1, source_target_pairs={{0,24},{4,28},{8,0},{12,4},{16,8},{20,12},{24,16},{28,20},{1,25},{... | collective-permute-start | bytes 196616 | tf_op jit(solution)/shard_map/ppermute | solution.py:28
  11.8 8.8 %collective-permute-start.1 = (bf16[128,256]{1,0:T(8,128)(2,1)S(1)}, bf16[128,256]{1,0:T(8,128)(2,1)S(1)}, u32[]{:S(2)}, u32[]{:S(2)}) collective-permute-start(bf16[128,256]{1,0:T(8,128)(2,1)S(1)} %project.1.own_ref.refs_0_), channel_id=1, source_target_pairs={{0,8},{4,12},{8,16},{12,20},{16,24},{20,28},{24,0},{28,4},{1,9},{5... | collective-permute-start | bytes 196616 | tf_op jit(solution)/shard_map/ppermute | solution.py:28
  12.5 8.1 %collective-permute-start.4 = (bf16[128,256]{1,0:T(8,128)(2,1)S(1)}, bf16[128,256]{1,0:T(8,128)(2,1)S(1)}, u32[]{:S(2)}, u32[]{:S(2)}) collective-permute-start(bf16[128,256]{1,0:T(8,128)(2,1)S(1)} %collective-permute-done.refs_1_), channel_id=1, source_target_pairs={{0,24},{4,28},{8,0},{12,4},{16,8},{20,12},{24,16},{28,20},{1,25},{... | collective-permute-start | bytes 196616 | tf_op jit(solution)/shard_map/ppermute | solution.py:28
  15.7 6.1 %collective-permute-start.2 = (bf16[128,256]{1,0:T(8,128)(2,1)S(1)}, bf16[128,256]{1,0:T(8,128)(2,1)S(1)}, u32[]{:S(2)}, u32[]{:S(2)}) collective-permute-start(bf16[128,256]{1,0:T(8,128)(2,1)S(1)} %collective-permute-done.refs_1_), channel_id=1, source_target_pairs={{0,8},{4,12},{8,16},{12,20},{16,24},{20,28},{24,0},{28,4},{1,9},{5... | collective-permute-start | bytes 196616 | tf_op jit(solution)/shard_map/ppermute | solution.py:28
  15.7 1.6 %copy-start.2 = (bf16[1024,1024]{1,0:T(8,128)(2,1)S(1)}, bf16[1024,1024]{1,0:T(8,128)(2,1)}, u32[]{:S(2)}) copy-start(bf16[1024,1024]{1,0:T(8,128)(2,1)} %up_ref.3) | copy-start | bytes 6291460
  27.5 5.0 %collective-permute-start.6 = (bf16[1,144,256]{2,1,0:T(8,128)(2,1)S(1)}, bf16[1,144,256]{2,1,0:T(8,128)(2,1)S(1)}, u32[]{:S(2)}, u32[]{:S(2)}) collective-permute-start(bf16[1,144,256]{2,1,0:T(8,128)(2,1)S(1)} %get-tuple-element.27.grad_ref), channel_id=1, source_target_pairs={{0,4},{4,0},{8,12},{12,8},{16,20},{20,16},{24,28},{28,24},{1,5},{5... | collective-permute-start | bytes 221192 | tf_op jit(solution)/shard_map/ppermute | solution.py:28
  29.0 11.2 %collective-permute-start.7 = (bf16[128,256]{1,0:T(8,128)(2,1)S(1)}, bf16[128,256]{1,0:T(8,128)(2,1)S(1)}, u32[]{:S(2)}, u32[]{:S(2)}) collective-permute-start(bf16[128,256]{1,0:T(8,128)(2,1)S(1)} %get-tuple-element.29), channel_id=1, source_target_pairs={{0,20},{4,16},{8,28},{12,24},{16,4},{20,0},{24,12},{28,8},{1,21},{... | collective-permute-start | bytes 196616 | tf_op jit(solution)/shard_map/ppermute | solution.py:28
  33.1 7.1 %collective-permute-start.8 = (bf16[128,256]{1,0:T(8,128)(2,1)S(1)}, bf16[128,256]{1,0:T(8,128)(2,1)S(1)}, u32[]{:S(2)}, u32[]{:S(2)}) collective-permute-start(bf16[128,256]{1,0:T(8,128)(2,1)S(1)} %get-tuple-element.30), channel_id=1, source_target_pairs={{0,24},{4,28},{8,0},{12,4},{16,8},{20,12},{24,16},{28,20},{1,25},{... | collective-permute-start | bytes 196616 | tf_op jit(solution)/shard_map/ppermute | solution.py:28
  35.3 6.1 %collective-permute-start.9 = (bf16[128,256]{1,0:T(8,128)(2,1)S(1)}, bf16[128,256]{1,0:T(8,128)(2,1)S(1)}, u32[]{:S(2)}, u32[]{:S(2)}) collective-permute-start(bf16[128,256]{1,0:T(8,128)(2,1)S(1)} %get-tuple-element.31), channel_id=1, source_target_pairs={{0,8},{4,12},{8,16},{12,20},{16,24},{20,28},{24,0},{28,4},{1,9},{5... | collective-permute-start | bytes 196616 | tf_op jit(solution)/shard_map/ppermute | solution.py:28
  35.3 1.6 %copy-start.3 = (bf16[1024,1024]{1,0:T(8,128)(2,1)S(1)}, bf16[1024,1024]{1,0:T(8,128)(2,1)}, u32[]{:S(2)}) copy-start(bf16[1024,1024]{1,0:T(8,128)(2,1)} %up_ref.3) | copy-start | bytes 6291460
  36.9 4.5 %copy-start = (bf16[8192,2,128]{2,1,0:T(2,128)(2,1)S(1)}, bf16[8192,2,128]{2,1,0:T(2,128)(2,1)}, u32[]{:S(2)}) copy-start(bf16[8192,2,128]{2,1,0:T(2,128)(2,1)} %param.7) | copy-start | bytes 12582916
  42.5 2.3 %collective-permute-start.14 = (bf16[32,4096]{1,0:T(8,128)(2,1)S(1)}, bf16[32,4096]{1,0:T(8,128)(2,1)S(1)}, u32[]{:S(2)}, u32[]{:S(2)}) collective-permute-start(bf16[32,4096]{1,0:T(8,128)(2,1)S(1)} %get-tuple-element.39), channel_id=1, source_target_pairs={{0,1},{1,0},{2,3},{3,2},{4,5},{5,4},{6,7},{7,6},{8,9},{9,8},{10,11... | collective-permute-start | bytes 786440 | tf_op jit(solution)/shard_map/ppermute | solution.py:493
  42.6 3.9 %collective-permute-start.13 = (bf16[32,4096]{1,0:T(8,128)(2,1)S(1)}, bf16[32,4096]{1,0:T(8,128)(2,1)S(1)}, u32[]{:S(2)}, u32[]{:S(2)}) collective-permute-start(bf16[32,4096]{1,0:T(8,128)(2,1)S(1)} %get-tuple-element.37), channel_id=1, source_target_pairs={{0,1},{1,0},{2,3},{3,2},{4,5},{5,4},{6,7},{7,6},{8,9},{9,8},{10,11... | collective-permute-start | bytes 786440 | tf_op jit(solution)/shard_map/ppermute | solution.py:493
  44.2 2.3 %collective-permute-start.10 = (bf16[32,4096]{1,0:T(8,128)(2,1)S(1)}, bf16[32,4096]{1,0:T(8,128)(2,1)S(1)}, u32[]{:S(2)}, u32[]{:S(2)}) collective-permute-start(bf16[32,4096]{1,0:T(8,128)(2,1)S(1)} %get-tuple-element.33), channel_id=1, source_target_pairs={{0,1},{1,0},{2,3},{3,2},{4,5},{5,4},{6,7},{7,6},{8,9},{9,8},{10,11... | collective-permute-start | bytes 786440 | tf_op jit(solution)/shard_map/ppermute | solution.py:493
  44.3 2.2 %collective-permute-start.11 = (bf16[32,4096]{1,0:T(8,128)(2,1)S(1)}, bf16[32,4096]{1,0:T(8,128)(2,1)S(1)}, u32[]{:S(2)}, u32[]{:S(2)}) collective-permute-start(bf16[32,4096]{1,0:T(8,128)(2,1)S(1)} %get-tuple-element.35), channel_id=1, source_target_pairs={{0,1},{1,0},{2,3},{3,2},{4,5},{5,4},{6,7},{7,6},{8,9},{9,8},{10,11... | collective-permute-start | bytes 786440 | tf_op jit(solution)/shard_map/ppermute | solution.py:493
  44.8 9.2 %collective-permute-start.15 = (bf16[32,4096]{1,0:T(8,128)(2,1)S(1)}, bf16[32,4096]{1,0:T(8,128)(2,1)S(1)}, u32[]{:S(2)}, u32[]{:S(2)}) collective-permute-start(bf16[32,4096]{1,0:T(8,128)(2,1)S(1)} %add_convert_fusion.1), channel_id=1, source_target_pairs={{0,2},{1,3},{2,0},{3,1},{4,6},{5,7},{6,4},{7,5},{8,10},{9,11},{10,... | collective-permute-start | bytes 786440 | tf_op jit(solution)/shard_map/ppermute | solution.py:493
  46.7 12.1 %collective-permute-start.12 = (bf16[32,4096]{1,0:T(8,128)(2,1)S(1)}, bf16[32,4096]{1,0:T(8,128)(2,1)S(1)}, u32[]{:S(2)}, u32[]{:S(2)}) collective-permute-start(bf16[32,4096]{1,0:T(8,128)(2,1)S(1)} %add_convert_fusion.4), channel_id=1, source_target_pairs={{0,2},{1,3},{2,0},{3,1},{4,6},{5,7},{6,4},{7,5},{8,10},{9,11},{10,... | collective-permute-start | bytes 786440 | tf_op jit(solution)/shard_map/ppermute | solution.py:493
